TPU v7x, 32 devices: a whole 2x2x4 slice. The times are simulated.
32 devices in a mesh: grp: 2 (over y), row: 4 (over z), col: 2 (over x), sub: 2 (over core).
Axes of the slice: x: 2, y: 2, z: 4, core: 2. Of those that a mesh axis runs over, the one named last changes fastest.
Arguments:
- homolog_activations: bfloat16 [128, 192, 256], P(('grp', 'col', 'sub'), 'row'), parts along dimension 0, may hold values from -6 to 6
- edge_activations: bfloat16 [384, 192, 128], P(('grp', 'row', 'sub'), 'col'), parts along dimension 0, may hold values from -6 to 6
- first_projection_matrix: bfloat16 [256, 32], replicated, may hold values from -0.375 to 0.375
- second_projection_matrix: bfloat16 [256, 32], replicated, may hold values from -0.375 to 0.375
- tensor_product_matrix: bfloat16 [1024, 128], replicated, may hold values from -1.5 to 1.5
- multiplicative_entry_matrix: bfloat16 [128, 640], replicated, may hold values from -0.5 to 0.5
- multiplicative_exit_matrix: bfloat16 [128, 128], replicated, may hold values from -0.5 to 0.5
Outputs:
- pair_out: bfloat16 [384, 192, 128], P(('grp', 'row', 'sub'), 'col'), parts along dimension 0
There are 2 independent parts, one for each index of `grp`. A program takes and returns all parts, laid end to end along the dimension named above; an argument that names none is the same for every part. Nothing has to cross between parts.
All inputs are finite; a program needn't handle non-finite values.
Results may differ from a plain program's by a relative error of at most 0.012.
Values may be sent and summed in bfloat16 or wider, within the bound.
No kernel may reach another device: no remote copies, remote signals or barrier semaphores. Data moves between devices by JAX's collectives and lax.ppermute only.
A program may use at most 128 MiB of HBM per device.

v0:
```python
import functools

import jax
import jax.numpy as jnp
from jax import lax
from jax.experimental import pallas as pl
from jax.experimental.pallas import tpu as pltpu
from jax.sharding import PartitionSpec as P


EPSILON = 1e-05
LANES = 128
VMEM_LIMIT = 60 * 1024 * 1024


def standardize_features(values):
    centred = values - jnp.mean(values, axis=-1, keepdims=True)
    spread = jnp.mean(centred * centred, axis=-1, keepdims=True)
    return centred * lax.rsqrt(spread + EPSILON)


def standardize_columns(values):
    centred = values - jnp.mean(values, axis=0, keepdims=True)
    spread = jnp.mean(centred * centred, axis=0, keepdims=True)
    return centred * lax.rsqrt(spread + EPSILON)


def vmem():
    return pl.BlockSpec(memory_space=pltpu.VMEM)


def smem():
    return pl.BlockSpec(memory_space=pltpu.SMEM)


def packing(count, cols):
    spare = -cols % LANES
    if spare and cols < LANES and cols % spare == 0:
        parts = cols // spare
        if count % (parts + 1) == 0:
            return parts, count // (parts + 1) * parts
    return 0, count


def lane_index(shape):
    return lax.broadcasted_iota(jnp.int32, shape, len(shape) - 1)


def weights_kernel(fw, w_ref, n_ref, x_ref, wt_ref, nt_ref, xt_ref, sc, st):
    C = w_ref.shape[1]
    sc[...] = w_ref[...].astype(jnp.float32)
    for b in range(fw):
        st[b * fw : (b + 1) * fw, :] = sc[pl.ds(b, fw, stride=fw), :]
    for t in range(fw * fw // C):
        wt_ref[:, t * C : (t + 1) * C] = st[t * C : (t + 1) * C, :].T.astype(jnp.bfloat16)
    for t in range(n_ref.shape[1] // C):
        nt_ref[t * C : (t + 1) * C, :] = n_ref[:, t * C : (t + 1) * C].astype(jnp.float32).T.astype(jnp.bfloat16)
    xt_ref[...] = x_ref[...].astype(jnp.float32).T.astype(jnp.bfloat16)


def weights(w, n, x, fw):
    K, C = w.shape
    bf = jnp.bfloat16
    return pl.pallas_call(
        functools.partial(weights_kernel, fw),
        out_shape=[jax.ShapeDtypeStruct((C, K), bf), jax.ShapeDtypeStruct(n.shape[::-1], bf), jax.ShapeDtypeStruct(x.shape[::-1], bf)],
        in_specs=[vmem()] * 3,
        out_specs=[vmem()] * 3,
        scratch_shapes=[pltpu.VMEM((K, C), jnp.float32)] * 2,
    )(w, n, x)


def prep_kernel(fw, own_ref, recv_ref, rt_ref, sc):
    groups, m, seqs, row_lanes = own_ref.shape
    res = row_lanes // fw
    chunk = sc.shape[2]
    pieces = [(ref, g) for ref in (own_ref, recv_ref) for g in range(groups)]
    per = chunk // seqs
    for u in range(len(pieces) // per):
        for mm in range(m):
            for t in range(row_lanes // LANES):
                block = jnp.concatenate(
                    [ref[g, mm, :, t * LANES : (t + 1) * LANES].astype(jnp.float32) for ref, g in pieces[u * per : (u + 1) * per]], axis=0
                )
                start = mm * row_lanes + t * LANES
                sc[u, start : start + LANES, :] = block.T
        for b in range(fw):
            rt_ref[b, :, u * chunk : (u + 1) * chunk] = sc[u, pl.ds(b, m * res, stride=fw), :].astype(jnp.bfloat16)


def prep(own, recv, fw):
    groups, m, seqs, row_lanes = own.shape
    total = 2 * groups * seqs
    chunk = min(total, LANES)
    cols = m * row_lanes // fw
    return pl.pallas_call(
        functools.partial(prep_kernel, fw),
        out_shape=jax.ShapeDtypeStruct((fw, cols, total), jnp.bfloat16),
        in_specs=[vmem(), vmem()],
        out_specs=vmem(),
        scratch_shapes=[pltpu.VMEM((total // chunk, m * row_lanes, chunk), jnp.float32)],
    )(own, recv)


def pair_kernel(cfg, sub_ref, l_ref, lr_ref, rt_ref, wt_ref, e_ref, went_ref, *rest):
    fw, C, J, S, full = cfg
    if full:
        mid_ref, gate_ref, lk_ref, ls_ref, rk_ref, rs_ref, lt, ot, nts, lsc, rsc = rest
    else:
        rk_ref, rs_ref, lt, ot, nts, rsc = rest
    half = C // 2
    IG = l_ref.shape[1] // fw
    wide = ot.shape[2] // 2
    for t in range(IG * fw // LANES):
        part = slice(t * LANES, (t + 1) * LANES)
        block = jnp.concatenate([l_ref[:, part].astype(jnp.float32), lr_ref[:, part].astype(jnp.float32)], axis=0)
        lt[part, :] = block.T.astype(jnp.bfloat16)
    ltv = lt[...]
    for b in range(fw):
        o = lax.dot_general(ltv, rt_ref[b], (((1,), (1,)), ((), ())), preferred_element_type=jnp.float32).astype(jnp.bfloat16)
        for i in range(IG):
            ot[i // 2, b * fw : (b + 1) * fw, i % 2 * wide : i % 2 * wide + J] = o[i * fw : (i + 1) * fw, :]
    wt = wt_ref[...]
    for h in range(IG // 2):
        pt = lax.dot_general(wt, ot[h], (((1,), (0,)), ((), ())), preferred_element_type=jnp.float32)
        for k in range(2):
            i = 2 * h + k
            et = e_ref[i].astype(jnp.float32).T
            mid = (et + pt[:, k * wide : k * wide + J] * (1.0 / S)).astype(jnp.bfloat16)
            if full:
                mid_ref[i] = mid
            nts[h, :, k * wide : k * wide + J] = standardize_columns(mid.astype(jnp.float32)).astype(jnp.bfloat16)

    def project(first, count, h):
        return lax.dot_general(went_ref[first * C : (first + count) * C, :], nts[h], (((1,), (0,)), ((), ())), preferred_element_type=jnp.float32)

    for h in range(IG // 2):
        if full:
            p = project(0, 2, h)
            x = jax.nn.sigmoid(p[C:]) * p[:C]
            for k in range(2):
                lsc[pl.ds((2 * h + k) * C, C), :J] = x[:, k * wide : k * wide + J]
        p = project(2, 2, h)
        x = jax.nn.sigmoid(p[C:]) * p[:C]
        for k in range(2):
            rsc[pl.ds((2 * h + k) * C, C), :J] = x[:, k * wide : k * wide + J]
        if full:
            x = jax.nn.sigmoid(project(4, 1, h)).astype(jnp.bfloat16)
            for k in range(2):
                gate_ref[2 * h + k] = x[:, k * wide : k * wide + J]
    sub = sub_ref[0]
    parts, main = packing(half, J)
    inside = lane_index((IG, LANES)) < J
    if full:
        for ref, base in ((lk_ref, sub * half), (ls_ref, (1 - sub) * half)):
            for ch in range(half):
                x = lsc[pl.ds(base + ch, IG, stride=C), :]
                ref[ch] = jnp.where(inside, x, 0.0).astype(jnp.bfloat16)
    for ref, base in ((rk_ref, sub * half), (rs_ref, (1 - sub) * half)):
        if parts == 0:
            for ch in range(half):
                x = rsc[pl.ds(base + ch, IG, stride=C), :]
                ref[ch] = jnp.where(inside, x, 0.0).astype(jnp.bfloat16)
        else:
            tails = half - main
            spare = LANES - J
            for q in range(tails):
                tail = rsc[pl.ds(base + main + q, IG, stride=C), :]
                for t in range(parts):
                    x = rsc[pl.ds(base + t * tails + q, IG, stride=C), :]
                    moved = pltpu.roll(tail, J - spare * t, 1)
                    ref[t * tails + q] = jnp.where(inside, x, moved).astype(jnp.bfloat16)


def pair(sub, l, lr, which, rt, wt, e, went, IG, full=True):
    _, part, IA = l.shape
    S = 2 * part
    fw, J, _ = rt.shape
    TI = IA // fw
    C = wt.shape[0]
    half = C // 2
    rows = packing(half, J)[1]
    wide = -(-J // LANES) * LANES
    bf = jnp.bfloat16
    tile = (jax.ShapeDtypeStruct((TI, C, J), bf), pl.BlockSpec((IG, C, J), lambda g: (g, 0, 0)))
    lefts = (jax.ShapeDtypeStruct((half, TI, LANES), bf), pl.BlockSpec((half, IG, LANES), lambda g: (0, g, 0)))
    rights = (jax.ShapeDtypeStruct((rows, TI, LANES), bf), pl.BlockSpec((rows, IG, LANES), lambda g: (0, g, 0)))
    outs = ([tile] * 2 + [lefts] * 2 if full else []) + [rights] * 2
    gated = pltpu.VMEM((IG * C, LANES), jnp.float32)
    f = pl.pallas_call(
        functools.partial(pair_kernel, (fw, C, J, S, full)),
        grid=(TI // IG,),
        out_shape=[o[0] for o in outs],
        in_specs=[
            smem(),
            pl.BlockSpec((None, part, IG * fw), lambda g: (which, 0, g)),
            pl.BlockSpec((None, part, IG * fw), lambda g: (which, 0, g)),
            pl.BlockSpec((fw, J, S), lambda g: (0, 0, 0)),
            pl.BlockSpec(wt.shape, lambda g: (0, 0)),
            pl.BlockSpec((IG, J, C), lambda g: (g, 0, 0)),
            pl.BlockSpec(went.shape, lambda g: (0, 0)),
        ],
        out_specs=[o[1] for o in outs],
        scratch_shapes=[
            pltpu.VMEM((IG * fw, S), bf),
            pltpu.VMEM((IG // 2, fw * fw, 2 * wide), bf),
            pltpu.VMEM((IG // 2, C, 2 * wide), bf),
            gated,
        ]
        + ([gated] if full else []),
        compiler_params=pltpu.CompilerParams(vmem_limit_bytes=VMEM_LIMIT),
        cost_estimate=pl.CostEstimate(flops=2 * TI * J * (S * fw * fw + fw * fw * C + 5 * C * C), bytes_accessed=4 * TI * J * C * 6, transcendentals=TI * J * C * 3),
    )
    return f(sub, l, lr, rt, wt, e, went)


def tri_kernel(cfg, n_slots, pos_ref, lk_ref, lr_ref, *rest):
    nr, nc, m, J = cfg
    slots = rest[:n_slots]
    outs = rest[n_slots : n_slots + 2 * nc]
    rv, lm, sem = rest[n_slots + 2 * nc :]
    half, TI, _ = lk_ref.shape
    row, col, sub = pos_ref[0], pos_ref[1], pos_ref[2]
    parts, main = packing(half, J)
    tails = half - main
    spare = LANES - J

    def copy(index):
        step, u = index // 2, index % 2
        hop = (step + 1) // 2
        origin = row - hop if step % 2 else row + hop
        return origin, pltpu.make_async_copy(slots[index], rv.at[jnp.clip(origin, 0, nr - 1), sub if u == 0 else 1 - sub], sem.at[index])

    for index in range(n_slots):
        origin, c = copy(index)

        @pl.when((origin >= 0) & (origin < nr))
        def _(c=c):
            c.start()

    inside = lane_index((2 * TI, LANES)) < J
    for ch in range(half):
        x = jnp.concatenate([lk_ref[ch], lr_ref[ch]], axis=0)
        if ch < main:
            lm[ch] = x
        else:
            f = x.astype(jnp.float32)
            for t in range(parts):
                moved = pltpu.roll(f, J - spare * t, 1)
                lm[main + (ch - main) * parts + t] = jnp.where(inside, 0.0, moved).astype(jnp.bfloat16)

    for index in range(n_slots):
        origin, c = copy(index)

        @pl.when((origin >= 0) & (origin < nr))
        def _(c=c):
            c.wait()

    def block(ch, start, pieces):
        right = rv[pl.ds(start, m), :, ch].reshape(m * 2 * TI, LANES)
        return lax.dot_general(lm[pieces], right, (((1,), (1,)), ((), ())), preferred_element_type=jnp.float32)

    for dc in range(nc):
        start = lax.rem(col + dc, nc) * m
        own_ref, other_ref = outs[2 * dc], outs[2 * dc + 1]
        for q in range(tails if parts else 0):
            tail = 0.0
            for t in range(parts):
                tail = tail + block(t * tails + q, start, main + q * parts + t)
            tail = jnp.concatenate([tail, jnp.zeros((2 * TI, spare), jnp.float32)], axis=1)
            for t in range(parts):
                x = block(t * tails + q, start, t * tails + q)
                x = jnp.concatenate([x, jnp.zeros((2 * TI, spare), jnp.float32)], axis=1)
                x = jnp.where(inside, x, pltpu.roll(tail, J - spare * t, 1)).astype(jnp.bfloat16)
                own_ref[t * tails + q] = x[:TI]
                other_ref[t * tails + q] = x[TI:]
        if not parts:
            for ch in range(half):
                x = block(ch, start, ch)
                if spare:
                    x = jnp.concatenate([x, jnp.zeros((2 * TI, spare), jnp.float32)], axis=1)
                x = x.astype(jnp.bfloat16)
                own_ref[ch] = x[:TI]
                other_ref[ch] = x[TI:]


def triangle(pos, lk, lr, slots, nr, nc, m, J):
    half, TI, _ = lk.shape
    parts, main = packing(half, J)
    rows = main
    bf = jnp.bfloat16
    n = len(slots)
    return pl.pallas_call(
        functools.partial(tri_kernel, (nr, nc, m, J), n),
        out_shape=[jax.ShapeDtypeStruct((rows, TI, LANES), bf)] * (2 * nc),
        in_specs=[smem(), vmem(), vmem()] + [pl.BlockSpec(memory_space=pl.ANY)] * n,
        out_specs=[vmem()] * (2 * nc),
        scratch_shapes=[
            pltpu.VMEM((nr, 2, rows, TI, LANES), bf),
            pltpu.VMEM((main + (half - main) * max(parts, 1), 2 * TI, LANES), bf),
            pltpu.SemaphoreType.DMA((n,)),
        ],
        compiler_params=pltpu.CompilerParams(vmem_limit_bytes=VMEM_LIMIT),
    )(pos, lk, lr, *slots)


def finish(sc, nts, mid_ref, gate_ref, wx_ref, out_ref):
    TI, C, J = mid_ref.shape
    wide = nts.shape[2] // 2
    wx = wx_ref[...]
    for i in range(TI):
        tri = sc[pl.ds(i, C, stride=TI), :][:, :J]
        nts[i // 2, :, i % 2 * wide : i % 2 * wide + J] = standardize_columns(tri).astype(jnp.bfloat16)
    for h in range(TI // 2):
        update = lax.dot_general(wx, nts[h], (((1,), (0,)), ((), ())), preferred_element_type=jnp.float32)
        for k in range(2):
            i = 2 * h + k
            res = mid_ref[i].astype(jnp.float32) + gate_ref[i].astype(jnp.float32) * update[:, k * wide : k * wide + J]
            out_ref[i] = res.T.astype(jnp.bfloat16)


def final_kernel(cfg, n, sub_ref, *rest):
    C, J = cfg
    own = rest[:n]
    other = rest[n : 2 * n]
    mid_ref, gate_ref, wx_ref, out_ref, sc, nts = rest[2 * n :]
    TI = mid_ref.shape[0]
    half = C // 2
    parts, main = packing(half, J)
    tails = half - main
    spare = LANES - J
    sub = sub_ref[0]
    lanes = lane_index((TI, LANES))
    for refs, base in ((own, sub * half), (other, (1 - sub) * half)):
        def total(ch, refs=refs):
            x = refs[0][ch].astype(jnp.float32)
            for ref in refs[1:]:
                x = x + ref[ch].astype(jnp.float32)
            return x.astype(jnp.bfloat16).astype(jnp.float32)

        for q in range(tails if parts else 0):
            tail = jnp.zeros((TI, LANES), jnp.float32)
            for t in range(parts):
                x = total(t * tails + q)
                sc[pl.ds((base + t * tails + q) * TI, TI), :] = x
                tail = jnp.where((lanes >= spare * t) & (lanes < spare * (t + 1)), pltpu.roll(x, LANES - J + spare * t, 1), tail)
            sc[pl.ds((base + main + q) * TI, TI), :] = tail
        if not parts:
            for ch in range(half):
                sc[pl.ds((base + ch) * TI, TI), :] = total(ch)
    finish(sc, nts, mid_ref, gate_ref, wx_ref, out_ref)


def final(sub, own, other, mid, gate, wx):
    TI, C, J = mid.shape
    n = len(own)
    return pl.pallas_call(
        functools.partial(final_kernel, (C, J), n),
        out_shape=jax.ShapeDtypeStruct((TI, J, C), jnp.bfloat16),
        in_specs=[smem()] + [vmem()] * (2 * n + 3),
        out_specs=vmem(),
        scratch_shapes=[pltpu.VMEM((C * TI, LANES), jnp.float32), pltpu.VMEM((TI // 2, C, 2 * LANES), jnp.bfloat16)],
        compiler_params=pltpu.CompilerParams(vmem_limit_bytes=VMEM_LIMIT),
    )(sub, *own, *other, mid, gate, wx)


def masked_left(lk_ref, lr_ref, lm, J):
    half, TI, _ = lk_ref.shape
    parts, main = packing(half, J)
    spare = LANES - J
    inside = lane_index((2 * TI, LANES)) < J
    for ch in range(half):
        x = jnp.concatenate([lk_ref[ch], lr_ref[ch]], axis=0)
        if ch < main:
            lm[ch] = x
        else:
            f = x.astype(jnp.float32)
            for t in range(parts):
                moved = pltpu.roll(f, J - spare * t, 1)
                lm[main + (ch - main) * parts + t] = jnp.where(inside, 0.0, moved).astype(jnp.bfloat16)


def shard_products(lm, rv, k, J, half, TI, store):
    parts, main = packing(half, J)
    tails = half - main

    def dot(left, row):
        right = rv[k, :, row].reshape(2 * TI, LANES)
        return lax.dot_general(lm[left], right, (((1,), (1,)), ((), ())), preferred_element_type=jnp.float32)

    def channel(ch):
        if ch < main:
            return dot(ch, ch)
        q = ch - main
        x = dot(main + q * parts, q)
        for t in range(1, parts):
            x = x + dot(main + q * parts + t, t * tails + q)
        return x

    pairs = half // 2
    cols = 4 * TI
    pad = jnp.zeros((2 * TI, LANES - cols), jnp.float32)
    p2, m2 = packing(pairs, cols)
    t2 = pairs - m2

    def both(q):
        return jnp.concatenate([channel(q), channel(q + pairs), pad], axis=1)

    inside = lane_index((2 * TI, LANES)) < cols
    spare = LANES - cols
    for q in range(t2):
        tail = both(m2 + q)
        for t in range(p2):
            store(t * t2 + q, jnp.where(inside, both(t * t2 + q), pltpu.roll(tail, cols - spare * t, 1)).astype(jnp.bfloat16))
    for q in range(0 if p2 else pairs):
        store(q, both(q).astype(jnp.bfloat16))


def early_kernel(J, n, pos_ref, lk_ref, lr_ref, *rest):
    own, up, down, far = rest[0:2], rest[2:4], rest[4:6], rest[6:8]
    outs = rest[8:14]
    rv, lm, acc, sem = rest[14:]
    half, TI, _ = lk_ref.shape
    row, col, sub = pos_ref[0], pos_ref[1], pos_ref[2]
    even = lax.rem(row, 2) == 0
    edge = (row == 0) | (row == n - 1)
    plan = [
        (None, own, 0),
        (even, down, 1),
        (jnp.logical_not(even), up, 1),
        (edge, far, 2),
        (jnp.logical_not(edge) & even, up, 2),
        (jnp.logical_not(edge) & jnp.logical_not(even), down, 2),
    ]

    def each(action):
        for cond, refs, k in plan:
            for u in range(2):
                c = pltpu.make_async_copy(refs[u], rv.at[k, sub if u == 0 else 1 - sub], sem.at[k, u])
                if cond is None:
                    action(c)
                else:
                    pl.when(cond)(lambda c=c: action(c))

    each(lambda c: c.start())
    masked_left(lk_ref, lr_ref, lm, J)
    each(lambda c: c.wait())
    for k in range(3):

        def store(r, x, k=k):
            acc[k, r] = x

        shard_products(lm, rv, k, J, half, TI, store)
    home = col == row // 2
    send = jnp.where(home, acc[2], acc[0])
    keep = jnp.where(home, acc[0], acc[2])
    for u in range(2):
        outs[u][...] = send[:, u * TI : (u + 1) * TI]
        outs[2 + u][...] = keep[:, u * TI : (u + 1) * TI]
        outs[4 + u][...] = acc[1, :, u * TI : (u + 1) * TI]


def late_kernel(J, n, pos_ref, lk_ref, lr_ref, a_ref, b_ref, *rest):
    up, down = rest[0:2], rest[2:4]
    outs = rest[4:8]
    rv, lm, acc, sem = rest[8:]
    half, TI, _ = lk_ref.shape
    row, col, sub = pos_ref[0], pos_ref[1], pos_ref[2]
    low = row < 2

    def each(action):
        for cond, refs in ((low, down), (jnp.logical_not(low), up)):
            for u in range(2):
                c = pltpu.make_async_copy(refs[u], rv.at[0, sub if u == 0 else 1 - sub], sem.at[u])
                pl.when(cond)(lambda c=c: action(c))

    each(lambda c: c.start())
    masked_left(lk_ref, lr_ref, lm, J)
    each(lambda c: c.wait())

    def store(r, x):
        acc[r] = x

    shard_products(lm, rv, 0, J, half, TI, store)
    home = col == row // 2
    for u, ref in enumerate((a_ref, b_ref)):
        late = acc[:, u * TI : (u + 1) * TI]
        early = ref[...]
        outs[u][...] = jnp.where(home, late, early)
        outs[2 + u][...] = jnp.where(home, early, late)


def split_call(kernel, shards, sems, n_out, pos, lk, lr, extra, slots, J, n):
    half, TI, _ = lk.shape
    parts, main = packing(half, J)
    rows = packing(half // 2, 4 * TI)[1]
    bf = jnp.bfloat16
    acc = (rows, 2 * TI, LANES)
    return pl.pallas_call(
        functools.partial(kernel, J, n),
        out_shape=[jax.ShapeDtypeStruct((rows, TI, LANES), bf)] * n_out,
        in_specs=[smem(), vmem(), vmem()] + [vmem()] * len(extra) + [pl.BlockSpec(memory_space=pl.ANY)] * len(slots),
        out_specs=[vmem()] * n_out,
        scratch_shapes=[
            pltpu.VMEM((shards, 2, main, TI, LANES), bf),
            pltpu.VMEM((main + (half - main) * max(parts, 1), 2 * TI, LANES), bf),
            pltpu.VMEM((shards,) + acc if shards > 1 else acc, bf),
            pltpu.SemaphoreType.DMA(sems),
        ],
        compiler_params=pltpu.CompilerParams(vmem_limit_bytes=VMEM_LIMIT),
        cost_estimate=pl.CostEstimate(flops=2 * shards * half * 48 * 48 * 512, bytes_accessed=shards * 2 * main * TI * LANES * 4, transcendentals=0),
    )(pos, lk, lr, *extra, *slots)


def final_pairs_kernel(cfg, pos_ref, *rest):
    C, _ = cfg
    own = (rest[0:2], rest[2:4])
    other = (rest[4:6], rest[6:8])
    mid_ref, gate_ref, wx_ref, out_ref, sc, nts = rest[8:]
    TI = mid_ref.shape[0]
    half = C // 2
    pairs = half // 2
    cols = 4 * TI
    parts, main = packing(pairs, cols)
    tails = pairs - main
    spare = LANES - cols
    row, col, sub = pos_ref[0], pos_ref[1], pos_ref[2]
    home = col == row // 2
    odd = lax.rem(row, 2) == 1
    first = jnp.where(home, jnp.logical_not(odd), odd)
    lanes = lane_index((TI, LANES))
    low = lanes < 2 * TI
    for groups, base in ((own, sub * half), (other, (1 - sub) * half)):

        def place(q, both):
            a = jnp.where(first, both[0], both[1])
            b = jnp.where(first, both[1], both[0])
            x = jnp.where(low, a, pltpu.roll(b, 2 * TI, 1))
            y = jnp.where(low, pltpu.roll(a, LANES - 2 * TI, 1), b)
            sc[pl.ds((base + q) * TI, TI), :] = x
            sc[pl.ds((base + q + pairs) * TI, TI), :] = y

        def total(g, r):
            x = groups[g][0][r].astype(jnp.float32) + groups[g][1][r].astype(jnp.float32)
            return x.astype(jnp.bfloat16).astype(jnp.float32)

        for q in range(tails if parts else 0):
            tail = [jnp.zeros((TI, LANES), jnp.float32)] * 2
            for t in range(parts):
                x = [total(g, t * tails + q) for g in range(2)]
                place(t * tails + q, x)
                part = (lanes >= spare * t) & (lanes < spare * (t + 1))
                tail = [jnp.where(part, pltpu.roll(x[g], LANES - cols + spare * t, 1), tail[g]) for g in range(2)]
            place(main + q, tail)
        for q in range(0 if parts else pairs):
            place(q, [total(g, q) for g in range(2)])
    finish(sc, nts, mid_ref, gate_ref, wx_ref, out_ref)


def final_pairs(pos, pieces, mid, gate, wx):
    TI, C, J = mid.shape
    return pl.pallas_call(
        functools.partial(final_pairs_kernel, (C, J)),
        out_shape=jax.ShapeDtypeStruct((TI, J, C), jnp.bfloat16),
        in_specs=[smem()] + [vmem()] * (len(pieces) + 3),
        out_specs=vmem(),
        scratch_shapes=[pltpu.VMEM((C * TI, LANES), jnp.float32), pltpu.VMEM((TI // 2, C, 2 * LANES), jnp.bfloat16)],
        compiler_params=pltpu.CompilerParams(vmem_limit_bytes=VMEM_LIMIT),
    )(pos, *pieces, mid, gate, wx)


def shift(x, axis, d):
    n = lax.axis_size(axis)
    return lax.ppermute(x, axis, [(i, (i + d) % n) for i in range(n)])


def step_along(x, axis, d, t):
    n = lax.axis_size(axis)
    return lax.ppermute(x, axis, [(i, i + d) for i in range(n) if 0 <= i + d < n and 0 <= i - d * (t - 1) < n])


def across(x, d):
    nc = lax.axis_size("col")
    return lax.ppermute(x, ("col", "sub"), [(c * 2 + s, (c + d) % nc * 2 + 1 - s) for c in range(nc) for s in range(2)])


def per_device(
    homolog_activations,
    edge_activations,
    first_projection_matrix,
    second_projection_matrix,
    tensor_product_matrix,
    multiplicative_entry_matrix,
    multiplicative_exit_matrix,
):
    seqs, residues, features = homolog_activations.shape
    tile_rows, tile_cols, _ = edge_activations.shape
    fw = first_projection_matrix.shape[1]
    nr, nc, ns = (lax.axis_size(a) for a in ("row", "col", "sub"))
    assert ns == 2
    row, col, sub = (lax.axis_index(a) for a in ("row", "col", "sub"))
    pos = jnp.stack([row, col, sub]).astype(jnp.int32)
    sub_id = pos[2:]
    m = tile_cols // residues

    normed = standardize_features(homolog_activations.astype(jnp.float32)).astype(jnp.bfloat16).reshape(seqs * residues, features)

    def project(matrix):
        return jnp.dot(normed, matrix, preferred_element_type=jnp.float32).astype(jnp.bfloat16).reshape(seqs, residues * fw)

    right = project(second_projection_matrix)
    left = project(first_projection_matrix)

    span = tile_rows * fw
    fast = nr == 4 and nc == 2
    if fast:
        hops = [lax.ppermute(x, "row", [(i, i ^ d) for i in range(nr)]) for d, x in ((3, jnp.stack([right, left])), (2, right), (1, right))]
        left_x = shift(left, "col", 1)
        outer_weight, entry, exit_matrix = weights(tensor_product_matrix, multiplicative_entry_matrix, multiplicative_exit_matrix, fw)
        rows = jnp.stack([right, hops[2], hops[1], hops[0][0]])

        def rows_of(c):
            return [lax.dynamic_index_in_dim(rows, row ^ (c * m + t), 0, keepdims=False) for t in range(m)]

        got = shift(jnp.stack(rows_of(1 - col) + [hops[0][1]]), "col", 1)
        rights = jnp.stack([jnp.stack(rows_of(col)), got[:m]])
        lefts = jnp.stack([jnp.concatenate([left, left_x], axis=0), jnp.concatenate([hops[0][1], got[m]], axis=0)])
        far_edges = lax.ppermute(edge_activations, "row", [(0, nr - 1), (nr - 1, 0)])
        rights_other = shift(rights, "sub", 1)
        left_own = lax.dynamic_slice_in_dim(lefts, sub * span, span, 2)
        left_other = shift(lax.dynamic_slice_in_dim(lefts, (1 - sub) * span, span, 2), "sub", 1)
        right_t = prep(rights, rights_other, fw)
        mid, gate, lk, ls, rk, rs = pair(sub_id, left_own, left_other, 0, right_t, outer_weight, edge_activations, entry, tile_rows)
        up, down = [step_along(rk, "row", 1, 1)], [step_along(rk, "row", -1, 1)]
        rr = shift(rs, "sub", 1)
        up, down = up + [step_along(rr, "row", 1, 1)], down + [step_along(rr, "row", -1, 1)]
        lr = shift(ls, "sub", 1)
        far_k, far_s = pair(sub_id, left_own, left_other, 1, right_t, outer_weight, far_edges, entry, tile_rows, False)
        up2 = [step_along(x, "row", 1, 2) for x in up]
        down2 = [step_along(x, "row", -1, 2) for x in down]
        far = [far_k, shift(far_s, "sub", 1)]
        send1, send1o, keep1, keep1o, rest, resto = split_call(early_kernel, 3, (3, 2), 6, pos, lk, lr, [], [rk, rr, *up, *down, *far], tile_cols, nr)
        got1, got1o, keep1o = shift(send1, "col", 1), across(send1o, 1), shift(keep1o, "sub", 1)
        send2, send2o, keep2, keep2o = split_call(late_kernel, 1, (2,), 4, pos, lk, lr, [rest, resto], [*up2, *down2], tile_cols, nr)
        got2, got2o, keep2o = shift(send2, "col", 1), across(send2o, 1), shift(keep2o, "sub", 1)
        return final_pairs(pos, [keep1, got1, keep2, got2, keep1o, got1o, keep2o, got2o], mid, gate, exit_matrix)

    outer_weight, entry, exit_matrix = weights(tensor_product_matrix, multiplicative_entry_matrix, multiplicative_exit_matrix, fw)
    rows = jnp.stack([right] + [shift(right, "row", d) for d in range(1, nr)])

    def rows_of(c):
        return jnp.stack([lax.dynamic_index_in_dim(rows, lax.rem(row - (c * m + t) + nr, nr), 0, keepdims=False) for t in range(m)])

    rights, lefts = [rows_of(col)], [left]
    for d in range(1, nc):
        rights.append(shift(rows_of(lax.rem(col + d, nc)), "col", d))
        lefts.append(shift(left, "col", d))
    rights = jnp.stack(rights)
    lefts = jnp.concatenate(lefts, axis=0)[None]
    rights_other = shift(rights, "sub", 1)
    left_own = lax.dynamic_slice_in_dim(lefts, sub * span, span, 2)
    left_other = shift(lax.dynamic_slice_in_dim(lefts, (1 - sub) * span, span, 2), "sub", 1)
    right_t = prep(rights, rights_other, fw)
    mid, gate, lk, ls, rk, rs = pair(sub_id, left_own, left_other, 0, right_t, outer_weight, edge_activations, entry, tile_rows)

    rr = shift(rs, "sub", 1)
    lr = shift(ls, "sub", 1)
    slots = [rk, rr]
    up, down = [rk, rr], [rk, rr]
    for t in range(1, nr):
        up = [step_along(x, "row", 1, t) for x in up]
        down = [step_along(x, "row", -1, t) for x in down]
        slots += up + down
    partial = triangle(pos, lk, lr, slots, nr, nc, m, tile_cols)

    own, other = [partial[0]], [shift(partial[1], "sub", 1)]
    for d in range(1, nc):
        own.append(shift(partial[2 * d], "col", d))
        other.append(across(partial[2 * d + 1], d))
    return final(sub_id, own, other, mid, gate, exit_matrix)


def solution(mesh):
    in_specs = (
        P(("grp", "col", "sub"), "row", None),
        P(("grp", "row", "sub"), "col", None),
        P(),
        P(),
        P(),
        P(),
        P(),
    )
    out_specs = P(("grp", "row", "sub"), "col", None)

    return jax.shard_map(per_device, mesh=mesh, in_specs=in_specs, out_specs=out_specs, check_vma=False)
```

profile of v0, /device:TPU:0, one launch (start us, length us, event | category | flops | bytes accessed | tf_op | source)
XLA Modules:
  0.0 106.6 jit_solution(17866013537441903258)
XLA Ops:
  0.0 1.2 %convert_reduce_fusion = f32[16,48]{1,0:T(8,128)S(1)} fusion(bf16[16,48,256]{2,1,0:T(8,128)(2,1)} %param.7), kind=kLoop, calls=%fused_computation.3 | loop fusion | flops 392448 | bytes 396288 | tf_op jit(solution)/shard_map/reduce_sum | solution.py:17
  2.5 3.1 %collective-permute-start.2 = (bf16[16,1536]{1,0:T(8,128)(2,1)S(1)}, bf16[16,1536]{1,0:T(8,128)(2,1)S(1)}, u32[]{:S(2)}, u32[]{:S(2)}) collective-permute-start(bf16[16,1536]{1,0:T(8,128)(2,1)S(1)} %reshape.23), channel_id=1, source_target_pairs={{0,4},{4,0},{8,12},{12,8},{1,5},{5,1},{9,13},{13,9},{2,6},{6,2},{1... | collective-permute-start | bytes 147464 | tf_op jit(solution)/shard_map/ppermute | solution.py:617
  5.7 2.6 %collective-permute-start.3 = (bf16[16,1536]{1,0:T(8,128)(2,1)S(1)}, bf16[16,1536]{1,0:T(8,128)(2,1)S(1)}, u32[]{:S(2)}, u32[]{:S(2)}) collective-permute-start(bf16[16,1536]{1,0:T(8,128)(2,1)S(1)} %reshape.23), channel_id=1, source_target_pairs={{0,8},{4,12},{8,0},{12,4},{1,9},{5,13},{9,1},{13,5},{2,10},{6,14},... | collective-permute-start | bytes 147464 | tf_op jit(solution)/shard_map/ppermute | solution.py:617
  8.9 1.6 %collective-permute-start = (bf16[16,1536]{1,0:T(8,128)(2,1)S(1)}, bf16[16,1536]{1,0:T(8,128)(2,1)S(1)}, u32[]{:S(2)}, u32[]{:S(2)}) collective-permute-start(bf16[16,1536]{1,0:T(8,128)(2,1)S(1)} %reshape.22), channel_id=1, source_target_pairs={{0,2},{2,0},{1,3},{3,1},{4,6},{6,4},{5,7},{7,5},{8,10},{10,8},{9,1... | collective-permute-start | bytes 147464 | tf_op jit(solution)/shard_map/ppermute | solution.py:574
  11.1 5.5 %collective-permute-start.13 = (bf16[24,96,128]{2,1,0:T(8,128)(2,1)S(1)}, bf16[24,96,128]{2,1,0:T(8,128)(2,1)}, u32[]{:S(2)}, u32[]{:S(2)}) collective-permute-start(bf16[24,96,128]{2,1,0:T(8,128)(2,1)S(1)} %copy-done.22), channel_id=1, source_target_pairs={{0,12},{12,0},{1,13},{13,1},{2,14},{14,2},{3,15},{15,3},{16,28},{2... | collective-permute-start | bytes 1769480 | tf_op jit(solution)/shard_map/ppermute | solution.py:628
  16.7 1.7 %collective-permute-done.1 = bf16[2,16,1536]{2,1,0:T(8,128)(2,1)S(1)} collective-permute-done((bf16[2,16,1536]{2,1,0:T(8,128)(2,1)S(1)}, bf16[2,16,1536]{2,1,0:T(8,128)(2,1)S(1)}, u32[]{:S(2)}, u32[]{:S(2)}) %collective-permute-start.1) | collective-permute-done | bytes 98336 | tf_op jit(solution)/shard_map/ppermute | solution.py:617
  18.5 0.6 collective-permute-start.4
  19.1 4.6 %collective-permute-done.4 = bf16[3,16,1536]{2,1,0:T(8,128)(2,1)S(1)} collective-permute-done((bf16[3,16,1536]{2,1,0:T(8,128)(2,1)S(1)}, bf16[3,16,1536]{2,1,0:T(8,128)(2,1)S(1)}, u32[]{:S(2)}, u32[]{:S(2)}) %collective-permute-start.4) | collective-permute-done | bytes 147488 | tf_op jit(solution)/shard_map/ppermute | solution.py:574
  23.9 0.7 fusion.4
  25.0 2.2 %shard_map.74 = (bf16[128,1024]{1,0:T(8,128)(2,1)}, bf16[640,128]{1,0:T(8,128)(2,1)}, bf16[128,128]{1,0:T(8,128)(2,1)}) custom-call(bf16[1024,128]{1,0:T(8,128)(2,1)} %w_ref.1, bf16[128,640]{1,0:T(8,128)(2,1)} %n_ref.1, bf16[128,128]{1,0:T(8,128)(2,1)} %x_ref.1), custom_call_target="tpu_custom_call" | custom-call | tf_op jit(solution)/shard_map/pallas_call | solution.py:64
  27.3 0.7 copy-done.14
  28.0 3.1 %shard_map.73.rt_ref = bf16[32,96,64]{2,1,0:T(8,128)(2,1)} custom-call(bf16[2,2,16,1536]{3,2,1,0:T(8,128)(2,1)} %copy-done.3, bf16[2,2,16,1536]{3,2,1,0:T(8,128)(2,1)} %copy-done.14), custom_call_target="tpu_custom_call" | custom-call | tf_op jit(solution)/shard_map/pallas_call | solution.py:96
  31.1 0.6 copy-done.23
  31.7 8.3 %shard_map.75 = (bf16[24,128,96]{2,1,0:T(8,128)(2,1)}, bf16[24,128,96]{2,1,0:T(8,128)(2,1)}, bf16[64,24,128]{2,1,0:T(8,128)(2,1)}, bf16[64,24,128]{2,1,0:T(8,128...) custom-call(s32[1]{0:T(128)} %bitcast.2.sub_ref, bf16[2,32,768]{2,1,0:T(8,128)(2,1)} %get-tuple-element.52.l_ref, ...), custom_call_target="tpu_custom_call" | custom-call | flops 1283457024 | bytes 7077888 | tf_op jit(solution)/shard_map/pallas_call | solution.py:214
  40.0 1.3 %collective-permute-start.11 = (bf16[48,24,128]{2,1,0:T(8,128)(2,1)}, bf16[48,24,128]{2,1,0:T(8,128)(2,1)S(1)}, u32[]{:S(2)}, u32[]{:S(2)}) collective-permute-start(bf16[48,24,128]{2,1,0:T(8,128)(2,1)} %get-tuple-element.30.rest_0_), channel_id=1, source_target_pairs={{4,0},{8,4},{12,8},{5,1},{9,5},{13,9},{6,2},{10,6},{14,10},{7,3},{... | collective-permute-start | bytes 884744 | tf_op jit(solution)/shard_map/ppermute | solution.py:579
  41.9 14.8 %collective-permute-start.9 = (bf16[48,24,128]{2,1,0:T(8,128)(2,1)}, bf16[48,24,128]{2,1,0:T(8,128)(2,1)S(1)}, u32[]{:S(2)}, u32[]{:S(2)}) collective-permute-start(bf16[48,24,128]{2,1,0:T(8,128)(2,1)} %get-tuple-element.30.rest_0_), channel_id=1, source_target_pairs={{0,4},{4,8},{8,12},{1,5},{5,9},{9,13},{2,6},{6,10},{10,14},{3,7},{... | collective-permute-start | bytes 884744 | tf_op jit(solution)/shard_map/ppermute | solution.py:579
  56.7 3.6 %collective-permute-start.10 = (bf16[48,24,128]{2,1,0:T(8,128)(2,1)S(1)}, bf16[48,24,128]{2,1,0:T(8,128)(2,1)S(1)}, u32[]{:S(2)}, u32[]{:S(2)}) collective-permute-start(bf16[48,24,128]{2,1,0:T(8,128)(2,1)S(1)} %collective-permute-done.8.rest_1_), channel_id=1, source_target_pairs={{0,4},{4,8},{8,12},{1,5},{5,9},{9,13},{2,6},{6,10},{10,14},{3,7},{... | collective-permute-start | bytes 884744 | tf_op jit(solution)/shard_map/ppermute | solution.py:579
  60.4 1.5 %collective-permute-start.12 = (bf16[48,24,128]{2,1,0:T(8,128)(2,1)S(1)}, bf16[48,24,128]{2,1,0:T(8,128)(2,1)S(1)}, u32[]{:S(2)}, u32[]{:S(2)}) collective-permute-start(bf16[48,24,128]{2,1,0:T(8,128)(2,1)S(1)} %collective-permute-done.8.rest_1_), channel_id=1, source_target_pairs={{4,0},{8,4},{12,8},{5,1},{9,5},{13,9},{6,2},{10,6},{14,10},{7,3},{... | collective-permute-start | bytes 884744 | tf_op jit(solution)/shard_map/ppermute | solution.py:579
  61.8 6.5 %shard_map.76 = (bf16[48,24,128]{2,1,0:T(8,128)(2,1)}, bf16[48,24,128]{2,1,0:T(8,128)(2,1)}) custom-call(s32[1]{0:T(128)} %bitcast.2.sub_ref, bf16[2,32,768]{2,1,0:T(8,128)(2,1)} %get-tuple-element.52.l_ref, bf16[2,32,768]{2,1,0:T(8,128)(2,1)} %copy-done.23, bf16[32,96,64]{2,1,0:T(8,128)(2,1)} %shard_map.73.rt_ref, ...), custom_call_target="tpu_custom_call" | custom-call | flops 1283457024 | bytes 7077888 | tf_op jit(solution)/shard_map/pallas_call | solution.py:214
  68.5 0.7 collective-permute-start.16
  69.2 1.3 %collective-permute-start.18 = (bf16[48,24,128]{2,1,0:T(8,128)(2,1)S(1)}, bf16[48,24,128]{2,1,0:T(8,128)(2,1)S(1)}, u32[]{:S(2)}, u32[]{:S(2)}) collective-permute-start(bf16[48,24,128]{2,1,0:T(8,128)(2,1)S(1)} %collective-permute-done.11.rest_4_), channel_id=1, source_target_pairs={{4,0},{8,4},{5,1},{9,5},{6,2},{10,6},{7,3},{11,7},{20,16},{24,20},... | collective-permute-start | bytes 884744 | tf_op jit(solution)/shard_map/ppermute | solution.py:579
  70.5 0.7 collective-permute-start.17
  71.2 1.3 %collective-permute-start.19 = (bf16[48,24,128]{2,1,0:T(8,128)(2,1)S(1)}, bf16[48,24,128]{2,1,0:T(8,128)(2,1)S(1)}, u32[]{:S(2)}, u32[]{:S(2)}) collective-permute-start(bf16[48,24,128]{2,1,0:T(8,128)(2,1)S(1)} %collective-permute-done.12.rest_5_), channel_id=1, source_target_pairs={{4,0},{8,4},{5,1},{9,5},{6,2},{10,6},{7,3},{11,7},{20,16},{24,20},... | collective-permute-start | bytes 884744 | tf_op jit(solution)/shard_map/ppermute | solution.py:579
  73.1 0.7 copy-done.13
  73.8 5.8 %shard_map.77 = (bf16[24,24,128]{2,1,0:T(8,128)(2,1)}, bf16[24,24,128]{2,1,0:T(8,128)(2,1)}, bf16[24,24,128]{2,1,0:T(8,128)(2,1)}, bf16[24,24,128]{2,1,0:T(8,128...) custom-call(s32[3]{0:T(128)} %pad_add_fusion.pos_ref, bf16[64,24,128]{2,1,0:T(8,128)(2,1)} %get-tuple-element.28.lk_ref, ...), custom_call_target="tpu_custom_call" | custom-call | flops 452984832 | bytes 3538944 | tf_op jit(solution)/shard_map/pallas_call | solution.py:499
  80.4 2.4 %collective-permute-done.18.rest_2_ = bf16[48,24,128]{2,1,0:T(8,128)(2,1)S(1)} collective-permute-done((bf16[48,24,128]{2,1,0:T(8,128)(2,1)S(1)}, bf16[48,24,128]{2,1,0:T(8,128)(2,1)S(1)}, u32[]{:S(2)}, u32[]{:S(2)}) %collective-permute-start.18) | collective-permute-done | bytes 294944 | tf_op jit(solution)/shard_map/ppermute | solution.py:579
  82.8 5.8 %collective-permute-done.19.rest_3_ = bf16[48,24,128]{2,1,0:T(8,128)(2,1)S(1)} collective-permute-done((bf16[48,24,128]{2,1,0:T(8,128)(2,1)S(1)}, bf16[48,24,128]{2,1,0:T(8,128)(2,1)S(1)}, u32[]{:S(2)}, u32[]{:S(2)}) %collective-permute-start.19) | collective-permute-done | bytes 294944 | tf_op jit(solution)/shard_map/ppermute | solution.py:579
  88.6 0.7 copy-done.7
  89.3 4.1 %shard_map.78 = (bf16[24,24,128]{2,1,0:T(8,128)(2,1)}, bf16[24,24,128]{2,1,0:T(8,128)(2,1)}, bf16[24,24,128]{2,1,0:T(8,128)(2,1)}, bf16[24,24,128]{2,1,0:T(8,128)(2,1)}) custom-call(s32[3]{0:T(128)} %pad_add_fusion.pos_ref, bf16[64,24,128]{2,1,0:T(8,128)(2,1)} %get-tuple-element.28.lk_ref, bf16[64,24,128]{2,1,0:T(8,128)(2,1)} %copy-done.2, ...), custom_call_target="tpu_custom_call" | custom-call | flops 150994944 | bytes 1179648 | tf_op jit(solution)/shard_map/pallas_call | solution.py:499
  94.0 1.6 %collective-permute-start.24 = (bf16[24,24,128]{2,1,0:T(8,128)(2,1)}, bf16[24,24,128]{2,1,0:T(8,128)(2,1)S(1)}, u32[]{:S(2)}, u32[]{:S(2)}) collective-permute-start(bf16[24,24,128]{2,1,0:T(8,128)(2,1)} %get-tuple-element.43), channel_id=1, source_target_pairs={{0,3},{1,2},{2,1},{3,0},{4,7},{5,6},{6,5},{7,4},{8,11},{9,10},{10,... | collective-permute-start | bytes 442376 | tf_op jit(solution)/shard_map/ppermute | solution.py:584
  95.6 4.8 %collective-permute-done.20.rest_3_ = bf16[24,24,128]{2,1,0:T(8,128)(2,1)S(1)} collective-permute-done((bf16[24,24,128]{2,1,0:T(8,128)(2,1)}, bf16[24,24,128]{2,1,0:T(8,128)(2,1)S(1)}, u32[]{:S(2)}, u32[]{:S(2)}) %collective-permute-start.20) | collective-permute-done | bytes 147488 | tf_op jit(solution)/shard_map/ppermute | solution.py:574
  101.5 5.1 %shard_map.79 = bf16[24,96,128]{2,1,0:T(8,128)(2,1)} custom-call(s32[3]{0:T(128)} %pad_add_fusion.pos_ref, bf16[24,24,128]{2,1,0:T(8,128)(2,1)} %get-tuple-element.34.rest_0_, bf16[24,24,128]{2,1,0:T(8,128)(2,1)} %copy-done.15, bf16[24,24,128]{2,1,0:T(8,128)(2,1)} %get-tuple-element.38.rest_2_, bf16[24,24,128]{2,1,0:T(8,128)(2,1)} %copy-done.18, ...), custom_call_target="tpu_custom_call" | custom-call | tf_op jit(solution)/shard_map/pallas_call | solution.py:562
  (99 shorter events, 7.1 us)
Async XLA Ops:
  2.3 5.9 %copy-start.21 = (bf16[256,32]{0,1:T(8,128)(2,1)S(1)}, bf16[256,32]{0,1:T(8,128)(2,1)}, u32[]{:S(2)}) copy-start(bf16[256,32]{0,1:T(8,128)(2,1)} %param.9) | copy-start | bytes 49156
  2.5 15.9 %collective-permute-start.2 = (bf16[16,1536]{1,0:T(8,128)(2,1)S(1)}, bf16[16,1536]{1,0:T(8,128)(2,1)S(1)}, u32[]{:S(2)}, u32[]{:S(2)}) collective-permute-start(bf16[16,1536]{1,0:T(8,128)(2,1)S(1)} %reshape.23), channel_id=1, source_target_pairs={{0,4},{4,0},{8,12},{12,8},{1,5},{5,1},{9,13},{13,9},{2,6},{6,2},{1... | collective-permute-start | bytes 147464 | tf_op jit(solution)/shard_map/ppermute | solution.py:617
  5.7 12.8 %collective-permute-start.3 = (bf16[16,1536]{1,0:T(8,128)(2,1)S(1)}, bf16[16,1536]{1,0:T(8,128)(2,1)S(1)}, u32[]{:S(2)}, u32[]{:S(2)}) collective-permute-start(bf16[16,1536]{1,0:T(8,128)(2,1)S(1)} %reshape.23), channel_id=1, source_target_pairs={{0,8},{4,12},{8,0},{12,4},{1,9},{5,13},{9,1},{13,5},{2,10},{6,14},... | collective-permute-start | bytes 147464 | tf_op jit(solution)/shard_map/ppermute | solution.py:617
  8.9 7.8 %collective-permute-start = (bf16[16,1536]{1,0:T(8,128)(2,1)S(1)}, bf16[16,1536]{1,0:T(8,128)(2,1)S(1)}, u32[]{:S(2)}, u32[]{:S(2)}) collective-permute-start(bf16[16,1536]{1,0:T(8,128)(2,1)S(1)} %reshape.22), channel_id=1, source_target_pairs={{0,2},{2,0},{1,3},{3,1},{4,6},{6,4},{5,7},{7,5},{8,10},{10,8},{9,1... | collective-permute-start | bytes 147464 | tf_op jit(solution)/shard_map/ppermute | solution.py:574
  10.8 7.6 %collective-permute-start.1 = (bf16[2,16,1536]{2,1,0:T(8,128)(2,1)S(1)}, bf16[2,16,1536]{2,1,0:T(8,128)(2,1)S(1)}, u32[]{:S(2)}, u32[]{:S(2)}) collective-permute-start(bf16[2,16,1536]{2,1,0:T(8,128)(2,1)S(1)} %pad_maximum_fusion.3), channel_id=1, source_target_pairs={{0,12},{4,8},{8,4},{12,0},{1,13},{5,9},{9,5},{13,1},{2,14},{6,10},... | collective-permute-start | bytes 294920 | tf_op jit(solution)/shard_map/ppermute | solution.py:617
  11.1 49.2 %collective-permute-start.13 = (bf16[24,96,128]{2,1,0:T(8,128)(2,1)S(1)}, bf16[24,96,128]{2,1,0:T(8,128)(2,1)}, u32[]{:S(2)}, u32[]{:S(2)}) collective-permute-start(bf16[24,96,128]{2,1,0:T(8,128)(2,1)S(1)} %copy-done.22), channel_id=1, source_target_pairs={{0,12},{12,0},{1,13},{13,1},{2,14},{14,2},{3,15},{15,3},{16,28},{2... | collective-permute-start | bytes 1769480 | tf_op jit(solution)/shard_map/ppermute | solution.py:628
  18.5 5.2 %collective-permute-start.4 = (bf16[3,16,1536]{2,1,0:T(8,128)(2,1)S(1)}, bf16[3,16,1536]{2,1,0:T(8,128)(2,1)S(1)}, u32[]{:S(2)}, u32[]{:S(2)}) collective-permute-start(bf16[3,16,1536]{2,1,0:T(8,128)(2,1)S(1)} %pad_maximum_fusion.2), channel_id=1, source_target_pairs={{0,2},{2,0},{1,3},{3,1},{4,6},{6,4},{5,7},{7,5},{8,10},{10,8},{9,1... | collective-permute-start | bytes 442376 | tf_op jit(solution)/shard_map/ppermute | solution.py:574
  23.8 3.5 %collective-permute-start.6 = (bf16[2,2,16,1536]{3,2,1,0:T(8,128)(2,1)S(1)}, bf16[2,2,16,1536]{3,2,1,0:T(8,128)(2,1)S(1)}, u32[]{:S(2)}, u32[]{:S(2)}) collective-permute-start(bf16[2,2,16,1536]{3,2,1,0:T(8,128)(2,1)S(1)} %pad_maximum_fusion.1.own_ref), channel_id=1, source_target_pairs={{0,1},{1,0},{2,3},{3,2},{4,5},{5,4},{6,7},{7,6},{8,9},{9,8},{10,11... | collective-permute-start | bytes 589832 | tf_op jit(solution)/shard_map/ppermute | solution.py:574
  24.6 6.5 %collective-permute-start.5 = (bf16[2,32,768]{2,1,0:T(8,128)(2,1)S(1)}, bf16[2,32,768]{2,1,0:T(8,128)(2,1)S(1)}, u32[]{:S(2)}, u32[]{:S(2)}) collective-permute-start(bf16[2,32,768]{2,1,0:T(8,128)(2,1)S(1)} %get-tuple-element.51), channel_id=1, source_target_pairs={{0,1},{1,0},{2,3},{3,2},{4,5},{5,4},{6,7},{7,6},{8,9},{9,8},{10,11... | collective-permute-start | bytes 294920 | tf_op jit(solution)/shard_map/ppermute | solution.py:574
  40.0 16.7 %collective-permute-start.8 = (bf16[48,24,128]{2,1,0:T(8,128)(2,1)}, bf16[48,24,128]{2,1,0:T(8,128)(2,1)S(1)}, u32[]{:S(2)}, u32[]{:S(2)}) collective-permute-start(bf16[48,24,128]{2,1,0:T(8,128)(2,1)} %get-tuple-element.31), channel_id=1, source_target_pairs={{0,1},{1,0},{2,3},{3,2},{4,5},{5,4},{6,7},{7,6},{8,9},{9,8},{10,11... | collective-permute-start | bytes 884744 | tf_op jit(solution)/shard_map/ppermute | solution.py:574
  40.0 28.3 %collective-permute-start.11 = (bf16[48,24,128]{2,1,0:T(8,128)(2,1)}, bf16[48,24,128]{2,1,0:T(8,128)(2,1)S(1)}, u32[]{:S(2)}, u32[]{:S(2)}) collective-permute-start(bf16[48,24,128]{2,1,0:T(8,128)(2,1)} %get-tuple-element.30.rest_0_), channel_id=1, source_target_pairs={{4,0},{8,4},{12,8},{5,1},{9,5},{13,9},{6,2},{10,6},{14,10},{7,3},{... | collective-permute-start | bytes 884744 | tf_op jit(solution)/shard_map/ppermute | solution.py:579
  41.3 27.8 %collective-permute-start.7 = (bf16[64,24,128]{2,1,0:T(8,128)(2,1)}, bf16[64,24,128]{2,1,0:T(8,128)(2,1)S(1)}, u32[]{:S(2)}, u32[]{:S(2)}) collective-permute-start(bf16[64,24,128]{2,1,0:T(8,128)(2,1)} %get-tuple-element.29), channel_id=1, source_target_pairs={{0,1},{1,0},{2,3},{3,2},{4,5},{5,4},{6,7},{7,6},{8,9},{9,8},{10,11... | collective-permute-start | bytes 1179656 | tf_op jit(solution)/shard_map/ppermute | solution.py:574
  41.9 26.6 %collective-permute-start.9 = (bf16[48,24,128]{2,1,0:T(8,128)(2,1)}, bf16[48,24,128]{2,1,0:T(8,128)(2,1)S(1)}, u32[]{:S(2)}, u32[]{:S(2)}) collective-permute-start(bf16[48,24,128]{2,1,0:T(8,128)(2,1)} %get-tuple-element.30.rest_0_), channel_id=1, source_target_pairs={{0,4},{4,8},{8,12},{1,5},{5,9},{9,13},{2,6},{6,10},{10,14},{3,7},{... | collective-permute-start | bytes 884744 | tf_op jit(solution)/shard_map/ppermute | solution.py:579
  56.7 11.7 %copy-start.10 = (bf16[48,24,128]{2,1,0:T(8,128)(2,1)}, bf16[48,24,128]{2,1,0:T(8,128)(2,1)S(1)}, u32[]{:S(2)}) copy-start(bf16[48,24,128]{2,1,0:T(8,128)(2,1)S(1)} %collective-permute-done.8.rest_1_) | copy-start | bytes 884740
  56.7 13.8 %collective-permute-start.10 = (bf16[48,24,128]{2,1,0:T(8,128)(2,1)S(1)}, bf16[48,24,128]{2,1,0:T(8,128)(2,1)S(1)}, u32[]{:S(2)}, u32[]{:S(2)}) collective-permute-start(bf16[48,24,128]{2,1,0:T(8,128)(2,1)S(1)} %collective-permute-done.8.rest_1_), channel_id=1, source_target_pairs={{0,4},{4,8},{8,12},{1,5},{5,9},{9,13},{2,6},{6,10},{10,14},{3,7},{... | collective-permute-start | bytes 884744 | tf_op jit(solution)/shard_map/ppermute | solution.py:579
  60.4 10.8 %collective-permute-start.12 = (bf16[48,24,128]{2,1,0:T(8,128)(2,1)S(1)}, bf16[48,24,128]{2,1,0:T(8,128)(2,1)S(1)}, u32[]{:S(2)}, u32[]{:S(2)}) collective-permute-start(bf16[48,24,128]{2,1,0:T(8,128)(2,1)S(1)} %collective-permute-done.8.rest_1_), channel_id=1, source_target_pairs={{4,0},{8,4},{12,8},{5,1},{9,5},{13,9},{6,2},{10,6},{14,10},{7,3},{... | collective-permute-start | bytes 884744 | tf_op jit(solution)/shard_map/ppermute | solution.py:579
  68.4 4.7 %collective-permute-start.14 = (bf16[48,24,128]{2,1,0:T(8,128)(2,1)}, bf16[48,24,128]{2,1,0:T(8,128)(2,1)S(1)}, u32[]{:S(2)}, u32[]{:S(2)}) collective-permute-start(bf16[48,24,128]{2,1,0:T(8,128)(2,1)} %get-tuple-element.33), channel_id=1, source_target_pairs={{0,1},{1,0},{2,3},{3,2},{4,5},{5,4},{6,7},{7,6},{8,9},{9,8},{10,11... | collective-permute-start | bytes 884744 | tf_op jit(solution)/shard_map/ppermute | solution.py:574
  68.5 11.8 %collective-permute-start.16 = (bf16[48,24,128]{2,1,0:T(8,128)(2,1)S(1)}, bf16[48,24,128]{2,1,0:T(8,128)(2,1)S(1)}, u32[]{:S(2)}, u32[]{:S(2)}) collective-permute-start(bf16[48,24,128]{2,1,0:T(8,128)(2,1)S(1)} %collective-permute-done.9.rest_2_), channel_id=1, source_target_pairs={{4,8},{8,12},{5,9},{9,13},{6,10},{10,14},{7,11},{11,15},{20,24},{2... | collective-permute-start | bytes 884744 | tf_op jit(solution)/shard_map/ppermute | solution.py:579
  69.2 13.6 %collective-permute-start.18 = (bf16[48,24,128]{2,1,0:T(8,128)(2,1)S(1)}, bf16[48,24,128]{2,1,0:T(8,128)(2,1)S(1)}, u32[]{:S(2)}, u32[]{:S(2)}) collective-permute-start(bf16[48,24,128]{2,1,0:T(8,128)(2,1)S(1)} %collective-permute-done.11.rest_4_), channel_id=1, source_target_pairs={{4,0},{8,4},{5,1},{9,5},{6,2},{10,6},{7,3},{11,7},{20,16},{24,20},... | collective-permute-start | bytes 884744 | tf_op jit(solution)/shard_map/ppermute | solution.py:579
  70.5 12.3 %collective-permute-start.17 = (bf16[48,24,128]{2,1,0:T(8,128)(2,1)S(1)}, bf16[48,24,128]{2,1,0:T(8,128)(2,1)S(1)}, u32[]{:S(2)}, u32[]{:S(2)}) collective-permute-start(bf16[48,24,128]{2,1,0:T(8,128)(2,1)S(1)} %collective-permute-done.10.rest_3_), channel_id=1, source_target_pairs={{4,8},{8,12},{5,9},{9,13},{6,10},{10,14},{7,11},{11,15},{20,24},{2... | collective-permute-start | bytes 884744 | tf_op jit(solution)/shard_map/ppermute | solution.py:579
  71.2 17.4 %collective-permute-start.19 = (bf16[48,24,128]{2,1,0:T(8,128)(2,1)S(1)}, bf16[48,24,128]{2,1,0:T(8,128)(2,1)S(1)}, u32[]{:S(2)}, u32[]{:S(2)}) collective-permute-start(bf16[48,24,128]{2,1,0:T(8,128)(2,1)S(1)} %collective-permute-done.12.rest_5_), channel_id=1, source_target_pairs={{4,0},{8,4},{5,1},{9,5},{6,2},{10,6},{7,3},{11,7},{20,16},{24,20},... | collective-permute-start | bytes 884744 | tf_op jit(solution)/shard_map/ppermute | solution.py:579
  79.6 14.4 %collective-permute-start.15 = (bf16[24,24,128]{2,1,0:T(8,128)(2,1)}, bf16[24,24,128]{2,1,0:T(8,128)(2,1)S(1)}, u32[]{:S(2)}, u32[]{:S(2)}) collective-permute-start(bf16[24,24,128]{2,1,0:T(8,128)(2,1)} %get-tuple-element.35), channel_id=1, source_target_pairs={{0,2},{2,0},{1,3},{3,1},{4,6},{6,4},{5,7},{7,5},{8,10},{10,8},{9,1... | collective-permute-start | bytes 442376 | tf_op jit(solution)/shard_map/ppermute | solution.py:574
  80.2 8.4 %copy-start.4 = (bf16[48,24,128]{2,1,0:T(8,128)(2,1)}, bf16[48,24,128]{2,1,0:T(8,128)(2,1)S(1)}, u32[]{:S(2)}) copy-start(bf16[48,24,128]{2,1,0:T(8,128)(2,1)S(1)} %collective-permute-done.16.rest_0_) | copy-start | bytes 884740
  80.2 15.4 %collective-permute-start.21 = (bf16[24,24,128]{2,1,0:T(8,128)(2,1)}, bf16[24,24,128]{2,1,0:T(8,128)(2,1)S(1)}, u32[]{:S(2)}, u32[]{:S(2)}) collective-permute-start(bf16[24,24,128]{2,1,0:T(8,128)(2,1)} %get-tuple-element.40), channel_id=1, source_target_pairs={{0,1},{1,0},{2,3},{3,2},{4,5},{5,4},{6,7},{7,6},{8,9},{9,8},{10,11... | collective-permute-start | bytes 442376 | tf_op jit(solution)/shard_map/ppermute | solution.py:574
  82.8 5.8 %copy-start.5 = (bf16[48,24,128]{2,1,0:T(8,128)(2,1)}, bf16[48,24,128]{2,1,0:T(8,128)(2,1)S(1)}, u32[]{:S(2)}) copy-start(bf16[48,24,128]{2,1,0:T(8,128)(2,1)S(1)} %collective-permute-done.18.rest_2_) | copy-start | bytes 884740
  82.8 12.8 %collective-permute-start.22 = (bf16[24,24,128]{2,1,0:T(8,128)(2,1)}, bf16[24,24,128]{2,1,0:T(8,128)(2,1)S(1)}, u32[]{:S(2)}, u32[]{:S(2)}) collective-permute-start(bf16[24,24,128]{2,1,0:T(8,128)(2,1)} %get-tuple-element.41), channel_id=1, source_target_pairs={{0,3},{1,2},{2,1},{3,0},{4,7},{5,6},{6,5},{7,4},{8,11},{9,10},{10,... | collective-permute-start | bytes 442376 | tf_op jit(solution)/shard_map/ppermute | solution.py:584
  82.8 5.8 %copy-start.6 = (bf16[48,24,128]{2,1,0:T(8,128)(2,1)}, bf16[48,24,128]{2,1,0:T(8,128)(2,1)S(1)}, u32[]{:S(2)}) copy-start(bf16[48,24,128]{2,1,0:T(8,128)(2,1)S(1)} %collective-permute-done.17.rest_1_) | copy-start | bytes 884740
  93.4 7.0 %collective-permute-start.20 = (bf16[24,24,128]{2,1,0:T(8,128)(2,1)}, bf16[24,24,128]{2,1,0:T(8,128)(2,1)S(1)}, u32[]{:S(2)}, u32[]{:S(2)}) collective-permute-start(bf16[24,24,128]{2,1,0:T(8,128)(2,1)} %get-tuple-element.39), channel_id=1, source_target_pairs={{0,2},{2,0},{1,3},{3,1},{4,6},{6,4},{5,7},{7,5},{8,10},{10,8},{9,1... | collective-permute-start | bytes 442376 | tf_op jit(solution)/shard_map/ppermute | solution.py:574
  94.0 6.4 %collective-permute-start.23 = (bf16[24,24,128]{2,1,0:T(8,128)(2,1)}, bf16[24,24,128]{2,1,0:T(8,128)(2,1)S(1)}, u32[]{:S(2)}, u32[]{:S(2)}) collective-permute-start(bf16[24,24,128]{2,1,0:T(8,128)(2,1)} %get-tuple-element.42), channel_id=1, source_target_pairs={{0,1},{1,0},{2,3},{3,2},{4,5},{5,4},{6,7},{7,6},{8,9},{9,8},{10,11... | collective-permute-start | bytes 442376 | tf_op jit(solution)/shard_map/ppermute | solution.py:574
  94.0 6.9 %copy-start.15 = (bf16[24,24,128]{2,1,0:T(8,128)(2,1)}, bf16[24,24,128]{2,1,0:T(8,128)(2,1)S(1)}, u32[]{:S(2)}) copy-start(bf16[24,24,128]{2,1,0:T(8,128)(2,1)S(1)} %collective-permute-done.15.rest_1_) | copy-start | bytes 442372
  94.0 6.9 %collective-permute-start.24 = (bf16[24,24,128]{2,1,0:T(8,128)(2,1)}, bf16[24,24,128]{2,1,0:T(8,128)(2,1)S(1)}, u32[]{:S(2)}, u32[]{:S(2)}) collective-permute-start(bf16[24,24,128]{2,1,0:T(8,128)(2,1)} %get-tuple-element.43), channel_id=1, source_target_pairs={{0,3},{1,2},{2,1},{3,0},{4,7},{5,6},{6,5},{7,4},{8,11},{9,10},{10,... | collective-permute-start | bytes 442376 | tf_op jit(solution)/shard_map/ppermute | solution.py:584
  95.6 5.3 %copy-start.16 = (bf16[24,24,128]{2,1,0:T(8,128)(2,1)}, bf16[24,24,128]{2,1,0:T(8,128)(2,1)S(1)}, u32[]{:S(2)}) copy-start(bf16[24,24,128]{2,1,0:T(8,128)(2,1)S(1)} %collective-permute-done.21.rest_4_) | copy-start | bytes 442372
  (17 other events, 34.5 us)
where the time goes:
time: 108 us; the launch traced here: 107 us
  starting transfers between devices  43 us (40%)
  Pallas kernels  35.1 us (32%)
  waiting for transfers between devices  19.8 us (18%)
  local copies, waits for them, and re-layouts  4.59 us (4%)
  other arithmetic  3.21 us (3%)
    ppermute x8, starting transfers between devices, step_along(): lax.ppermute(x, axis, [(i, i + d) for i in range(n) if 0 <= i + d < n and...  25.1 us
    pallas_call x2, Pallas kernels, pair(): return f(sub, l, lr, rt, wt, e, went)  14.8 us
    pallas_call x2, Pallas kernels, split_call(): pl.pallas_call(functools.partial(kernel, J, n), out_shape=[jax.ShapeDtype...  9.87 us
    ppermute x11, waiting for transfers between devices, shift(): return lax.ppermute(x, axis, [(i, (i + d) % n) for i in range(n)])  9.38 us
    ppermute x8, waiting for transfers between devices, step_along(): lax.ppermute(x, axis, [(i, i + d) for i in range(n) if 0 <= i + d < n and...  8.23 us
    ppermute x3, starting transfers between devices, per_device(): lax.ppermute(x, 'row', [(i, i ^ d) for i in range(nr)])  5.99 us
    ppermute x1, starting transfers between devices, per_device(): lax.ppermute(edge_activations, 'row', [(0, nr - 1), (nr - 1, 0)])  5.5 us
    pallas_call x1, Pallas kernels, final_pairs(): pl.pallas_call(functools.partial(final_pairs_kernel, (C, J)), out_shape=j...  5.06 us
  transfers between devices with their start and end apart: 25, of which 6 were waited for; matrix products, arithmetic and copies ran while one was open for 2% of the time, Pallas kernels for 28%

commit v1 on v0

--- a/solution.py
+++ b/solution.py
@@ -369,32 +369,28 @@
     parts, main = packing(half, J)
     spare = LANES - J
     inside = lane_index((2 * TI, LANES)) < J
-    for ch in range(half):
-        x = jnp.concatenate([lk_ref[ch], lr_ref[ch]], axis=0)
-        if ch < main:
-            lm[ch] = x
-        else:
-            f = x.astype(jnp.float32)
-            for t in range(parts):
-                moved = pltpu.roll(f, J - spare * t, 1)
-                lm[main + (ch - main) * parts + t] = jnp.where(inside, 0.0, moved).astype(jnp.bfloat16)
-
-
-def shard_products(lm, rv, k, J, half, TI, store):
+    for ch in range(main, half):
+        f = jnp.concatenate([lk_ref[ch], lr_ref[ch]], axis=0).astype(jnp.float32)
+        for t in range(parts):
+            moved = pltpu.roll(f, J - spare * t, 1)
+            lm[(ch - main) * parts + t] = jnp.where(inside, 0.0, moved).astype(jnp.bfloat16)
+
+
+def shard_products(lk_ref, lr_ref, lm, rv, k, J, half, TI, store):
     parts, main = packing(half, J)
     tails = half - main
 
     def dot(left, row):
         right = rv[k, :, row].reshape(2 * TI, LANES)
-        return lax.dot_general(lm[left], right, (((1,), (1,)), ((), ())), preferred_element_type=jnp.float32)
+        return lax.dot_general(left, right, (((1,), (1,)), ((), ())), preferred_element_type=jnp.float32)
 
     def channel(ch):
         if ch < main:
-            return dot(ch, ch)
+            return dot(jnp.concatenate([lk_ref[ch], lr_ref[ch]], axis=0), ch)
         q = ch - main
-        x = dot(main + q * parts, q)
+        x = dot(lm[q * parts], q)
         for t in range(1, parts):
-            x = x + dot(main + q * parts + t, t * tails + q)
+            x = x + dot(lm[q * parts + t], t * tails + q)
         return x
 
     pairs = half // 2
@@ -417,21 +413,13 @@
 
 
 def early_kernel(J, n, pos_ref, lk_ref, lr_ref, *rest):
-    own, up, down, far = rest[0:2], rest[2:4], rest[4:6], rest[6:8]
+    own, near, mids, far = rest[0:2], rest[2:4], rest[4:6], rest[6:8]
     outs = rest[8:14]
     rv, lm, acc, sem = rest[14:]
     half, TI, _ = lk_ref.shape
     row, col, sub = pos_ref[0], pos_ref[1], pos_ref[2]
-    even = lax.rem(row, 2) == 0
     edge = (row == 0) | (row == n - 1)
-    plan = [
-        (None, own, 0),
-        (even, down, 1),
-        (jnp.logical_not(even), up, 1),
-        (edge, far, 2),
-        (jnp.logical_not(edge) & even, up, 2),
-        (jnp.logical_not(edge) & jnp.logical_not(even), down, 2),
-    ]
+    plan = [(None, own, 0), (None, near, 1), (edge, far, 2), (jnp.logical_not(edge), mids, 2)]
 
     def each(action):
         for cond, refs, k in plan:
@@ -450,7 +438,7 @@
         def store(r, x, k=k):
             acc[k, r] = x
 
-        shard_products(lm, rv, k, J, half, TI, store)
+        shard_products(lk_ref, lr_ref, lm, rv, k, J, half, TI, store)
     home = col == row // 2
     send = jnp.where(home, acc[2], acc[0])
     keep = jnp.where(home, acc[0], acc[2])
@@ -461,15 +449,15 @@
 
 
 def late_kernel(J, n, pos_ref, lk_ref, lr_ref, a_ref, b_ref, *rest):
-    up, down = rest[0:2], rest[2:4]
+    inner, outward = rest[0:2], rest[2:4]
     outs = rest[4:8]
     rv, lm, acc, sem = rest[8:]
     half, TI, _ = lk_ref.shape
     row, col, sub = pos_ref[0], pos_ref[1], pos_ref[2]
-    low = row < 2
+    edge = (row == 0) | (row == n - 1)
 
     def each(action):
-        for cond, refs in ((low, down), (jnp.logical_not(low), up)):
+        for cond, refs in ((edge, outward), (jnp.logical_not(edge), inner)):
             for u in range(2):
                 c = pltpu.make_async_copy(refs[u], rv.at[0, sub if u == 0 else 1 - sub], sem.at[u])
                 pl.when(cond)(lambda c=c: action(c))
@@ -481,7 +469,7 @@
     def store(r, x):
         acc[r] = x
 
-    shard_products(lm, rv, 0, J, half, TI, store)
+    shard_products(lk_ref, lr_ref, lm, rv, 0, J, half, TI, store)
     home = col == row // 2
     for u, ref in enumerate((a_ref, b_ref)):
         late = acc[:, u * TI : (u + 1) * TI]
@@ -503,7 +491,7 @@
         out_specs=[vmem()] * n_out,
         scratch_shapes=[
             pltpu.VMEM((shards, 2, main, TI, LANES), bf),
-            pltpu.VMEM((main + (half - main) * max(parts, 1), 2 * TI, LANES), bf),
+            pltpu.VMEM(((half - main) * max(parts, 1), 2 * TI, LANES), bf),
             pltpu.VMEM((shards,) + acc if shards > 1 else acc, bf),
             pltpu.SemaphoreType.DMA(sems),
         ],
@@ -512,61 +500,103 @@
     )(pos, lk, lr, *extra, *slots)
 
 
-def final_pairs_kernel(cfg, pos_ref, *rest):
-    C, _ = cfg
-    own = (rest[0:2], rest[2:4])
-    other = (rest[4:6], rest[6:8])
-    mid_ref, gate_ref, wx_ref, out_ref, sc, nts = rest[8:]
-    TI = mid_ref.shape[0]
+def add_group(C, TI, own, other, sub, sc):
     half = C // 2
     pairs = half // 2
     cols = 4 * TI
     parts, main = packing(pairs, cols)
     tails = pairs - main
     spare = LANES - cols
-    row, col, sub = pos_ref[0], pos_ref[1], pos_ref[2]
-    home = col == row // 2
-    odd = lax.rem(row, 2) == 1
-    first = jnp.where(home, jnp.logical_not(odd), odd)
     lanes = lane_index((TI, LANES))
-    low = lanes < 2 * TI
-    for groups, base in ((own, sub * half), (other, (1 - sub) * half)):
-
-        def place(q, both):
-            a = jnp.where(first, both[0], both[1])
-            b = jnp.where(first, both[1], both[0])
-            x = jnp.where(low, a, pltpu.roll(b, 2 * TI, 1))
-            y = jnp.where(low, pltpu.roll(a, LANES - 2 * TI, 1), b)
+    for refs, base in ((own, sub * pairs), (other, (1 - sub) * pairs)):
+
+        def put(q, x, base=base):
             sc[pl.ds((base + q) * TI, TI), :] = x
-            sc[pl.ds((base + q + pairs) * TI, TI), :] = y
-
-        def total(g, r):
-            x = groups[g][0][r].astype(jnp.float32) + groups[g][1][r].astype(jnp.float32)
+
+        def total(r, refs=refs):
+            x = refs[0][r].astype(jnp.float32) + refs[1][r].astype(jnp.float32)
             return x.astype(jnp.bfloat16).astype(jnp.float32)
 
         for q in range(tails if parts else 0):
-            tail = [jnp.zeros((TI, LANES), jnp.float32)] * 2
+            tail = jnp.zeros((TI, LANES), jnp.float32)
             for t in range(parts):
-                x = [total(g, t * tails + q) for g in range(2)]
-                place(t * tails + q, x)
+                x = total(t * tails + q)
+                put(t * tails + q, x)
                 part = (lanes >= spare * t) & (lanes < spare * (t + 1))
-                tail = [jnp.where(part, pltpu.roll(x[g], LANES - cols + spare * t, 1), tail[g]) for g in range(2)]
-            place(main + q, tail)
+                tail = jnp.where(part, pltpu.roll(x, LANES - cols + spare * t, 1), tail)
+            put(main + q, tail)
         for q in range(0 if parts else pairs):
-            place(q, [total(g, q) for g in range(2)])
-    finish(sc, nts, mid_ref, gate_ref, wx_ref, out_ref)
-
-
-def final_pairs(pos, pieces, mid, gate, wx):
-    TI, C, J = mid.shape
+            put(q, total(q))
+
+
+def group_updates(C, TI, sc, nts, wx_ref, emit):
+    span = 2 * TI
+    pairs = C // 4
+    low = lane_index((C // 2, LANES)) < span
+    for h in range(TI // 2):
+        a = sc[pl.ds(2 * h, C // 2, stride=TI), :]
+        b = sc[pl.ds(2 * h + 1, C // 2, stride=TI), :]
+        x = jnp.where(low, a, pltpu.roll(b, span, 1))
+        y = jnp.where(low, pltpu.roll(a, LANES - span, 1), b)
+        tri = jnp.concatenate([x[:pairs], y[:pairs], x[pairs:], y[pairs:]], axis=0)
+        nts[h // 2, :, h % 2 * LANES : (h % 2 + 1) * LANES] = standardize_columns(tri).astype(jnp.bfloat16)
+    wx = wx_ref[...]
+    for g in range(TI // 4):
+        update = lax.dot_general(wx, nts[g], (((1,), (0,)), ((), ())), preferred_element_type=jnp.float32)
+        for k in range(2):
+            x = update[:, k * LANES : (k + 1) * LANES].T
+            emit(4 * g + 2 * k, x[:span])
+            emit(4 * g + 2 * k + 1, x[span : 2 * span])
+
+
+def lower_half_first(pos_ref):
+    home = pos_ref[1] == pos_ref[0] // 2
+    odd = lax.rem(pos_ref[0], 2) == 1
+    return jnp.where(home, jnp.logical_not(odd), odd)
+
+
+def finish_early_kernel(pos_ref, a_ref, b_ref, c_ref, d_ref, mid_ref, gate_ref, wx_ref, out_ref, m_ref, g_ref, sc, nts):
+    TI, C, _ = mid_ref.shape
+    span = 2 * TI
+    first = lower_half_first(pos_ref)
+    add_group(C, TI, (a_ref, b_ref), (c_ref, d_ref), pos_ref[2], sc)
+
+    def emit(i, update):
+        mid = mid_ref[i].astype(jnp.float32).T
+        gate = gate_ref[i].astype(jnp.float32).T
+        m1, m2 = mid[:span], mid[span:]
+        g1, g2 = gate[:span], gate[span:]
+        out_ref[i] = (jnp.where(first, m1, m2) + jnp.where(first, g1, g2) * update).astype(jnp.bfloat16)
+        m_ref[i] = jnp.where(first, m2, m1).astype(jnp.bfloat16)
+        g_ref[i] = jnp.where(first, g2, g1).astype(jnp.bfloat16)
+
+    group_updates(C, TI, sc, nts, wx_ref, emit)
+
+
+def finish_late_kernel(pos_ref, a_ref, b_ref, c_ref, d_ref, early_ref, m_ref, g_ref, wx_ref, out_ref, sc, nts):
+    TI, span, C = early_ref.shape
+    first = lower_half_first(pos_ref)
+    add_group(C, TI, (a_ref, b_ref), (c_ref, d_ref), pos_ref[2], sc)
+
+    def emit(i, update):
+        late = m_ref[i].astype(jnp.float32) + g_ref[i].astype(jnp.float32) * update
+        early = early_ref[i].astype(jnp.float32)
+        out_ref[i, :span] = jnp.where(first, early, late).astype(jnp.bfloat16)
+        out_ref[i, span:] = jnp.where(first, late, early).astype(jnp.bfloat16)
+
+    group_updates(C, TI, sc, nts, wx_ref, emit)
+
+
+def finish_group(kernel, shapes, C, TI, *args):
     return pl.pallas_call(
-        functools.partial(final_pairs_kernel, (C, J)),
-        out_shape=jax.ShapeDtypeStruct((TI, J, C), jnp.bfloat16),
-        in_specs=[smem()] + [vmem()] * (len(pieces) + 3),
-        out_specs=vmem(),
-        scratch_shapes=[pltpu.VMEM((C * TI, LANES), jnp.float32), pltpu.VMEM((TI // 2, C, 2 * LANES), jnp.bfloat16)],
+        kernel,
+        out_shape=[jax.ShapeDtypeStruct(x, jnp.bfloat16) for x in shapes],
+        in_specs=[smem()] + [vmem()] * (len(args) - 1),
+        out_specs=[vmem()] * len(shapes),
+        scratch_shapes=[pltpu.VMEM((C // 2 * TI, LANES), jnp.float32), pltpu.VMEM((TI // 4, C, 2 * LANES), jnp.bfloat16)],
         compiler_params=pltpu.CompilerParams(vmem_limit_bytes=VMEM_LIMIT),
-    )(pos, *pieces, mid, gate, wx)
+        cost_estimate=pl.CostEstimate(flops=2 * C * C * TI * 2 * TI, bytes_accessed=TI * TI * C * 20, transcendentals=0),
+    )(*args)
 
 
 def shift(x, axis, d):
@@ -594,7 +624,7 @@
     multiplicative_exit_matrix,
 ):
     seqs, residues, features = homolog_activations.shape
-    tile_rows, tile_cols, _ = edge_activations.shape
+    tile_rows, tile_cols, width = edge_activations.shape
     fw = first_projection_matrix.shape[1]
     nr, nc, ns = (lax.axis_size(a) for a in ("row", "col", "sub"))
     assert ns == 2
@@ -631,19 +661,28 @@
         left_other = shift(lax.dynamic_slice_in_dim(lefts, (1 - sub) * span, span, 2), "sub", 1)
         right_t = prep(rights, rights_other, fw)
         mid, gate, lk, ls, rk, rs = pair(sub_id, left_own, left_other, 0, right_t, outer_weight, edge_activations, entry, tile_rows)
-        up, down = [step_along(rk, "row", 1, 1)], [step_along(rk, "row", -1, 1)]
+        outer = [(i, i ^ 1) for i in range(nr)]
+        inner = [(1, 2), (2, 1)]
+        outward = [(1, 0), (2, 3)]
+
+        def along(x, pairs):
+            return lax.ppermute(x, "row", pairs)
+
+        near, mids = [along(rk, outer)], [along(rk, inner)]
         rr = shift(rs, "sub", 1)
-        up, down = up + [step_along(rr, "row", 1, 1)], down + [step_along(rr, "row", -1, 1)]
+        near, mids = near + [along(rr, outer)], mids + [along(rr, inner)]
         lr = shift(ls, "sub", 1)
         far_k, far_s = pair(sub_id, left_own, left_other, 1, right_t, outer_weight, far_edges, entry, tile_rows, False)
-        up2 = [step_along(x, "row", 1, 2) for x in up]
-        down2 = [step_along(x, "row", -1, 2) for x in down]
+        last_in, last_out = [along(near[0], inner)], [along(mids[0], outward)]
+        last_in, last_out = last_in + [along(near[1], inner)], last_out + [along(mids[1], outward)]
         far = [far_k, shift(far_s, "sub", 1)]
-        send1, send1o, keep1, keep1o, rest, resto = split_call(early_kernel, 3, (3, 2), 6, pos, lk, lr, [], [rk, rr, *up, *down, *far], tile_cols, nr)
+        send1, send1o, keep1, keep1o, rest, resto = split_call(early_kernel, 3, (3, 2), 6, pos, lk, lr, [], [rk, rr, *near, *mids, *far], tile_cols, nr)
         got1, got1o, keep1o = shift(send1, "col", 1), across(send1o, 1), shift(keep1o, "sub", 1)
-        send2, send2o, keep2, keep2o = split_call(late_kernel, 1, (2,), 4, pos, lk, lr, [rest, resto], [*up2, *down2], tile_cols, nr)
+        group = (tile_rows, 2 * tile_rows, width)
+        done1, mid2, gate2 = finish_group(finish_early_kernel, [group] * 3, width, tile_rows, pos, keep1, got1, keep1o, got1o, mid, gate, exit_matrix)
+        send2, send2o, keep2, keep2o = split_call(late_kernel, 1, (2,), 4, pos, lk, lr, [rest, resto], [*last_in, *last_out], tile_cols, nr)
         got2, got2o, keep2o = shift(send2, "col", 1), across(send2o, 1), shift(keep2o, "sub", 1)
-        return final_pairs(pos, [keep1, got1, keep2, got2, keep1o, got1o, keep2o, got2o], mid, gate, exit_matrix)
+        return finish_group(finish_late_kernel, [edge_activations.shape], width, tile_rows, pos, keep2, got2, keep2o, got2o, done1, mid2, gate2, exit_matrix)[0]
 
     outer_weight, entry, exit_matrix = weights(tensor_product_matrix, multiplicative_entry_matrix, multiplicative_exit_matrix, fw)
     rows = jnp.stack([right] + [shift(right, "row", d) for d in range(1, nr)])

time: 108 us -> 101 us (0.935)
  starting transfers between devices: 43 us -> 37.9 us
  waiting for transfers between devices: 19.8 us -> 16.2 us
  Pallas kernels: 35.1 us -> 36.7 us
    ppermute x8, starting transfers between devices: 25.1 us -> 19 us  [along(): return lax.ppermute(x, 'row', pairs)]
    ppermute x11, waiting for transfers between devices: 9.38 us -> 4.91 us  [shift(): return lax.ppermute(x, axis, [(i, (i + d) % n) for i in range(n)])]
    pallas_call x1 -> x2, Pallas kernels: 5.06 us -> 6.8 us  [finish_group(): pl.pallas_call(kernel, out_shape=[jax.ShapeDtypeStruct(x, jnp.bfloat16) f...]
    ppermute x2, starting transfers between devices: 1.61 us -> 2.87 us  [across(): lax.ppermute(x, ('col', 'sub'), [(c * 2 + s, (c + d) % nc * 2 + 1 - s) fo...]
  transfers between devices with their start and end apart: 25 -> 25, of which waited for: 6 -> 8; matrix products, arithmetic and copies ran while one was open for 2% -> 2% of each run, Pallas kernels for 28% -> 34%
where the time goes in v1:
time: 101 us; the launch traced here: 100 us
  starting transfers between devices  37.9 us (38%)
  Pallas kernels  36.7 us (36%)
  waiting for transfers between devices  16.2 us (16%)
  local copies, waits for them, and re-layouts  5.31 us (5%)
  other arithmetic  3.22 us (3%)
    ppermute x8, starting transfers between devices, along(): return lax.ppermute(x, 'row', pairs)  19 us
    pallas_call x2, Pallas kernels, pair(): return f(sub, l, lr, rt, wt, e, went)  14.8 us
    pallas_call x2, Pallas kernels, split_call(): pl.pallas_call(functools.partial(kernel, J, n), out_shape=[jax.ShapeDtype...  9.8 us
    ppermute x8, waiting for transfers between devices, along(): return lax.ppermute(x, 'row', pairs)  9.2 us
    pallas_call x2, Pallas kernels, finish_group(): pl.pallas_call(kernel, out_shape=[jax.ShapeDtypeStruct(x, jnp.bfloat16) f...  6.8 us
    ppermute x3, starting transfers between devices, per_device(): lax.ppermute(x, 'row', [(i, i ^ d) for i in range(nr)])  5.99 us
    ppermute x1, starting transfers between devices, per_device(): lax.ppermute(edge_activations, 'row', [(0, nr - 1), (nr - 1, 0)])  5.5 us
    ppermute x11, waiting for transfers between devices, shift(): return lax.ppermute(x, axis, [(i, (i + d) % n) for i in range(n)])  4.91 us
  transfers between devices with their start and end apart: 25, of which 8 were waited for; matrix products, arithmetic and copies ran while one was open for 2% of the time, Pallas kernels for 34%

profile of v1, /device:TPU:0, one launch (start us, length us, event | category | flops | bytes accessed | tf_op | source)
XLA Modules:
  0.0 100.3 jit_solution(1603756386762476240)
XLA Ops:
  0.0 1.2 %convert_reduce_fusion = f32[16,48]{1,0:T(8,128)S(1)} fusion(bf16[16,48,256]{2,1,0:T(8,128)(2,1)} %param.7), kind=kLoop, calls=%fused_computation.3 | loop fusion | flops 392448 | bytes 396288 | tf_op jit(solution)/shard_map/reduce_sum | solution.py:17
  2.5 3.1 %collective-permute-start.2 = (bf16[16,1536]{1,0:T(8,128)(2,1)S(1)}, bf16[16,1536]{1,0:T(8,128)(2,1)S(1)}, u32[]{:S(2)}, u32[]{:S(2)}) collective-permute-start(bf16[16,1536]{1,0:T(8,128)(2,1)S(1)} %reshape.23), channel_id=1, source_target_pairs={{0,4},{4,0},{8,12},{12,8},{1,5},{5,1},{9,13},{13,9},{2,6},{6,2},{1... | collective-permute-start | bytes 147464 | tf_op jit(solution)/shard_map/ppermute | solution.py:647
  5.7 2.6 %collective-permute-start.3 = (bf16[16,1536]{1,0:T(8,128)(2,1)S(1)}, bf16[16,1536]{1,0:T(8,128)(2,1)S(1)}, u32[]{:S(2)}, u32[]{:S(2)}) collective-permute-start(bf16[16,1536]{1,0:T(8,128)(2,1)S(1)} %reshape.23), channel_id=1, source_target_pairs={{0,8},{4,12},{8,0},{12,4},{1,9},{5,13},{9,1},{13,5},{2,10},{6,14},... | collective-permute-start | bytes 147464 | tf_op jit(solution)/shard_map/ppermute | solution.py:647
  8.9 1.6 %collective-permute-start = (bf16[16,1536]{1,0:T(8,128)(2,1)S(1)}, bf16[16,1536]{1,0:T(8,128)(2,1)S(1)}, u32[]{:S(2)}, u32[]{:S(2)}) collective-permute-start(bf16[16,1536]{1,0:T(8,128)(2,1)S(1)} %reshape.22), channel_id=1, source_target_pairs={{0,2},{2,0},{1,3},{3,1},{4,6},{6,4},{5,7},{7,5},{8,10},{10,8},{9,1... | collective-permute-start | bytes 147464 | tf_op jit(solution)/shard_map/ppermute | solution.py:604
  11.1 5.5 %collective-permute-start.13 = (bf16[24,96,128]{2,1,0:T(8,128)(2,1)S(1)}, bf16[24,96,128]{2,1,0:T(8,128)(2,1)}, u32[]{:S(2)}, u32[]{:S(2)}) collective-permute-start(bf16[24,96,128]{2,1,0:T(8,128)(2,1)S(1)} %copy-done.22), channel_id=1, source_target_pairs={{0,12},{12,0},{1,13},{13,1},{2,14},{14,2},{3,15},{15,3},{16,28},{2... | collective-permute-start | bytes 1769480 | tf_op jit(solution)/shard_map/ppermute | solution.py:658
  16.7 1.7 %collective-permute-done.1 = bf16[2,16,1536]{2,1,0:T(8,128)(2,1)S(1)} collective-permute-done((bf16[2,16,1536]{2,1,0:T(8,128)(2,1)S(1)}, bf16[2,16,1536]{2,1,0:T(8,128)(2,1)S(1)}, u32[]{:S(2)}, u32[]{:S(2)}) %collective-permute-start.1) | collective-permute-done | bytes 98336 | tf_op jit(solution)/shard_map/ppermute | solution.py:647
  19.1 4.6 %collective-permute-done.4 = bf16[3,16,1536]{2,1,0:T(8,128)(2,1)S(1)} collective-permute-done((bf16[3,16,1536]{2,1,0:T(8,128)(2,1)S(1)}, bf16[3,16,1536]{2,1,0:T(8,128)(2,1)S(1)}, u32[]{:S(2)}, u32[]{:S(2)}) %collective-permute-start.4) | collective-permute-done | bytes 147488 | tf_op jit(solution)/shard_map/ppermute | solution.py:604
  23.9 0.7 fusion.4
  25.1 2.2 %shard_map.74 = (bf16[128,1024]{1,0:T(8,128)(2,1)}, bf16[640,128]{1,0:T(8,128)(2,1)}, bf16[128,128]{1,0:T(8,128)(2,1)}) custom-call(bf16[1024,128]{1,0:T(8,128)(2,1)} %w_ref.1, bf16[128,640]{1,0:T(8,128)(2,1)} %n_ref.1, bf16[128,128]{1,0:T(8,128)(2,1)} %x_ref.1), custom_call_target="tpu_custom_call" | custom-call | tf_op jit(solution)/shard_map/pallas_call | solution.py:64
  27.3 0.7 copy-done.14
  28.0 3.1 %shard_map.73.rt_ref = bf16[32,96,64]{2,1,0:T(8,128)(2,1)} custom-call(bf16[2,2,16,1536]{3,2,1,0:T(8,128)(2,1)} %copy-done.3, bf16[2,2,16,1536]{3,2,1,0:T(8,128)(2,1)} %copy-done.14), custom_call_target="tpu_custom_call" | custom-call | tf_op jit(solution)/shard_map/pallas_call | solution.py:96
  31.1 0.7 copy-done.23
  31.7 8.3 %shard_map.75 = (bf16[24,128,96]{2,1,0:T(8,128)(2,1)}, bf16[24,128,96]{2,1,0:T(8,128)(2,1)}, bf16[64,24,128]{2,1,0:T(8,128)(2,1)}, bf16[64,24,128]{2,1,0:T(8,128...) custom-call(s32[1]{0:T(128)} %bitcast.2.sub_ref, bf16[2,32,768]{2,1,0:T(8,128)(2,1)} %get-tuple-element.58.l_ref, ...), custom_call_target="tpu_custom_call" | custom-call | flops 1283457024 | bytes 7077888 | tf_op jit(solution)/shard_map/pallas_call | solution.py:214
  40.1 0.7 collective-permute-start.11
  41.3 13.5 %collective-permute-start.9 = (bf16[48,24,128]{2,1,0:T(8,128)(2,1)}, bf16[48,24,128]{2,1,0:T(8,128)(2,1)S(1)}, u32[]{:S(2)}, u32[]{:S(2)}) collective-permute-start(bf16[48,24,128]{2,1,0:T(8,128)(2,1)} %get-tuple-element.33.rest_0_), channel_id=1, source_target_pairs={{0,4},{4,0},{8,12},{12,8},{1,5},{5,1},{9,13},{13,9},{2,6},{6,2},{1... | collective-permute-start | bytes 884744 | tf_op jit(solution)/shard_map/ppermute | solution.py:669
  54.9 0.8 collective-permute-start.12
  55.7 6.5 %shard_map.76 = (bf16[48,24,128]{2,1,0:T(8,128)(2,1)}, bf16[48,24,128]{2,1,0:T(8,128)(2,1)}) custom-call(s32[1]{0:T(128)} %bitcast.2.sub_ref, bf16[2,32,768]{2,1,0:T(8,128)(2,1)} %get-tuple-element.58.l_ref, bf16[2,32,768]{2,1,0:T(8,128)(2,1)} %copy-done.23, bf16[32,96,64]{2,1,0:T(8,128)(2,1)} %shard_map.73.rt_ref, ...), custom_call_target="tpu_custom_call" | custom-call | flops 1283457024 | bytes 7077888 | tf_op jit(solution)/shard_map/pallas_call | solution.py:214
  62.8 0.7 collective-permute-start.15
  63.5 1.3 %collective-permute-start.17 = (bf16[48,24,128]{2,1,0:T(8,128)(2,1)S(1)}, bf16[48,24,128]{2,1,0:T(8,128)(2,1)S(1)}, u32[]{:S(2)}, u32[]{:S(2)}) collective-permute-start(bf16[48,24,128]{2,1,0:T(8,128)(2,1)S(1)} %collective-permute-done.11.rest_4_), channel_id=1, source_target_pairs={{4,0},{8,12},{5,1},{9,13},{6,2},{10,14},{7,3},{11,15},{20,16},{24,... | collective-permute-start | bytes 884744 | tf_op jit(solution)/shard_map/ppermute | solution.py:669
  64.8 3.7 %collective-permute-done.10.rest_3_ = bf16[48,24,128]{2,1,0:T(8,128)(2,1)S(1)} collective-permute-done((bf16[48,24,128]{2,1,0:T(8,128)(2,1)S(1)}, bf16[48,24,128]{2,1,0:T(8,128)(2,1)S(1)}, u32[]{:S(2)}, u32[]{:S(2)}) %collective-permute-start.10) | collective-permute-done | bytes 294944 | tf_op jit(solution)/shard_map/ppermute | solution.py:669
  68.6 0.7 collective-permute-start.16
  69.3 1.3 %collective-permute-start.18 = (bf16[48,24,128]{2,1,0:T(8,128)(2,1)S(1)}, bf16[48,24,128]{2,1,0:T(8,128)(2,1)S(1)}, u32[]{:S(2)}, u32[]{:S(2)}) collective-permute-start(bf16[48,24,128]{2,1,0:T(8,128)(2,1)S(1)} %collective-permute-done.12.rest_5_), channel_id=1, source_target_pairs={{4,0},{8,12},{5,1},{9,13},{6,2},{10,14},{7,3},{11,15},{20,16},{24,... | collective-permute-start | bytes 884744 | tf_op jit(solution)/shard_map/ppermute | solution.py:669
  71.2 0.7 copy-done.13
  71.9 5.8 %shard_map.77 = (bf16[24,24,128]{2,1,0:T(8,128)(2,1)}, bf16[24,24,128]{2,1,0:T(8,128)(2,1)}, bf16[24,24,128]{2,1,0:T(8,128)(2,1)}, bf16[24,24,128]{2,1,0:T(8,128...) custom-call(s32[3]{0:T(128)} %pad_add_fusion.pos_ref, bf16[64,24,128]{2,1,0:T(8,128)(2,1)} %get-tuple-element.31.lk_ref, ...), custom_call_target="tpu_custom_call" | custom-call | flops 452984832 | bytes 3538944 | tf_op jit(solution)/shard_map/pallas_call | solution.py:487
  78.6 1.2 %collective-permute-start.24 = (bf16[24,24,128]{2,1,0:T(8,128)(2,1)}, bf16[24,24,128]{2,1,0:T(8,128)(2,1)S(1)}, u32[]{:S(2)}, u32[]{:S(2)}) collective-permute-start(bf16[24,24,128]{2,1,0:T(8,128)(2,1)} %get-tuple-element.46), channel_id=1, source_target_pairs={{0,3},{1,2},{2,1},{3,0},{4,7},{5,6},{6,5},{7,4},{8,11},{9,10},{10,... | collective-permute-start | bytes 442376 | tf_op jit(solution)/shard_map/ppermute | solution.py:614
  79.9 4.6 %collective-permute-done.18.rest_3_ = bf16[48,24,128]{2,1,0:T(8,128)(2,1)S(1)} collective-permute-done((bf16[48,24,128]{2,1,0:T(8,128)(2,1)S(1)}, bf16[48,24,128]{2,1,0:T(8,128)(2,1)S(1)}, u32[]{:S(2)}, u32[]{:S(2)}) %collective-permute-start.18) | collective-permute-done | bytes 294944 | tf_op jit(solution)/shard_map/ppermute | solution.py:669
  84.4 0.7 copy-done.7
  85.1 4.0 %shard_map.78 = (bf16[24,24,128]{2,1,0:T(8,128)(2,1)}, bf16[24,24,128]{2,1,0:T(8,128)(2,1)}, bf16[24,24,128]{2,1,0:T(8,128)(2,1)}, bf16[24,24,128]{2,1,0:T(8,128)(2,1)}) custom-call(s32[3]{0:T(128)} %pad_add_fusion.pos_ref, bf16[64,24,128]{2,1,0:T(8,128)(2,1)} %get-tuple-element.31.lk_ref, bf16[64,24,128]{2,1,0:T(8,128)(2,1)} %copy-done.2, ...), custom_call_target="tpu_custom_call" | custom-call | flops 150994944 | bytes 1179648 | tf_op jit(solution)/shard_map/pallas_call | solution.py:487
  89.8 1.6 %collective-permute-start.21 = (bf16[24,24,128]{2,1,0:T(8,128)(2,1)}, bf16[24,24,128]{2,1,0:T(8,128)(2,1)S(1)}, u32[]{:S(2)}, u32[]{:S(2)}) collective-permute-start(bf16[24,24,128]{2,1,0:T(8,128)(2,1)} %get-tuple-element.42), channel_id=1, source_target_pairs={{0,3},{1,2},{2,1},{3,0},{4,7},{5,6},{6,5},{7,4},{8,11},{9,10},{10,... | collective-permute-start | bytes 442376 | tf_op jit(solution)/shard_map/ppermute | solution.py:614
  91.4 0.6 copy-done.16
  92.1 3.8 %shard_map.79 = (bf16[24,48,128]{2,1,0:T(8,128)(2,1)}, bf16[24,48,128]{2,1,0:T(8,128)(2,1)}, bf16[24,48,128]{2,1,0:T(8,128)(2,1)}) custom-call(s32[3]{0:T(128)} %pad_add_fusion.pos_ref, bf16[24,24,128]{2,1,0:T(8,128)(2,1)} %get-tuple-element.43.a_ref, bf16[24,24,128]{2,1,0:T(8,128)(2,1)} %copy-done.15, bf16[24,24,128]{2,1,0:T(8,128)(2,1)} %copy-done.16, ...), custom_call_target="tpu_custom_call" | custom-call | flops 37748736 | bytes 1474560 | tf_op jit(solution)/shard_map/pallas_call | solution.py:591
  97.2 3.0 %shard_map.80 = bf16[24,96,128]{2,1,0:T(8,128)(2,1)} custom-call(s32[3]{0:T(128)} %pad_add_fusion.pos_ref, bf16[24,24,128]{2,1,0:T(8,128)(2,1)} %get-tuple-element.39.a_ref, bf16[24,24,128]{2,1,0:T(8,128)(2,1)} %copy-done.18, bf16[24,24,128]{2,1,0:T(8,128)(2,1)} %copy-done.19, bf16[24,24,128]{2,1,0:T(8,128)(2,1)} %copy-done.20, ...), custom_call_target="tpu_custom_call" | custom-call | flops 37748736 | bytes 1474560 | tf_op jit(solution)/shard_map/pallas_call | solution.py:591
  (100 shorter events, 8.8 us)
Async XLA Ops:
  2.3 5.9 %copy-start.21 = (bf16[256,32]{0,1:T(8,128)(2,1)S(1)}, bf16[256,32]{0,1:T(8,128)(2,1)}, u32[]{:S(2)}) copy-start(bf16[256,32]{0,1:T(8,128)(2,1)} %param.9) | copy-start | bytes 49156
  2.5 15.9 %collective-permute-start.2 = (bf16[16,1536]{1,0:T(8,128)(2,1)S(1)}, bf16[16,1536]{1,0:T(8,128)(2,1)S(1)}, u32[]{:S(2)}, u32[]{:S(2)}) collective-permute-start(bf16[16,1536]{1,0:T(8,128)(2,1)S(1)} %reshape.23), channel_id=1, source_target_pairs={{0,4},{4,0},{8,12},{12,8},{1,5},{5,1},{9,13},{13,9},{2,6},{6,2},{1... | collective-permute-start | bytes 147464 | tf_op jit(solution)/shard_map/ppermute | solution.py:647
  5.7 12.8 %collective-permute-start.3 = (bf16[16,1536]{1,0:T(8,128)(2,1)S(1)}, bf16[16,1536]{1,0:T(8,128)(2,1)S(1)}, u32[]{:S(2)}, u32[]{:S(2)}) collective-permute-start(bf16[16,1536]{1,0:T(8,128)(2,1)S(1)} %reshape.23), channel_id=1, source_target_pairs={{0,8},{4,12},{8,0},{12,4},{1,9},{5,13},{9,1},{13,5},{2,10},{6,14},... | collective-permute-start | bytes 147464 | tf_op jit(solution)/shard_map/ppermute | solution.py:647
  8.9 7.8 %collective-permute-start = (bf16[16,1536]{1,0:T(8,128)(2,1)S(1)}, bf16[16,1536]{1,0:T(8,128)(2,1)S(1)}, u32[]{:S(2)}, u32[]{:S(2)}) collective-permute-start(bf16[16,1536]{1,0:T(8,128)(2,1)S(1)} %reshape.22), channel_id=1, source_target_pairs={{0,2},{2,0},{1,3},{3,1},{4,6},{6,4},{5,7},{7,5},{8,10},{10,8},{9,1... | collective-permute-start | bytes 147464 | tf_op jit(solution)/shard_map/ppermute | solution.py:604
  10.8 7.6 %collective-permute-start.1 = (bf16[2,16,1536]{2,1,0:T(8,128)(2,1)S(1)}, bf16[2,16,1536]{2,1,0:T(8,128)(2,1)S(1)}, u32[]{:S(2)}, u32[]{:S(2)}) collective-permute-start(bf16[2,16,1536]{2,1,0:T(8,128)(2,1)S(1)} %pad_maximum_fusion.3), channel_id=1, source_target_pairs={{0,12},{4,8},{8,4},{12,0},{1,13},{5,9},{9,5},{13,1},{2,14},{6,10},... | collective-permute-start | bytes 294920 | tf_op jit(solution)/shard_map/ppermute | solution.py:647
  11.1 43.7 %collective-permute-start.13 = (bf16[24,96,128]{2,1,0:T(8,128)(2,1)S(1)}, bf16[24,96,128]{2,1,0:T(8,128)(2,1)}, u32[]{:S(2)}, u32[]{:S(2)}) collective-permute-start(bf16[24,96,128]{2,1,0:T(8,128)(2,1)S(1)} %copy-done.22), channel_id=1, source_target_pairs={{0,12},{12,0},{1,13},{13,1},{2,14},{14,2},{3,15},{15,3},{16,28},{2... | collective-permute-start | bytes 1769480 | tf_op jit(solution)/shard_map/ppermute | solution.py:658
  18.5 5.2 %collective-permute-start.4 = (bf16[3,16,1536]{2,1,0:T(8,128)(2,1)S(1)}, bf16[3,16,1536]{2,1,0:T(8,128)(2,1)S(1)}, u32[]{:S(2)}, u32[]{:S(2)}) collective-permute-start(bf16[3,16,1536]{2,1,0:T(8,128)(2,1)S(1)} %pad_maximum_fusion.2), channel_id=1, source_target_pairs={{0,2},{2,0},{1,3},{3,1},{4,6},{6,4},{5,7},{7,5},{8,10},{10,8},{9,1... | collective-permute-start | bytes 442376 | tf_op jit(solution)/shard_map/ppermute | solution.py:604
  23.8 3.5 %collective-permute-start.6 = (bf16[2,2,16,1536]{3,2,1,0:T(8,128)(2,1)S(1)}, bf16[2,2,16,1536]{3,2,1,0:T(8,128)(2,1)S(1)}, u32[]{:S(2)}, u32[]{:S(2)}) collective-permute-start(bf16[2,2,16,1536]{3,2,1,0:T(8,128)(2,1)S(1)} %pad_maximum_fusion.1.own_ref), channel_id=1, source_target_pairs={{0,1},{1,0},{2,3},{3,2},{4,5},{5,4},{6,7},{7,6},{8,9},{9,8},{10,11... | collective-permute-start | bytes 589832 | tf_op jit(solution)/shard_map/ppermute | solution.py:604
  24.6 6.5 %collective-permute-start.5 = (bf16[2,32,768]{2,1,0:T(8,128)(2,1)S(1)}, bf16[2,32,768]{2,1,0:T(8,128)(2,1)S(1)}, u32[]{:S(2)}, u32[]{:S(2)}) collective-permute-start(bf16[2,32,768]{2,1,0:T(8,128)(2,1)S(1)} %get-tuple-element.57), channel_id=1, source_target_pairs={{0,1},{1,0},{2,3},{3,2},{4,5},{5,4},{6,7},{7,6},{8,9},{9,8},{10,11... | collective-permute-start | bytes 294920 | tf_op jit(solution)/shard_map/ppermute | solution.py:604
  40.0 14.8 %collective-permute-start.8 = (bf16[48,24,128]{2,1,0:T(8,128)(2,1)}, bf16[48,24,128]{2,1,0:T(8,128)(2,1)S(1)}, u32[]{:S(2)}, u32[]{:S(2)}) collective-permute-start(bf16[48,24,128]{2,1,0:T(8,128)(2,1)} %get-tuple-element.34), channel_id=1, source_target_pairs={{0,1},{1,0},{2,3},{3,2},{4,5},{5,4},{6,7},{7,6},{8,9},{9,8},{10,11... | collective-permute-start | bytes 884744 | tf_op jit(solution)/shard_map/ppermute | solution.py:604
  40.1 22.2 %collective-permute-start.11 = (bf16[48,24,128]{2,1,0:T(8,128)(2,1)}, bf16[48,24,128]{2,1,0:T(8,128)(2,1)S(1)}, u32[]{:S(2)}, u32[]{:S(2)}) collective-permute-start(bf16[48,24,128]{2,1,0:T(8,128)(2,1)} %get-tuple-element.33.rest_0_), channel_id=1, source_target_pairs={{4,8},{8,4},{5,9},{9,5},{6,10},{10,6},{7,11},{11,7},{20,24},{24,20... | collective-permute-start | bytes 884744 | tf_op jit(solution)/shard_map/ppermute | solution.py:669
  40.7 22.8 %collective-permute-start.7 = (bf16[64,24,128]{2,1,0:T(8,128)(2,1)}, bf16[64,24,128]{2,1,0:T(8,128)(2,1)S(1)}, u32[]{:S(2)}, u32[]{:S(2)}) collective-permute-start(bf16[64,24,128]{2,1,0:T(8,128)(2,1)} %get-tuple-element.32), channel_id=1, source_target_pairs={{0,1},{1,0},{2,3},{3,2},{4,5},{5,4},{6,7},{7,6},{8,9},{9,8},{10,11... | collective-permute-start | bytes 1179656 | tf_op jit(solution)/shard_map/ppermute | solution.py:604
  41.3 21.6 %collective-permute-start.9 = (bf16[48,24,128]{2,1,0:T(8,128)(2,1)}, bf16[48,24,128]{2,1,0:T(8,128)(2,1)S(1)}, u32[]{:S(2)}, u32[]{:S(2)}) collective-permute-start(bf16[48,24,128]{2,1,0:T(8,128)(2,1)} %get-tuple-element.33.rest_0_), channel_id=1, source_target_pairs={{0,4},{4,0},{8,12},{12,8},{1,5},{5,1},{9,13},{13,9},{2,6},{6,2},{1... | collective-permute-start | bytes 884744 | tf_op jit(solution)/shard_map/ppermute | solution.py:669
  54.8 7.4 %copy-start.10 = (bf16[48,24,128]{2,1,0:T(8,128)(2,1)}, bf16[48,24,128]{2,1,0:T(8,128)(2,1)S(1)}, u32[]{:S(2)}) copy-start(bf16[48,24,128]{2,1,0:T(8,128)(2,1)S(1)} %collective-permute-done.8.rest_1_) | copy-start | bytes 884740
  54.8 13.8 %collective-permute-start.10 = (bf16[48,24,128]{2,1,0:T(8,128)(2,1)S(1)}, bf16[48,24,128]{2,1,0:T(8,128)(2,1)S(1)}, u32[]{:S(2)}, u32[]{:S(2)}) collective-permute-start(bf16[48,24,128]{2,1,0:T(8,128)(2,1)S(1)} %collective-permute-done.8.rest_1_), channel_id=1, source_target_pairs={{0,4},{4,0},{8,12},{12,8},{1,5},{5,1},{9,13},{13,9},{2,6},{6,2},{1... | collective-permute-start | bytes 884744 | tf_op jit(solution)/shard_map/ppermute | solution.py:669
  54.9 14.4 %collective-permute-start.12 = (bf16[48,24,128]{2,1,0:T(8,128)(2,1)S(1)}, bf16[48,24,128]{2,1,0:T(8,128)(2,1)S(1)}, u32[]{:S(2)}, u32[]{:S(2)}) collective-permute-start(bf16[48,24,128]{2,1,0:T(8,128)(2,1)S(1)} %collective-permute-done.8.rest_1_), channel_id=1, source_target_pairs={{4,8},{8,4},{5,9},{9,5},{6,10},{10,6},{7,11},{11,7},{20,24},{24,20... | collective-permute-start | bytes 884744 | tf_op jit(solution)/shard_map/ppermute | solution.py:669
  62.2 8.9 %copy-start.8 = (bf16[48,24,128]{2,1,0:T(8,128)(2,1)}, bf16[48,24,128]{2,1,0:T(8,128)(2,1)S(1)}, u32[]{:S(2)}) copy-start(bf16[48,24,128]{2,1,0:T(8,128)(2,1)S(1)} %collective-permute-done.11.rest_4_) | copy-start | bytes 884740
  62.2 8.9 %collective-permute-start.14 = (bf16[48,24,128]{2,1,0:T(8,128)(2,1)}, bf16[48,24,128]{2,1,0:T(8,128)(2,1)S(1)}, u32[]{:S(2)}, u32[]{:S(2)}) collective-permute-start(bf16[48,24,128]{2,1,0:T(8,128)(2,1)} %get-tuple-element.36), channel_id=1, source_target_pairs={{0,1},{1,0},{2,3},{3,2},{4,5},{5,4},{6,7},{7,6},{8,9},{9,8},{10,11... | collective-permute-start | bytes 884744 | tf_op jit(solution)/shard_map/ppermute | solution.py:604
  62.8 8.3 %copy-start.12 = (bf16[48,24,128]{2,1,0:T(8,128)(2,1)}, bf16[48,24,128]{2,1,0:T(8,128)(2,1)S(1)}, u32[]{:S(2)}) copy-start(bf16[48,24,128]{2,1,0:T(8,128)(2,1)S(1)} %collective-permute-done.9.rest_2_) | copy-start | bytes 884740
  62.8 15.4 %collective-permute-start.15 = (bf16[48,24,128]{2,1,0:T(8,128)(2,1)S(1)}, bf16[48,24,128]{2,1,0:T(8,128)(2,1)S(1)}, u32[]{:S(2)}, u32[]{:S(2)}) collective-permute-start(bf16[48,24,128]{2,1,0:T(8,128)(2,1)S(1)} %collective-permute-done.9.rest_2_), channel_id=1, source_target_pairs={{4,8},{8,4},{5,9},{9,5},{6,10},{10,6},{7,11},{11,7},{20,24},{24,20... | collective-permute-start | bytes 884744 | tf_op jit(solution)/shard_map/ppermute | solution.py:669
  63.5 7.6 %copy-start.2 = (bf16[64,24,128]{2,1,0:T(8,128)(2,1)}, bf16[64,24,128]{2,1,0:T(8,128)(2,1)S(1)}, u32[]{:S(2)}) copy-start(bf16[64,24,128]{2,1,0:T(8,128)(2,1)S(1)} %collective-permute-done.7.lr_ref) | copy-start | bytes 1179652
  63.5 15.1 %collective-permute-start.17 = (bf16[48,24,128]{2,1,0:T(8,128)(2,1)S(1)}, bf16[48,24,128]{2,1,0:T(8,128)(2,1)S(1)}, u32[]{:S(2)}, u32[]{:S(2)}) collective-permute-start(bf16[48,24,128]{2,1,0:T(8,128)(2,1)S(1)} %collective-permute-done.11.rest_4_), channel_id=1, source_target_pairs={{4,0},{8,12},{5,1},{9,13},{6,2},{10,14},{7,3},{11,15},{20,16},{24,... | collective-permute-start | bytes 884744 | tf_op jit(solution)/shard_map/ppermute | solution.py:669
  68.6 11.3 %collective-permute-start.16 = (bf16[48,24,128]{2,1,0:T(8,128)(2,1)S(1)}, bf16[48,24,128]{2,1,0:T(8,128)(2,1)S(1)}, u32[]{:S(2)}, u32[]{:S(2)}) collective-permute-start(bf16[48,24,128]{2,1,0:T(8,128)(2,1)S(1)} %collective-permute-done.10.rest_3_), channel_id=1, source_target_pairs={{4,8},{8,4},{5,9},{9,5},{6,10},{10,6},{7,11},{11,7},{20,24},{24,20... | collective-permute-start | bytes 884744 | tf_op jit(solution)/shard_map/ppermute | solution.py:669
  69.3 15.2 %collective-permute-start.18 = (bf16[48,24,128]{2,1,0:T(8,128)(2,1)S(1)}, bf16[48,24,128]{2,1,0:T(8,128)(2,1)S(1)}, u32[]{:S(2)}, u32[]{:S(2)}) collective-permute-start(bf16[48,24,128]{2,1,0:T(8,128)(2,1)S(1)} %collective-permute-done.12.rest_5_), channel_id=1, source_target_pairs={{4,0},{8,12},{5,1},{9,13},{6,2},{10,14},{7,3},{11,15},{20,16},{24,... | collective-permute-start | bytes 884744 | tf_op jit(solution)/shard_map/ppermute | solution.py:669
  77.6 12.1 %collective-permute-start.22 = (bf16[24,24,128]{2,1,0:T(8,128)(2,1)}, bf16[24,24,128]{2,1,0:T(8,128)(2,1)S(1)}, u32[]{:S(2)}, u32[]{:S(2)}) collective-permute-start(bf16[24,24,128]{2,1,0:T(8,128)(2,1)} %get-tuple-element.44), channel_id=1, source_target_pairs={{0,2},{2,0},{1,3},{3,1},{4,6},{6,4},{5,7},{7,5},{8,10},{10,8},{9,1... | collective-permute-start | bytes 442376 | tf_op jit(solution)/shard_map/ppermute | solution.py:604
  78.2 6.2 %copy-start.4 = (bf16[48,24,128]{2,1,0:T(8,128)(2,1)}, bf16[48,24,128]{2,1,0:T(8,128)(2,1)S(1)}, u32[]{:S(2)}) copy-start(bf16[48,24,128]{2,1,0:T(8,128)(2,1)S(1)} %collective-permute-done.15.rest_0_) | copy-start | bytes 884740
  78.2 13.2 %collective-permute-start.23 = (bf16[24,24,128]{2,1,0:T(8,128)(2,1)}, bf16[24,24,128]{2,1,0:T(8,128)(2,1)S(1)}, u32[]{:S(2)}, u32[]{:S(2)}) collective-permute-start(bf16[24,24,128]{2,1,0:T(8,128)(2,1)} %get-tuple-element.45), channel_id=1, source_target_pairs={{0,1},{1,0},{2,3},{3,2},{4,5},{5,4},{6,7},{7,6},{8,9},{9,8},{10,11... | collective-permute-start | bytes 442376 | tf_op jit(solution)/shard_map/ppermute | solution.py:604
  78.6 5.8 %copy-start.5 = (bf16[48,24,128]{2,1,0:T(8,128)(2,1)}, bf16[48,24,128]{2,1,0:T(8,128)(2,1)S(1)}, u32[]{:S(2)}) copy-start(bf16[48,24,128]{2,1,0:T(8,128)(2,1)S(1)} %collective-permute-done.17.rest_2_) | copy-start | bytes 884740
  78.6 12.8 %collective-permute-start.24 = (bf16[24,24,128]{2,1,0:T(8,128)(2,1)}, bf16[24,24,128]{2,1,0:T(8,128)(2,1)S(1)}, u32[]{:S(2)}, u32[]{:S(2)}) collective-permute-start(bf16[24,24,128]{2,1,0:T(8,128)(2,1)} %get-tuple-element.46), channel_id=1, source_target_pairs={{0,3},{1,2},{2,1},{3,0},{4,7},{5,6},{6,5},{7,4},{8,11},{9,10},{10,... | collective-permute-start | bytes 442376 | tf_op jit(solution)/shard_map/ppermute | solution.py:614
  89.2 7.0 %collective-permute-start.19 = (bf16[24,24,128]{2,1,0:T(8,128)(2,1)}, bf16[24,24,128]{2,1,0:T(8,128)(2,1)S(1)}, u32[]{:S(2)}, u32[]{:S(2)}) collective-permute-start(bf16[24,24,128]{2,1,0:T(8,128)(2,1)} %get-tuple-element.40), channel_id=1, source_target_pairs={{0,2},{2,0},{1,3},{3,1},{4,6},{6,4},{5,7},{7,5},{8,10},{10,8},{9,1... | collective-permute-start | bytes 442376 | tf_op jit(solution)/shard_map/ppermute | solution.py:604
  89.8 6.4 %collective-permute-start.20 = (bf16[24,24,128]{2,1,0:T(8,128)(2,1)}, bf16[24,24,128]{2,1,0:T(8,128)(2,1)S(1)}, u32[]{:S(2)}, u32[]{:S(2)}) collective-permute-start(bf16[24,24,128]{2,1,0:T(8,128)(2,1)} %get-tuple-element.41), channel_id=1, source_target_pairs={{0,1},{1,0},{2,3},{3,2},{4,5},{5,4},{6,7},{7,6},{8,9},{9,8},{10,11... | collective-permute-start | bytes 442376 | tf_op jit(solution)/shard_map/ppermute | solution.py:604
  89.8 6.8 %collective-permute-start.21 = (bf16[24,24,128]{2,1,0:T(8,128)(2,1)}, bf16[24,24,128]{2,1,0:T(8,128)(2,1)S(1)}, u32[]{:S(2)}, u32[]{:S(2)}) collective-permute-start(bf16[24,24,128]{2,1,0:T(8,128)(2,1)} %get-tuple-element.42), channel_id=1, source_target_pairs={{0,3},{1,2},{2,1},{3,0},{4,7},{5,6},{6,5},{7,4},{8,11},{9,10},{10,... | collective-permute-start | bytes 442376 | tf_op jit(solution)/shard_map/ppermute | solution.py:614
  (17 other events, 23.5 us)

commit v2 on v1

--- a/solution.py
+++ b/solution.py
@@ -11,6 +11,10 @@
 EPSILON = 1e-05
 LANES = 128
 VMEM_LIMIT = 60 * 1024 * 1024
+
+
+def grant(mib):
+    return pltpu.CompilerParams(vmem_limit_bytes=mib * 1024 * 1024)
 
 
 def standardize_features(values):
@@ -67,6 +71,7 @@
         in_specs=[vmem()] * 3,
         out_specs=[vmem()] * 3,
         scratch_shapes=[pltpu.VMEM((K, C), jnp.float32)] * 2,
+        compiler_params=grant(4),
     )(w, n, x)
 
 
@@ -99,11 +104,20 @@
         in_specs=[vmem(), vmem()],
         out_specs=vmem(),
         scratch_shapes=[pltpu.VMEM((total // chunk, m * row_lanes, chunk), jnp.float32)],
+        compiler_params=grant(8),
     )(own, recv)
 
 
-def pair_kernel(cfg, sub_ref, l_ref, lr_ref, rt_ref, wt_ref, e_ref, went_ref, *rest):
-    fw, C, J, S, full = cfg
+def pair_kernel(cfg, pos_ref, *refs):
+    last = cfg[5]
+    if last:
+        pl.when((pos_ref[0] == 0) | (pos_ref[0] == last))(lambda: pair_body(cfg, pos_ref, *refs))
+    else:
+        pair_body(cfg, pos_ref, *refs)
+
+
+def pair_body(cfg, pos_ref, l_ref, lr_ref, rt_ref, wt_ref, e_ref, went_ref, *rest):
+    fw, C, J, S, full, _ = cfg
     if full:
         mid_ref, gate_ref, lk_ref, ls_ref, rk_ref, rs_ref, lt, ot, nts, lsc, rsc = rest
     else:
@@ -148,7 +162,7 @@
             x = jax.nn.sigmoid(project(4, 1, h)).astype(jnp.bfloat16)
             for k in range(2):
                 gate_ref[2 * h + k] = x[:, k * wide : k * wide + J]
-    sub = sub_ref[0]
+    sub = pos_ref[2]
     parts, main = packing(half, J)
     inside = lane_index((IG, LANES)) < J
     if full:
@@ -172,7 +186,8 @@
                     ref[t * tails + q] = jnp.where(inside, x, moved).astype(jnp.bfloat16)
 
 
-def pair(sub, l, lr, which, rt, wt, e, went, IG, full=True):
+def pair(pos, l, lr, which, rt, wt, e, went, IG, last=0):
+    full = not last
     _, part, IA = l.shape
     S = 2 * part
     fw, J, _ = rt.shape
@@ -188,7 +203,7 @@
     outs = ([tile] * 2 + [lefts] * 2 if full else []) + [rights] * 2
     gated = pltpu.VMEM((IG * C, LANES), jnp.float32)
     f = pl.pallas_call(
-        functools.partial(pair_kernel, (fw, C, J, S, full)),
+        functools.partial(pair_kernel, (fw, C, J, S, full, last)),
         grid=(TI // IG,),
         out_shape=[o[0] for o in outs],
         in_specs=[
@@ -208,10 +223,10 @@
             gated,
         ]
         + ([gated] if full else []),
-        compiler_params=pltpu.CompilerParams(vmem_limit_bytes=VMEM_LIMIT),
+        compiler_params=grant(28),
         cost_estimate=pl.CostEstimate(flops=2 * TI * J * (S * fw * fw + fw * fw * C + 5 * C * C), bytes_accessed=4 * TI * J * C * 6, transcendentals=TI * J * C * 3),
     )
-    return f(sub, l, lr, rt, wt, e, went)
+    return f(pos, l, lr, rt, wt, e, went)
 
 
 def tri_kernel(cfg, n_slots, pos_ref, lk_ref, lr_ref, *rest):
@@ -495,7 +510,7 @@
             pltpu.VMEM((shards,) + acc if shards > 1 else acc, bf),
             pltpu.SemaphoreType.DMA(sems),
         ],
-        compiler_params=pltpu.CompilerParams(vmem_limit_bytes=VMEM_LIMIT),
+        compiler_params=grant(12 if shards > 1 else 6),
         cost_estimate=pl.CostEstimate(flops=2 * shards * half * 48 * 48 * 512, bytes_accessed=shards * 2 * main * TI * LANES * 4, transcendentals=0),
     )(pos, lk, lr, *extra, *slots)
 
@@ -594,7 +609,7 @@
         in_specs=[smem()] + [vmem()] * (len(args) - 1),
         out_specs=[vmem()] * len(shapes),
         scratch_shapes=[pltpu.VMEM((C // 2 * TI, LANES), jnp.float32), pltpu.VMEM((TI // 4, C, 2 * LANES), jnp.bfloat16)],
-        compiler_params=pltpu.CompilerParams(vmem_limit_bytes=VMEM_LIMIT),
+        compiler_params=grant(8),
         cost_estimate=pl.CostEstimate(flops=2 * C * C * TI * 2 * TI, bytes_accessed=TI * TI * C * 20, transcendentals=0),
     )(*args)
 
@@ -660,7 +675,7 @@
         left_own = lax.dynamic_slice_in_dim(lefts, sub * span, span, 2)
         left_other = shift(lax.dynamic_slice_in_dim(lefts, (1 - sub) * span, span, 2), "sub", 1)
         right_t = prep(rights, rights_other, fw)
-        mid, gate, lk, ls, rk, rs = pair(sub_id, left_own, left_other, 0, right_t, outer_weight, edge_activations, entry, tile_rows)
+        mid, gate, lk, ls, rk, rs = pair(pos, left_own, left_other, 0, right_t, outer_weight, edge_activations, entry, tile_rows)
         outer = [(i, i ^ 1) for i in range(nr)]
         inner = [(1, 2), (2, 1)]
         outward = [(1, 0), (2, 3)]
@@ -672,7 +687,7 @@
         rr = shift(rs, "sub", 1)
         near, mids = near + [along(rr, outer)], mids + [along(rr, inner)]
         lr = shift(ls, "sub", 1)
-        far_k, far_s = pair(sub_id, left_own, left_other, 1, right_t, outer_weight, far_edges, entry, tile_rows, False)
+        far_k, far_s = pair(pos, left_own, left_other, 1, right_t, outer_weight, far_edges, entry, tile_rows, nr - 1)
         last_in, last_out = [along(near[0], inner)], [along(mids[0], outward)]
         last_in, last_out = last_in + [along(near[1], inner)], last_out + [along(mids[1], outward)]
         far = [far_k, shift(far_s, "sub", 1)]
@@ -700,7 +715,7 @@
     left_own = lax.dynamic_slice_in_dim(lefts, sub * span, span, 2)
     left_other = shift(lax.dynamic_slice_in_dim(lefts, (1 - sub) * span, span, 2), "sub", 1)
     right_t = prep(rights, rights_other, fw)
-    mid, gate, lk, ls, rk, rs = pair(sub_id, left_own, left_other, 0, right_t, outer_weight, edge_activations, entry, tile_rows)
+    mid, gate, lk, ls, rk, rs = pair(pos, left_own, left_other, 0, right_t, outer_weight, edge_activations, entry, tile_rows)
 
     rr = shift(rs, "sub", 1)
     lr = shift(ls, "sub", 1)

time: 101 us -> 86.8 us (0.86)
  Pallas kernels: 36.7 us -> 22.3 us
  waiting for transfers between devices: 16.2 us -> 21.2 us
  local copies, waits for them, and re-layouts: 5.31 us -> 1.92 us
  other arithmetic: 3.22 us -> 2.06 us
    pallas_call x2, Pallas kernels: 9.8 us -> 5.37 us  [split_call(): pl.pallas_call(functools.partial(kernel, J, n), out_shape=[jax.ShapeDtype...]
    pallas_call x2, Pallas kernels: 14.8 us -> 11.4 us  [pair(): return f(pos, l, lr, rt, wt, e, went)]
    unnamed x48 -> x14, local copies, waits for them, and re-layouts: 4.12 us -> 0.73 us
    ppermute x8, waiting for transfers between devices: 9.2 us -> 12.5 us  [along(): return lax.ppermute(x, 'row', pairs)]
    ppermute x11, waiting for transfers between devices: 4.91 us -> 8.13 us  [shift(): return lax.ppermute(x, axis, [(i, (i + d) % n) for i in range(n)])]
    pallas_call x2, Pallas kernels: 6.8 us -> 3.94 us  [finish_group(): pl.pallas_call(kernel, out_shape=[jax.ShapeDtypeStruct(x, jnp.bfloat16) f...]
    pallas_call x1, Pallas kernels: 3.11 us -> 1.2 us  [prep(): pl.pallas_call(functools.partial(prep_kernel, fw), out_shape=jax.ShapeDty...]
    pallas_call x1, Pallas kernels: 2.23 us -> 0.46 us  [weights(): pl.pallas_call(functools.partial(weights_kernel, fw), out_shape=[jax.Shap...]
  transfers between devices with their start and end apart: 25 -> 25, of which waited for: 8 -> 8; matrix products, arithmetic and copies ran while one was open for 2% -> 1% of each run, Pallas kernels for 34% -> 24%
where the time goes in v2:
time: 86.8 us; the launch traced here: 85.6 us
  starting transfers between devices  37.2 us (43%)
  Pallas kernels  22.3 us (26%)
  waiting for transfers between devices  21.2 us (24%)
  other arithmetic  2.06 us (2%)
  local copies, waits for them, and re-layouts  1.92 us (2%)
    ppermute x8, starting transfers between devices, along(): return lax.ppermute(x, 'row', pairs)  18.8 us
    ppermute x8, waiting for transfers between devices, along(): return lax.ppermute(x, 'row', pairs)  12.5 us
    pallas_call x2, Pallas kernels, pair(): return f(pos, l, lr, rt, wt, e, went)  11.4 us
    ppermute x11, waiting for transfers between devices, shift(): return lax.ppermute(x, axis, [(i, (i + d) % n) for i in range(n)])  8.13 us
    ppermute x3, starting transfers between devices, per_device(): lax.ppermute(x, 'row', [(i, i ^ d) for i in range(nr)])  5.99 us
    ppermute x1, starting transfers between devices, per_device(): lax.ppermute(edge_activations, 'row', [(0, nr - 1), (nr - 1, 0)])  5.5 us
    pallas_call x2, Pallas kernels, split_call(): pl.pallas_call(functools.partial(kernel, J, n), out_shape=[jax.ShapeDtype...  5.37 us
    ppermute x11, starting transfers between devices, shift(): return lax.ppermute(x, axis, [(i, (i + d) % n) for i in range(n)])  4.67 us
  transfers between devices with their start and end apart: 25, of which 8 were waited for; matrix products, arithmetic and copies ran while one was open for 1% of the time, Pallas kernels for 24%

profile of v2, /device:TPU:0, one launch (start us, length us, event | category | flops | bytes accessed | tf_op | source)
XLA Modules:
  0.0 85.6 jit_solution(6260897782458214347)
XLA Ops:
  0.0 1.2 %convert_reduce_fusion = f32[16,48]{1,0:T(8,128)S(1)} fusion(bf16[16,48,256]{2,1,0:T(8,128)(2,1)} %param.7), kind=kLoop, calls=%fused_computation.3 | loop fusion | flops 392448 | bytes 396288 | tf_op jit(solution)/shard_map/reduce_sum | solution.py:21
  2.5 3.1 %collective-permute-start.2 = (bf16[16,1536]{1,0:T(8,128)(2,1)S(1)}, bf16[16,1536]{1,0:T(8,128)(2,1)S(1)}, u32[]{:S(2)}, u32[]{:S(2)}) collective-permute-start(bf16[16,1536]{1,0:T(8,128)(2,1)S(1)} %reshape.23), channel_id=1, source_target_pairs={{0,4},{4,0},{8,12},{12,8},{1,5},{5,1},{9,13},{13,9},{2,6},{6,2},{1... | collective-permute-start | bytes 147464 | tf_op jit(solution)/shard_map/ppermute | solution.py:662
  5.7 2.6 %collective-permute-start.3 = (bf16[16,1536]{1,0:T(8,128)(2,1)S(1)}, bf16[16,1536]{1,0:T(8,128)(2,1)S(1)}, u32[]{:S(2)}, u32[]{:S(2)}) collective-permute-start(bf16[16,1536]{1,0:T(8,128)(2,1)S(1)} %reshape.23), channel_id=1, source_target_pairs={{0,8},{4,12},{8,0},{12,4},{1,9},{5,13},{9,1},{13,5},{2,10},{6,14},... | collective-permute-start | bytes 147464 | tf_op jit(solution)/shard_map/ppermute | solution.py:662
  8.9 1.6 %collective-permute-start = (bf16[16,1536]{1,0:T(8,128)(2,1)S(1)}, bf16[16,1536]{1,0:T(8,128)(2,1)S(1)}, u32[]{:S(2)}, u32[]{:S(2)}) collective-permute-start(bf16[16,1536]{1,0:T(8,128)(2,1)S(1)} %reshape.22), channel_id=1, source_target_pairs={{0,2},{2,0},{1,3},{3,1},{4,6},{6,4},{5,7},{7,5},{8,10},{10,8},{9,1... | collective-permute-start | bytes 147464 | tf_op jit(solution)/shard_map/ppermute | solution.py:619
  11.1 5.5 %collective-permute-start.13 = (bf16[24,96,128]{2,1,0:T(8,128)(2,1)S(1)}, bf16[24,96,128]{2,1,0:T(8,128)(2,1)S(1)}, u32[]{:S(2)}, u32[]{:S(2)}) collective-permute-start(bf16[24,96,128]{2,1,0:T(8,128)(2,1)S(1)} %copy-done.4), channel_id=1, source_target_pairs={{0,12},{12,0},{1,13},{13,1},{2,14},{14,2},{3,15},{15,3},{16,28},{2... | collective-permute-start | bytes 1769480 | tf_op jit(solution)/shard_map/ppermute | solution.py:673
  16.7 0.7 copy-done.3
  18.5 0.6 collective-permute-start.4
  19.2 4.6 %collective-permute-done.4 = bf16[3,16,1536]{2,1,0:T(8,128)(2,1)S(1)} collective-permute-done((bf16[3,16,1536]{2,1,0:T(8,128)(2,1)S(1)}, bf16[3,16,1536]{2,1,0:T(8,128)(2,1)S(1)}, u32[]{:S(2)}, u32[]{:S(2)}) %collective-permute-start.4) | collective-permute-done | bytes 147488 | tf_op jit(solution)/shard_map/ppermute | solution.py:619
  24.6 0.7 collective-permute-done.6.recv_ref
  25.3 1.2 %shard_map.73.refs_2_ = bf16[32,96,64]{2,1,0:T(8,128)(2,1)S(1)} custom-call(bf16[2,2,16,1536]{3,2,1,0:T(8,128)(2,1)S(1)} %pad_maximum_fusion.1.own_ref, bf16[2,2,16,1536]{3,2,1,0:T(8,128)(2,1)S(1)} %collective-permute-done.6.recv_ref), custom_call_target="tpu_custom_call" | custom-call | tf_op jit(solution)/shard_map/pallas_call | solution.py:101
  26.5 6.4 %shard_map.75 = (bf16[24,128,96]{2,1,0:T(8,128)(2,1)S(1)}, bf16[24,128,96]{2,1,0:T(8,128)(2,1)S(1)}, bf16[64,24,128]{2,1,0:T(8,128)(2,1)S(1)}, bf16[64,24,128]{2...) custom-call(s32[3]{0:T(128)S(1)} %pad_add_fusion.pos_ref, ...), custom_call_target="tpu_custom_call" | custom-call | flops 1283457024 | bytes 7077888 | tf_op jit(solution)/shard_map/pallas_call | solution.py:229
  33.2 0.7 collective-permute-start.11
  34.3 13.5 %collective-permute-start.9 = (bf16[48,24,128]{2,1,0:T(8,128)(2,1)S(1)}, bf16[48,24,128]{2,1,0:T(8,128)(2,1)S(1)}, u32[]{:S(2)}, u32[]{:S(2)}) collective-permute-start(bf16[48,24,128]{2,1,0:T(8,128)(2,1)S(1)} %get-tuple-element.33.rest_0_), channel_id=1, source_target_pairs={{0,4},{4,0},{8,12},{12,8},{1,5},{5,1},{9,13},{13,9},{2,6},{6,2},{1... | collective-permute-start | bytes 884744 | tf_op jit(solution)/shard_map/ppermute | solution.py:684
  47.8 0.7 collective-permute-start.12
  48.5 4.9 %shard_map.76 = (bf16[48,24,128]{2,1,0:T(8,128)(2,1)S(1)}, bf16[48,24,128]{2,1,0:T(8,128)(2,1)S(1)}) custom-call(s32[3]{0:T(128)S(1)} %pad_add_fusion.pos_ref, bf16[2,32,768]{2,1,0:T(8,128)(2,1)S(1)} %get-tuple-element.58.refs_0_, bf16[2,32,768]{2,1,0:T(8,128)(2,1)S(1)} %collective-permute-done.5.refs_1_, bf16[32,96,64]{2,1,0:T(8,128)(2,1)S(1)} %shard_map.73.refs_2_, ...), custom_call_target="tpu_custom_call" | custom-call | flops 1283457024 | bytes 7077888 | tf_op jit(solution)/shard_map/pallas_call | solution.py:229
  53.5 2.1 %collective-permute-done.9.rest_2_ = bf16[48,24,128]{2,1,0:T(8,128)(2,1)S(1)} collective-permute-done((bf16[48,24,128]{2,1,0:T(8,128)(2,1)S(1)}, bf16[48,24,128]{2,1,0:T(8,128)(2,1)S(1)}, u32[]{:S(2)}, u32[]{:S(2)}) %collective-permute-start.9) | collective-permute-done | bytes 294944 | tf_op jit(solution)/shard_map/ppermute | solution.py:684
  55.6 0.7 collective-permute-start.15
  56.3 1.3 %collective-permute-start.17 = (bf16[48,24,128]{2,1,0:T(8,128)(2,1)S(1)}, bf16[48,24,128]{2,1,0:T(8,128)(2,1)S(1)}, u32[]{:S(2)}, u32[]{:S(2)}) collective-permute-start(bf16[48,24,128]{2,1,0:T(8,128)(2,1)S(1)} %collective-permute-done.11.rest_4_), channel_id=1, source_target_pairs={{4,0},{8,12},{5,1},{9,13},{6,2},{10,14},{7,3},{11,15},{20,16},{24,... | collective-permute-start | bytes 884744 | tf_op jit(solution)/shard_map/ppermute | solution.py:684
  57.6 3.8 %collective-permute-done.10.rest_3_ = bf16[48,24,128]{2,1,0:T(8,128)(2,1)S(1)} collective-permute-done((bf16[48,24,128]{2,1,0:T(8,128)(2,1)S(1)}, bf16[48,24,128]{2,1,0:T(8,128)(2,1)S(1)}, u32[]{:S(2)}, u32[]{:S(2)}) %collective-permute-start.10) | collective-permute-done | bytes 294944 | tf_op jit(solution)/shard_map/ppermute | solution.py:684
  61.4 0.7 collective-permute-start.16
  62.1 1.3 %collective-permute-start.18 = (bf16[48,24,128]{2,1,0:T(8,128)(2,1)S(1)}, bf16[48,24,128]{2,1,0:T(8,128)(2,1)S(1)}, u32[]{:S(2)}, u32[]{:S(2)}) collective-permute-start(bf16[48,24,128]{2,1,0:T(8,128)(2,1)S(1)} %collective-permute-done.12.rest_5_), channel_id=1, source_target_pairs={{4,0},{8,12},{5,1},{9,13},{6,2},{10,14},{7,3},{11,15},{20,16},{24,... | collective-permute-start | bytes 884744 | tf_op jit(solution)/shard_map/ppermute | solution.py:684
  63.4 3.5 %shard_map.77 = (bf16[24,24,128]{2,1,0:T(8,128)(2,1)S(1)}, bf16[24,24,128]{2,1,0:T(8,128)(2,1)S(1)}, bf16[24,24,128]{2,1,0:T(8,128)(2,1)S(1)}, bf16[24,24,128]{2...) custom-call(s32[3]{0:T(128)S(1)} %pad_add_fusion.pos_ref, ...), custom_call_target="tpu_custom_call" | custom-call | flops 452984832 | bytes 3538944 | tf_op jit(solution)/shard_map/pallas_call | solution.py:502
  66.9 0.6 collective-permute-start.22
  67.5 1.0 %collective-permute-done.17.rest_2_ = bf16[48,24,128]{2,1,0:T(8,128)(2,1)S(1)} collective-permute-done((bf16[48,24,128]{2,1,0:T(8,128)(2,1)S(1)}, bf16[48,24,128]{2,1,0:T(8,128)(2,1)S(1)}, u32[]{:S(2)}, u32[]{:S(2)}) %collective-permute-start.17) | collective-permute-done | bytes 294944 | tf_op jit(solution)/shard_map/ppermute | solution.py:684
  68.5 0.6 collective-permute-start.24
  69.1 5.7 %collective-permute-done.18.rest_3_ = bf16[48,24,128]{2,1,0:T(8,128)(2,1)S(1)} collective-permute-done((bf16[48,24,128]{2,1,0:T(8,128)(2,1)S(1)}, bf16[48,24,128]{2,1,0:T(8,128)(2,1)S(1)}, u32[]{:S(2)}, u32[]{:S(2)}) %collective-permute-start.18) | collective-permute-done | bytes 294944 | tf_op jit(solution)/shard_map/ppermute | solution.py:684
  74.8 1.9 %shard_map.78 = (bf16[24,24,128]{2,1,0:T(8,128)(2,1)S(1)}, bf16[24,24,128]{2,1,0:T(8,128)(2,1)S(1)}, bf16[24,24,128]{2,1,0:T(8,128)(2,1)S(1)}, bf16[24,24,128]{2,1,0:T(8,128)(2,1)S(1)}) custom-call(s32[3]{0:T(128)S(1)} %pad_add_fusion.pos_ref, bf16[64,24,128]{2,1,0:T(8,128)(2,1)S(1)} %get-tuple-element.31.lk_ref, ...), custom_call_target="tpu_custom_call" | custom-call | flops 150994944 | bytes 1179648 | tf_op jit(solution)/shard_map/pallas_call | solution.py:502
  76.7 0.6 collective-permute-start.19
  77.3 1.6 %collective-permute-start.21 = (bf16[24,24,128]{2,1,0:T(8,128)(2,1)S(1)}, bf16[24,24,128]{2,1,0:T(8,128)(2,1)S(1)}, u32[]{:S(2)}, u32[]{:S(2)}) collective-permute-start(bf16[24,24,128]{2,1,0:T(8,128)(2,1)S(1)} %get-tuple-element.42), channel_id=1, source_target_pairs={{0,3},{1,2},{2,1},{3,0},{4,7},{5,6},{6,5},{7,4},{8,11},{9,10},{10,... | collective-permute-start | bytes 442376 | tf_op jit(solution)/shard_map/ppermute | solution.py:629
  78.9 1.7 %shard_map.79 = (bf16[24,48,128]{2,1,0:T(8,128)(2,1)S(1)}, bf16[24,48,128]{2,1,0:T(8,128)(2,1)S(1)}, bf16[24,48,128]{2,1,0:T(8,128)(2,1)S(1)}) custom-call(s32[3]{0:T(128)S(1)} %pad_add_fusion.pos_ref, bf16[24,24,128]{2,1,0:T(8,128)(2,1)S(1)} %get-tuple-element.43.a_ref, bf16[24,24,128]{2,1,0:T(8,128)(2,1)S(1)} %collective-permute-done.22.b_ref, ...), custom_call_target="tpu_custom_call" | custom-call | flops 37748736 | bytes 1474560 | tf_op jit(solution)/shard_map/pallas_call | solution.py:606
  80.6 2.8 %collective-permute-done.19.b_ref = bf16[24,24,128]{2,1,0:T(8,128)(2,1)S(1)} collective-permute-done((bf16[24,24,128]{2,1,0:T(8,128)(2,1)S(1)}, bf16[24,24,128]{2,1,0:T(8,128)(2,1)S(1)}, u32[]{:S(2)}, u32[]{:S(2)}) %collective-permute-start.19) | collective-permute-done | bytes 147488 | tf_op jit(solution)/shard_map/ppermute | solution.py:619
  83.4 2.2 %shard_map.80 = bf16[24,96,128]{2,1,0:T(8,128)(2,1)} custom-call(s32[3]{0:T(128)S(1)} %pad_add_fusion.pos_ref, bf16[24,24,128]{2,1,0:T(8,128)(2,1)S(1)} %get-tuple-element.39.a_ref, bf16[24,24,128]{2,1,0:T(8,128)(2,1)S(1)} %collective-permute-done.19.b_ref, bf16[24,24,128]{2,1,0:T(8,128)(2,1)S(1)} %collective-permute-done.20.c_ref, ...), custom_call_target="tpu_custom_call" | custom-call | flops 37748736 | bytes 1474560 | tf_op jit(solution)/shard_map/pallas_call | solution.py:606
  (66 shorter events, 5.2 us)
Async XLA Ops:
  0.0 1.9 %copy-start = (bf16[256,32]{0,1:T(8,128)(2,1)S(1)}, bf16[256,32]{0,1:T(8,128)(2,1)}, u32[]{:S(2)}) copy-start(bf16[256,32]{0,1:T(8,128)(2,1)} %param.10) | copy-start | bytes 49156
  0.0 1.3 %copy-start.5 = (bf16[16,48,256]{2,1,0:T(8,128)(2,1)S(1)}, bf16[16,48,256]{2,1,0:T(8,128)(2,1)}, u32[]{:S(2)}) copy-start(bf16[16,48,256]{2,1,0:T(8,128)(2,1)} %param.7) | copy-start | bytes 1179652
  2.3 5.9 %copy-start.6 = (bf16[256,32]{0,1:T(8,128)(2,1)S(1)}, bf16[256,32]{0,1:T(8,128)(2,1)}, u32[]{:S(2)}) copy-start(bf16[256,32]{0,1:T(8,128)(2,1)} %param.9) | copy-start | bytes 49156
  2.5 15.9 %collective-permute-start.2 = (bf16[16,1536]{1,0:T(8,128)(2,1)S(1)}, bf16[16,1536]{1,0:T(8,128)(2,1)S(1)}, u32[]{:S(2)}, u32[]{:S(2)}) collective-permute-start(bf16[16,1536]{1,0:T(8,128)(2,1)S(1)} %reshape.23), channel_id=1, source_target_pairs={{0,4},{4,0},{8,12},{12,8},{1,5},{5,1},{9,13},{13,9},{2,6},{6,2},{1... | collective-permute-start | bytes 147464 | tf_op jit(solution)/shard_map/ppermute | solution.py:662
  5.7 12.8 %collective-permute-start.3 = (bf16[16,1536]{1,0:T(8,128)(2,1)S(1)}, bf16[16,1536]{1,0:T(8,128)(2,1)S(1)}, u32[]{:S(2)}, u32[]{:S(2)}) collective-permute-start(bf16[16,1536]{1,0:T(8,128)(2,1)S(1)} %reshape.23), channel_id=1, source_target_pairs={{0,8},{4,12},{8,0},{12,4},{1,9},{5,13},{9,1},{13,5},{2,10},{6,14},... | collective-permute-start | bytes 147464 | tf_op jit(solution)/shard_map/ppermute | solution.py:662
  8.5 2.7 %copy-start.4 = (bf16[24,96,128]{2,1,0:T(8,128)(2,1)S(1)}, bf16[24,96,128]{2,1,0:T(8,128)(2,1)}, u32[]{:S(2)}) copy-start(bf16[24,96,128]{2,1,0:T(8,128)(2,1)} %refs_4_.1) | copy-start | bytes 1769476
  8.9 9.0 %collective-permute-start = (bf16[16,1536]{1,0:T(8,128)(2,1)S(1)}, bf16[16,1536]{1,0:T(8,128)(2,1)S(1)}, u32[]{:S(2)}, u32[]{:S(2)}) collective-permute-start(bf16[16,1536]{1,0:T(8,128)(2,1)S(1)} %reshape.22), channel_id=1, source_target_pairs={{0,2},{2,0},{1,3},{3,1},{4,6},{6,4},{5,7},{7,5},{8,10},{10,8},{9,1... | collective-permute-start | bytes 147464 | tf_op jit(solution)/shard_map/ppermute | solution.py:619
  10.6 6.1 %copy-start.1 = (bf16[1024,128]{1,0:T(8,128)(2,1)S(1)}, bf16[1024,128]{1,0:T(8,128)(2,1)}, u32[]{:S(2)}) copy-start(bf16[1024,128]{1,0:T(8,128)(2,1)} %w_ref.1) | copy-start | bytes 786436
  10.8 5.9 %copy-start.2 = (bf16[128,640]{1,0:T(8,128)(2,1)S(1)}, bf16[128,640]{1,0:T(8,128)(2,1)}, u32[]{:S(2)}) copy-start(bf16[128,640]{1,0:T(8,128)(2,1)} %n_ref.1) | copy-start | bytes 491524
  10.8 7.6 %collective-permute-start.1 = (bf16[2,16,1536]{2,1,0:T(8,128)(2,1)S(1)}, bf16[2,16,1536]{2,1,0:T(8,128)(2,1)S(1)}, u32[]{:S(2)}, u32[]{:S(2)}) collective-permute-start(bf16[2,16,1536]{2,1,0:T(8,128)(2,1)S(1)} %pad_maximum_fusion.3), channel_id=1, source_target_pairs={{0,12},{4,8},{8,4},{12,0},{1,13},{5,9},{9,5},{13,1},{2,14},{6,10},... | collective-permute-start | bytes 294920 | tf_op jit(solution)/shard_map/ppermute | solution.py:662
  11.1 36.7 %collective-permute-start.13 = (bf16[24,96,128]{2,1,0:T(8,128)(2,1)S(1)}, bf16[24,96,128]{2,1,0:T(8,128)(2,1)S(1)}, u32[]{:S(2)}, u32[]{:S(2)}) collective-permute-start(bf16[24,96,128]{2,1,0:T(8,128)(2,1)S(1)} %copy-done.4), channel_id=1, source_target_pairs={{0,12},{12,0},{1,13},{13,1},{2,14},{14,2},{3,15},{15,3},{16,28},{2... | collective-permute-start | bytes 1769480 | tf_op jit(solution)/shard_map/ppermute | solution.py:673
  16.7 0.8 copy-start.3
  18.5 5.2 %collective-permute-start.4 = (bf16[3,16,1536]{2,1,0:T(8,128)(2,1)S(1)}, bf16[3,16,1536]{2,1,0:T(8,128)(2,1)S(1)}, u32[]{:S(2)}, u32[]{:S(2)}) collective-permute-start(bf16[3,16,1536]{2,1,0:T(8,128)(2,1)S(1)} %pad_maximum_fusion.2), channel_id=1, source_target_pairs={{0,2},{2,0},{1,3},{3,1},{4,6},{6,4},{5,7},{7,5},{8,10},{10,8},{9,1... | collective-permute-start | bytes 442376 | tf_op jit(solution)/shard_map/ppermute | solution.py:619
  23.8 1.5 %collective-permute-start.6 = (bf16[2,2,16,1536]{3,2,1,0:T(8,128)(2,1)S(1)}, bf16[2,2,16,1536]{3,2,1,0:T(8,128)(2,1)S(1)}, u32[]{:S(2)}, u32[]{:S(2)}) collective-permute-start(bf16[2,2,16,1536]{3,2,1,0:T(8,128)(2,1)S(1)} %pad_maximum_fusion.1.own_ref), channel_id=1, source_target_pairs={{0,1},{1,0},{2,3},{3,2},{4,5},{5,4},{6,7},{7,6},{8,9},{9,8},{10,11... | collective-permute-start | bytes 589832 | tf_op jit(solution)/shard_map/ppermute | solution.py:619
  23.9 2.6 %collective-permute-start.5 = (bf16[2,32,768]{2,1,0:T(8,128)(2,1)S(1)}, bf16[2,32,768]{2,1,0:T(8,128)(2,1)S(1)}, u32[]{:S(2)}, u32[]{:S(2)}) collective-permute-start(bf16[2,32,768]{2,1,0:T(8,128)(2,1)S(1)} %get-tuple-element.57), channel_id=1, source_target_pairs={{0,1},{1,0},{2,3},{3,2},{4,5},{5,4},{6,7},{7,6},{8,9},{9,8},{10,11... | collective-permute-start | bytes 294920 | tf_op jit(solution)/shard_map/ppermute | solution.py:619
  32.9 14.8 %collective-permute-start.8 = (bf16[48,24,128]{2,1,0:T(8,128)(2,1)S(1)}, bf16[48,24,128]{2,1,0:T(8,128)(2,1)S(1)}, u32[]{:S(2)}, u32[]{:S(2)}) collective-permute-start(bf16[48,24,128]{2,1,0:T(8,128)(2,1)S(1)} %get-tuple-element.34), channel_id=1, source_target_pairs={{0,1},{1,0},{2,3},{3,2},{4,5},{5,4},{6,7},{7,6},{8,9},{9,8},{10,11... | collective-permute-start | bytes 884744 | tf_op jit(solution)/shard_map/ppermute | solution.py:619
  33.2 20.3 %collective-permute-start.11 = (bf16[48,24,128]{2,1,0:T(8,128)(2,1)S(1)}, bf16[48,24,128]{2,1,0:T(8,128)(2,1)S(1)}, u32[]{:S(2)}, u32[]{:S(2)}) collective-permute-start(bf16[48,24,128]{2,1,0:T(8,128)(2,1)S(1)} %get-tuple-element.33.rest_0_), channel_id=1, source_target_pairs={{4,8},{8,4},{5,9},{9,5},{6,10},{10,6},{7,11},{11,7},{20,24},{24,20... | collective-permute-start | bytes 884744 | tf_op jit(solution)/shard_map/ppermute | solution.py:684
  33.8 22.5 %collective-permute-start.7 = (bf16[64,24,128]{2,1,0:T(8,128)(2,1)S(1)}, bf16[64,24,128]{2,1,0:T(8,128)(2,1)S(1)}, u32[]{:S(2)}, u32[]{:S(2)}) collective-permute-start(bf16[64,24,128]{2,1,0:T(8,128)(2,1)S(1)} %get-tuple-element.32), channel_id=1, source_target_pairs={{0,1},{1,0},{2,3},{3,2},{4,5},{5,4},{6,7},{7,6},{8,9},{9,8},{10,11... | collective-permute-start | bytes 1179656 | tf_op jit(solution)/shard_map/ppermute | solution.py:619
  34.3 21.4 %collective-permute-start.9 = (bf16[48,24,128]{2,1,0:T(8,128)(2,1)S(1)}, bf16[48,24,128]{2,1,0:T(8,128)(2,1)S(1)}, u32[]{:S(2)}, u32[]{:S(2)}) collective-permute-start(bf16[48,24,128]{2,1,0:T(8,128)(2,1)S(1)} %get-tuple-element.33.rest_0_), channel_id=1, source_target_pairs={{0,4},{4,0},{8,12},{12,8},{1,5},{5,1},{9,13},{13,9},{2,6},{6,2},{1... | collective-permute-start | bytes 884744 | tf_op jit(solution)/shard_map/ppermute | solution.py:684
  47.8 13.6 %collective-permute-start.10 = (bf16[48,24,128]{2,1,0:T(8,128)(2,1)S(1)}, bf16[48,24,128]{2,1,0:T(8,128)(2,1)S(1)}, u32[]{:S(2)}, u32[]{:S(2)}) collective-permute-start(bf16[48,24,128]{2,1,0:T(8,128)(2,1)S(1)} %collective-permute-done.8.rest_1_), channel_id=1, source_target_pairs={{0,4},{4,0},{8,12},{12,8},{1,5},{5,1},{9,13},{13,9},{2,6},{6,2},{1... | collective-permute-start | bytes 884744 | tf_op jit(solution)/shard_map/ppermute | solution.py:684
  47.8 14.3 %collective-permute-start.12 = (bf16[48,24,128]{2,1,0:T(8,128)(2,1)S(1)}, bf16[48,24,128]{2,1,0:T(8,128)(2,1)S(1)}, u32[]{:S(2)}, u32[]{:S(2)}) collective-permute-start(bf16[48,24,128]{2,1,0:T(8,128)(2,1)S(1)} %collective-permute-done.8.rest_1_), channel_id=1, source_target_pairs={{4,8},{8,4},{5,9},{9,5},{6,10},{10,6},{7,11},{11,7},{20,24},{24,20... | collective-permute-start | bytes 884744 | tf_op jit(solution)/shard_map/ppermute | solution.py:684
  53.4 10.0 %collective-permute-start.14 = (bf16[48,24,128]{2,1,0:T(8,128)(2,1)S(1)}, bf16[48,24,128]{2,1,0:T(8,128)(2,1)S(1)}, u32[]{:S(2)}, u32[]{:S(2)}) collective-permute-start(bf16[48,24,128]{2,1,0:T(8,128)(2,1)S(1)} %get-tuple-element.36), channel_id=1, source_target_pairs={{0,1},{1,0},{2,3},{3,2},{4,5},{5,4},{6,7},{7,6},{8,9},{9,8},{10,11... | collective-permute-start | bytes 884744 | tf_op jit(solution)/shard_map/ppermute | solution.py:619
  55.6 11.9 %collective-permute-start.15 = (bf16[48,24,128]{2,1,0:T(8,128)(2,1)S(1)}, bf16[48,24,128]{2,1,0:T(8,128)(2,1)S(1)}, u32[]{:S(2)}, u32[]{:S(2)}) collective-permute-start(bf16[48,24,128]{2,1,0:T(8,128)(2,1)S(1)} %collective-permute-done.9.rest_2_), channel_id=1, source_target_pairs={{4,8},{8,4},{5,9},{9,5},{6,10},{10,6},{7,11},{11,7},{20,24},{24,20... | collective-permute-start | bytes 884744 | tf_op jit(solution)/shard_map/ppermute | solution.py:684
  56.3 12.2 %collective-permute-start.17 = (bf16[48,24,128]{2,1,0:T(8,128)(2,1)S(1)}, bf16[48,24,128]{2,1,0:T(8,128)(2,1)S(1)}, u32[]{:S(2)}, u32[]{:S(2)}) collective-permute-start(bf16[48,24,128]{2,1,0:T(8,128)(2,1)S(1)} %collective-permute-done.11.rest_4_), channel_id=1, source_target_pairs={{4,0},{8,12},{5,1},{9,13},{6,2},{10,14},{7,3},{11,15},{20,16},{24,... | collective-permute-start | bytes 884744 | tf_op jit(solution)/shard_map/ppermute | solution.py:684
  61.4 7.7 %collective-permute-start.16 = (bf16[48,24,128]{2,1,0:T(8,128)(2,1)S(1)}, bf16[48,24,128]{2,1,0:T(8,128)(2,1)S(1)}, u32[]{:S(2)}, u32[]{:S(2)}) collective-permute-start(bf16[48,24,128]{2,1,0:T(8,128)(2,1)S(1)} %collective-permute-done.10.rest_3_), channel_id=1, source_target_pairs={{4,8},{8,4},{5,9},{9,5},{6,10},{10,6},{7,11},{11,7},{20,24},{24,20... | collective-permute-start | bytes 884744 | tf_op jit(solution)/shard_map/ppermute | solution.py:684
  62.1 12.7 %collective-permute-start.18 = (bf16[48,24,128]{2,1,0:T(8,128)(2,1)S(1)}, bf16[48,24,128]{2,1,0:T(8,128)(2,1)S(1)}, u32[]{:S(2)}, u32[]{:S(2)}) collective-permute-start(bf16[48,24,128]{2,1,0:T(8,128)(2,1)S(1)} %collective-permute-done.12.rest_5_), channel_id=1, source_target_pairs={{4,0},{8,12},{5,1},{9,13},{6,2},{10,14},{7,3},{11,15},{20,16},{24,... | collective-permute-start | bytes 884744 | tf_op jit(solution)/shard_map/ppermute | solution.py:684
  66.9 10.4 %collective-permute-start.22 = (bf16[24,24,128]{2,1,0:T(8,128)(2,1)S(1)}, bf16[24,24,128]{2,1,0:T(8,128)(2,1)S(1)}, u32[]{:S(2)}, u32[]{:S(2)}) collective-permute-start(bf16[24,24,128]{2,1,0:T(8,128)(2,1)S(1)} %get-tuple-element.44), channel_id=1, source_target_pairs={{0,2},{2,0},{1,3},{3,1},{4,6},{6,4},{5,7},{7,5},{8,10},{10,8},{9,1... | collective-permute-start | bytes 442376 | tf_op jit(solution)/shard_map/ppermute | solution.py:619
  67.5 11.4 %collective-permute-start.23 = (bf16[24,24,128]{2,1,0:T(8,128)(2,1)S(1)}, bf16[24,24,128]{2,1,0:T(8,128)(2,1)S(1)}, u32[]{:S(2)}, u32[]{:S(2)}) collective-permute-start(bf16[24,24,128]{2,1,0:T(8,128)(2,1)S(1)} %get-tuple-element.45), channel_id=1, source_target_pairs={{0,1},{1,0},{2,3},{3,2},{4,5},{5,4},{6,7},{7,6},{8,9},{9,8},{10,11... | collective-permute-start | bytes 442376 | tf_op jit(solution)/shard_map/ppermute | solution.py:619
  68.5 10.4 %collective-permute-start.24 = (bf16[24,24,128]{2,1,0:T(8,128)(2,1)S(1)}, bf16[24,24,128]{2,1,0:T(8,128)(2,1)S(1)}, u32[]{:S(2)}, u32[]{:S(2)}) collective-permute-start(bf16[24,24,128]{2,1,0:T(8,128)(2,1)S(1)} %get-tuple-element.46), channel_id=1, source_target_pairs={{0,3},{1,2},{2,1},{3,0},{4,7},{5,6},{6,5},{7,4},{8,11},{9,10},{10,... | collective-permute-start | bytes 442376 | tf_op jit(solution)/shard_map/ppermute | solution.py:629
  76.7 6.7 %collective-permute-start.19 = (bf16[24,24,128]{2,1,0:T(8,128)(2,1)S(1)}, bf16[24,24,128]{2,1,0:T(8,128)(2,1)S(1)}, u32[]{:S(2)}, u32[]{:S(2)}) collective-permute-start(bf16[24,24,128]{2,1,0:T(8,128)(2,1)S(1)} %get-tuple-element.40), channel_id=1, source_target_pairs={{0,2},{2,0},{1,3},{3,1},{4,6},{6,4},{5,7},{7,5},{8,10},{10,8},{9,1... | collective-permute-start | bytes 442376 | tf_op jit(solution)/shard_map/ppermute | solution.py:619
  77.3 6.2 %collective-permute-start.20 = (bf16[24,24,128]{2,1,0:T(8,128)(2,1)S(1)}, bf16[24,24,128]{2,1,0:T(8,128)(2,1)S(1)}, u32[]{:S(2)}, u32[]{:S(2)}) collective-permute-start(bf16[24,24,128]{2,1,0:T(8,128)(2,1)S(1)} %get-tuple-element.41), channel_id=1, source_target_pairs={{0,1},{1,0},{2,3},{3,2},{4,5},{5,4},{6,7},{7,6},{8,9},{9,8},{10,11... | collective-permute-start | bytes 442376 | tf_op jit(solution)/shard_map/ppermute | solution.py:619
  77.3 6.2 %collective-permute-start.21 = (bf16[24,24,128]{2,1,0:T(8,128)(2,1)S(1)}, bf16[24,24,128]{2,1,0:T(8,128)(2,1)S(1)}, u32[]{:S(2)}, u32[]{:S(2)}) collective-permute-start(bf16[24,24,128]{2,1,0:T(8,128)(2,1)S(1)} %get-tuple-element.42), channel_id=1, source_target_pairs={{0,3},{1,2},{2,1},{3,0},{4,7},{5,6},{6,5},{7,4},{8,11},{9,10},{10,... | collective-permute-start | bytes 442376 | tf_op jit(solution)/shard_map/ppermute | solution.py:629

commit v3 on v2

--- a/solution.py
+++ b/solution.py
@@ -391,13 +391,12 @@
             lm[(ch - main) * parts + t] = jnp.where(inside, 0.0, moved).astype(jnp.bfloat16)
 
 
-def shard_products(lk_ref, lr_ref, lm, rv, k, J, half, TI, store):
+def shard_products(lk_ref, lr_ref, lm, right, ways, J, half, TI, store):
     parts, main = packing(half, J)
     tails = half - main
 
     def dot(left, row):
-        right = rv[k, :, row].reshape(2 * TI, LANES)
-        return lax.dot_general(left, right, (((1,), (1,)), ((), ())), preferred_element_type=jnp.float32)
+        return lax.dot_general(left, right(row), (((1,), (1,)), ((), ())), preferred_element_type=jnp.float32)
 
     def channel(ch):
         if ch < main:
@@ -408,23 +407,23 @@
             x = x + dot(lm[q * parts + t], t * tails + q)
         return x
 
-    pairs = half // 2
+    count = half // ways
     cols = 4 * TI
     pad = jnp.zeros((2 * TI, LANES - cols), jnp.float32)
-    p2, m2 = packing(pairs, cols)
-    t2 = pairs - m2
-
-    def both(q):
-        return jnp.concatenate([channel(q), channel(q + pairs), pad], axis=1)
+    p2, m2 = packing(count, cols)
+    t2 = count - m2
+
+    def beside(q):
+        return jnp.concatenate([channel(q + w * count) for w in range(ways)] + [pad], axis=1)
 
     inside = lane_index((2 * TI, LANES)) < cols
     spare = LANES - cols
     for q in range(t2):
-        tail = both(m2 + q)
+        tail = beside(m2 + q)
         for t in range(p2):
-            store(t * t2 + q, jnp.where(inside, both(t * t2 + q), pltpu.roll(tail, cols - spare * t, 1)).astype(jnp.bfloat16))
-    for q in range(0 if p2 else pairs):
-        store(q, both(q).astype(jnp.bfloat16))
+            store(t * t2 + q, jnp.where(inside, beside(t * t2 + q), pltpu.roll(tail, cols - spare * t, 1)).astype(jnp.bfloat16))
+    for q in range(0 if p2 else count):
+        store(q, beside(q).astype(jnp.bfloat16))
 
 
 def early_kernel(J, n, pos_ref, lk_ref, lr_ref, *rest):
@@ -453,7 +452,7 @@
         def store(r, x, k=k):
             acc[k, r] = x
 
-        shard_products(lk_ref, lr_ref, lm, rv, k, J, half, TI, store)
+        shard_products(lk_ref, lr_ref, lm, lambda r, k=k: rv[k, :, r].reshape(2 * TI, LANES), 2, J, half, TI, store)
     home = col == row // 2
     send = jnp.where(home, acc[2], acc[0])
     keep = jnp.where(home, acc[0], acc[2])
@@ -463,19 +462,17 @@
         outs[4 + u][...] = acc[1, :, u * TI : (u + 1) * TI]
 
 
-def late_kernel(J, n, pos_ref, lk_ref, lr_ref, a_ref, b_ref, *rest):
-    inner, outward = rest[0:2], rest[2:4]
-    outs = rest[4:8]
-    rv, lm, acc, sem = rest[8:]
+def late_kernel(u, J, n, pos_ref, lk_ref, lr_ref, a_ref, b_ref, inner, outward, *rest):
+    outs = rest[:4]
+    rv, lm, acc, sem = rest[4:]
     half, TI, _ = lk_ref.shape
-    row, col, sub = pos_ref[0], pos_ref[1], pos_ref[2]
+    row, col = pos_ref[0], pos_ref[1]
     edge = (row == 0) | (row == n - 1)
 
     def each(action):
-        for cond, refs in ((edge, outward), (jnp.logical_not(edge), inner)):
-            for u in range(2):
-                c = pltpu.make_async_copy(refs[u], rv.at[0, sub if u == 0 else 1 - sub], sem.at[u])
-                pl.when(cond)(lambda c=c: action(c))
+        for cond, ref in ((edge, outward), (jnp.logical_not(edge), inner)):
+            c = pltpu.make_async_copy(ref, rv, sem.at[0])
+            pl.when(cond)(lambda c=c: action(c))
 
     each(lambda c: c.start())
     masked_left(lk_ref, lr_ref, lm, J)
@@ -484,64 +481,80 @@
     def store(r, x):
         acc[r] = x
 
-    shard_products(lk_ref, lr_ref, lm, rv, 0, J, half, TI, store)
+    shard_products(lk_ref, lr_ref, lm, lambda r: rv[r], 4, J, half, TI, store)
     home = col == row // 2
-    for u, ref in enumerate((a_ref, b_ref)):
-        late = acc[:, u * TI : (u + 1) * TI]
-        early = ref[...]
-        outs[u][...] = jnp.where(home, late, early)
-        outs[2 + u][...] = jnp.where(home, early, late)
-
-
-def split_call(kernel, shards, sems, n_out, pos, lk, lr, extra, slots, J, n):
+    count = acc.shape[0]
+    for k, ref in enumerate((a_ref, b_ref)):
+        late = acc[:, k * TI : (k + 1) * TI]
+        early = ref[u * count : (u + 1) * count]
+        outs[k][...] = jnp.where(home, late, early)
+        outs[2 + k][...] = jnp.where(home, early, late)
+
+
+def products(kernel, right_shape, acc_shape, sems, n_out, pos, lk, lr, extra, slots, J, n):
     half, TI, _ = lk.shape
     parts, main = packing(half, J)
-    rows = packing(half // 2, 4 * TI)[1]
     bf = jnp.bfloat16
-    acc = (rows, 2 * TI, LANES)
+    rows = acc_shape[-3]
     return pl.pallas_call(
         functools.partial(kernel, J, n),
         out_shape=[jax.ShapeDtypeStruct((rows, TI, LANES), bf)] * n_out,
         in_specs=[smem(), vmem(), vmem()] + [vmem()] * len(extra) + [pl.BlockSpec(memory_space=pl.ANY)] * len(slots),
         out_specs=[vmem()] * n_out,
         scratch_shapes=[
-            pltpu.VMEM((shards, 2, main, TI, LANES), bf),
+            pltpu.VMEM(right_shape, bf),
             pltpu.VMEM(((half - main) * max(parts, 1), 2 * TI, LANES), bf),
-            pltpu.VMEM((shards,) + acc if shards > 1 else acc, bf),
+            pltpu.VMEM(acc_shape, bf),
             pltpu.SemaphoreType.DMA(sems),
         ],
-        compiler_params=grant(12 if shards > 1 else 6),
-        cost_estimate=pl.CostEstimate(flops=2 * shards * half * 48 * 48 * 512, bytes_accessed=shards * 2 * main * TI * LANES * 4, transcendentals=0),
+        compiler_params=grant(12 if len(right_shape) > 3 else 6),
+        cost_estimate=pl.CostEstimate(flops=half * TI * TI * J * 4, bytes_accessed=main * TI * LANES * 16, transcendentals=0),
     )(pos, lk, lr, *extra, *slots)
 
 
-def add_group(C, TI, own, other, sub, sc):
+def add_group(C, TI, own, other, sub, sc, quads):
     half = C // 2
     pairs = half // 2
     cols = 4 * TI
-    parts, main = packing(pairs, cols)
-    tails = pairs - main
     spare = LANES - cols
     lanes = lane_index((TI, LANES))
-    for refs, base in ((own, sub * pairs), (other, (1 - sub) * pairs)):
+
+    def total(refs, r):
+        x = refs[0][r].astype(jnp.float32) + refs[1][r].astype(jnp.float32)
+        return x.astype(jnp.bfloat16).astype(jnp.float32)
+
+    def unpack(count, rows):
+        parts, main = packing(count, cols)
+        if not parts:
+            return [rows(r) for r in range(count)]
+        tails = count - main
+        out = [rows(r) for r in range(main)]
+        for q in range(tails):
+            tail = jnp.zeros((TI, LANES), jnp.float32)
+            for t in range(parts):
+                part = (lanes >= spare * t) & (lanes < spare * (t + 1))
+                tail = jnp.where(part, pltpu.roll(out[t * tails + q], LANES - cols + spare * t, 1), tail)
+            out.append(tail)
+        return out
+
+    for k, (refs, base) in enumerate(((own, sub * pairs), (other, (1 - sub) * pairs))):
 
         def put(q, x, base=base):
             sc[pl.ds((base + q) * TI, TI), :] = x
 
-        def total(r, refs=refs):
-            x = refs[0][r].astype(jnp.float32) + refs[1][r].astype(jnp.float32)
-            return x.astype(jnp.bfloat16).astype(jnp.float32)
-
-        for q in range(tails if parts else 0):
-            tail = jnp.zeros((TI, LANES), jnp.float32)
-            for t in range(parts):
-                x = total(t * tails + q)
-                put(t * tails + q, x)
-                part = (lanes >= spare * t) & (lanes < spare * (t + 1))
-                tail = jnp.where(part, pltpu.roll(x, LANES - cols + spare * t, 1), tail)
-            put(main + q, tail)
-        for q in range(0 if parts else pairs):
-            put(q, total(q))
+        if not quads:
+            size = refs[0][0].shape[0]
+            for q, x in enumerate(unpack(pairs, lambda r, refs=refs: total(refs[r // size], r % size))):
+                put(q, x)
+        else:
+            swap = sub == (0 if k else 1)
+            left = lax.rem(lanes, 2 * TI) < TI
+            a, b = (unpack(pairs // 2, lambda r, refs=refs, u=u: total(refs[u], r)) for u in range(2))
+            for q in range(pairs // 2):
+                x = jnp.where(swap, b[q], a[q])
+                y = jnp.where(swap, a[q], b[q])
+                put(q, jnp.where(left, x, pltpu.roll(y, TI, 1)))
+                put(q + pairs // 2, jnp.where(left, pltpu.roll(x, LANES - TI, 1), y))
 
 
 def group_updates(C, TI, sc, nts, wx_ref, emit):
@@ -574,7 +587,7 @@
     TI, C, _ = mid_ref.shape
     span = 2 * TI
     first = lower_half_first(pos_ref)
-    add_group(C, TI, (a_ref, b_ref), (c_ref, d_ref), pos_ref[2], sc)
+    add_group(C, TI, [(a_ref, b_ref)], [(c_ref, d_ref)], pos_ref[2], sc, False)
 
     def emit(i, update):
         mid = mid_ref[i].astype(jnp.float32).T
@@ -588,10 +601,14 @@
     group_updates(C, TI, sc, nts, wx_ref, emit)
 
 
-def finish_late_kernel(pos_ref, a_ref, b_ref, c_ref, d_ref, early_ref, m_ref, g_ref, wx_ref, out_ref, sc, nts):
+def finish_late_kernel(pos_ref, *refs):
+    pieces, (early_ref, m_ref, g_ref, wx_ref, out_ref, sc, nts) = refs[:8], refs[8:]
     TI, span, C = early_ref.shape
     first = lower_half_first(pos_ref)
-    add_group(C, TI, (a_ref, b_ref), (c_ref, d_ref), pos_ref[2], sc)
+    home = pos_ref[1] == pos_ref[0] // 2
+    args = (C, TI, [pieces[0:2], pieces[2:4]], [pieces[4:6], pieces[6:8]], pos_ref[2], sc)
+    pl.when(home)(lambda: add_group(*args, False))
+    pl.when(jnp.logical_not(home))(lambda: add_group(*args, True))
 
     def emit(i, update):
         late = m_ref[i].astype(jnp.float32) + g_ref[i].astype(jnp.float32) * update
@@ -691,13 +708,21 @@
         last_in, last_out = [along(near[0], inner)], [along(mids[0], outward)]
         last_in, last_out = last_in + [along(near[1], inner)], last_out + [along(mids[1], outward)]
         far = [far_k, shift(far_s, "sub", 1)]
-        send1, send1o, keep1, keep1o, rest, resto = split_call(early_kernel, 3, (3, 2), 6, pos, lk, lr, [], [rk, rr, *near, *mids, *far], tile_cols, nr)
+        rows, pairs = rk.shape[0], packing(width // 4, 4 * tile_rows)[1]
+        shards = (3, 2, rows, tile_rows, LANES)
+        acc = (3, pairs, 2 * tile_rows, LANES)
+        send1, send1o, keep1, keep1o, rest, resto = products(early_kernel, shards, acc, (3, 2), 6, pos, lk, lr, [], [rk, rr, *near, *mids, *far], tile_cols, nr)
         got1, got1o, keep1o = shift(send1, "col", 1), across(send1o, 1), shift(keep1o, "sub", 1)
         group = (tile_rows, 2 * tile_rows, width)
         done1, mid2, gate2 = finish_group(finish_early_kernel, [group] * 3, width, tile_rows, pos, keep1, got1, keep1o, got1o, mid, gate, exit_matrix)
-        send2, send2o, keep2, keep2o = split_call(late_kernel, 1, (2,), 4, pos, lk, lr, [rest, resto], [*last_in, *last_out], tile_cols, nr)
-        got2, got2o, keep2o = shift(send2, "col", 1), across(send2o, 1), shift(keep2o, "sub", 1)
-        return finish_group(finish_late_kernel, [edge_activations.shape], width, tile_rows, pos, keep2, got2, keep2o, got2o, done1, mid2, gate2, exit_matrix)[0]
+        own, other = [], []
+        acc = (pairs // 2, 2 * tile_rows, LANES)
+        for u in range(2):
+            kernel = functools.partial(late_kernel, u)
+            send, sendo, keep, keepo = products(kernel, rk.shape, acc, (1,), 4, pos, lk, lr, [rest, resto], [last_in[u], last_out[u]], tile_cols, nr)
+            own += [keep, shift(send, "col", 1)]
+            other += [shift(keepo, "sub", 1), across(sendo, 1)]
+        return finish_group(finish_late_kernel, [edge_activations.shape], width, tile_rows, pos, *own, *other, done1, mid2, gate2, exit_matrix)[0]
 
     outer_weight, entry, exit_matrix = weights(tensor_product_matrix, multiplicative_entry_matrix, multiplicative_exit_matrix, fw)
     rows = jnp.stack([right] + [shift(right, "row", d) for d in range(1, nr)])

time: 86.8 us -> 88.2 us (1.016)
  Pallas kernels: 22.3 us -> 23.9 us
    ppermute x8, waiting for transfers between devices: 12.5 us -> 10.7 us  [along(): return lax.ppermute(x, 'row', pairs)]
    ppermute x11 -> x13, starting transfers between devices: 4.67 us -> 6.31 us  [shift(): return lax.ppermute(x, axis, [(i, (i + d) % n) for i in range(n)])]
    ppermute x2 -> x3, starting transfers between devices: 2.26 us -> 0.63 us  [across(): lax.ppermute(x, ('col', 'sub'), [(c * 2 + s, (c + d) % nc * 2 + 1 - s) fo...]
    pallas_call x2 -> x3, Pallas kernels: 5.37 us -> 6.94 us  [products(): pl.pallas_call(functools.partial(kernel, J, n), out_shape=[jax.ShapeDtype...]
    ppermute x2 -> x3, waiting for transfers between devices: 0.01 us -> 1.43 us  [across(): lax.ppermute(x, ('col', 'sub'), [(c * 2 + s, (c + d) % nc * 2 + 1 - s) fo...]
    ppermute x11 -> x13, waiting for transfers between devices: 8.13 us -> 7.92 us  [shift(): return lax.ppermute(x, axis, [(i, (i + d) % n) for i in range(n)])]
  transfers between devices with their start and end apart: 25 -> 28, of which waited for: 8 -> 11; matrix products, arithmetic and copies ran while one was open for 1% -> 1% of each run, Pallas kernels for 24% -> 25%
where the time goes in v3:
time: 88.2 us; the launch traced here: 86.7 us
  starting transfers between devices  37.3 us (42%)
  Pallas kernels  23.9 us (27%)
  waiting for transfers between devices  20.6 us (23%)
  other arithmetic  2.06 us (2%)
  local copies, waits for them, and re-layouts  1.92 us (2%)
    ppermute x8, starting transfers between devices, along(): return lax.ppermute(x, 'row', pairs)  18.9 us
    pallas_call x2, Pallas kernels, pair(): return f(pos, l, lr, rt, wt, e, went)  11.3 us
    ppermute x8, waiting for transfers between devices, along(): return lax.ppermute(x, 'row', pairs)  10.7 us
    ppermute x13, waiting for transfers between devices, shift(): return lax.ppermute(x, axis, [(i, (i + d) % n) for i in range(n)])  7.92 us
    pallas_call x3, Pallas kernels, products(): pl.pallas_call(functools.partial(kernel, J, n), out_shape=[jax.ShapeDtype...  6.94 us
    ppermute x13, starting transfers between devices, shift(): return lax.ppermute(x, axis, [(i, (i + d) % n) for i in range(n)])  6.31 us
    ppermute x3, starting transfers between devices, per_device(): lax.ppermute(x, 'row', [(i, i ^ d) for i in range(nr)])  5.99 us
    ppermute x1, starting transfers between devices, per_device(): lax.ppermute(edge_activations, 'row', [(0, nr - 1), (nr - 1, 0)])  5.5 us
  transfers between devices with their start and end apart: 28, of which 11 were waited for; matrix products, arithmetic and copies ran while one was open for 1% of the time, Pallas kernels for 25%

profile of v3, /device:TPU:0, one launch (start us, length us, event | category | flops | bytes accessed | tf_op | source)
XLA Modules:
  0.0 86.7 jit_solution(12404174304764176995)
XLA Ops:
  0.0 1.2 %convert_reduce_fusion = f32[16,48]{1,0:T(8,128)S(1)} fusion(bf16[16,48,256]{2,1,0:T(8,128)(2,1)} %param.7), kind=kLoop, calls=%fused_computation.3 | loop fusion | flops 392448 | bytes 396288 | tf_op jit(solution)/shard_map/reduce_sum | solution.py:21
  2.5 3.1 %collective-permute-start.2 = (bf16[16,1536]{1,0:T(8,128)(2,1)S(1)}, bf16[16,1536]{1,0:T(8,128)(2,1)S(1)}, u32[]{:S(2)}, u32[]{:S(2)}) collective-permute-start(bf16[16,1536]{1,0:T(8,128)(2,1)S(1)} %reshape.23), channel_id=1, source_target_pairs={{0,4},{4,0},{8,12},{12,8},{1,5},{5,1},{9,13},{13,9},{2,6},{6,2},{1... | collective-permute-start | bytes 147464 | tf_op jit(solution)/shard_map/ppermute | solution.py:679
  5.7 2.6 %collective-permute-start.3 = (bf16[16,1536]{1,0:T(8,128)(2,1)S(1)}, bf16[16,1536]{1,0:T(8,128)(2,1)S(1)}, u32[]{:S(2)}, u32[]{:S(2)}) collective-permute-start(bf16[16,1536]{1,0:T(8,128)(2,1)S(1)} %reshape.23), channel_id=1, source_target_pairs={{0,8},{4,12},{8,0},{12,4},{1,9},{5,13},{9,1},{13,5},{2,10},{6,14},... | collective-permute-start | bytes 147464 | tf_op jit(solution)/shard_map/ppermute | solution.py:679
  8.9 1.6 %collective-permute-start = (bf16[16,1536]{1,0:T(8,128)(2,1)S(1)}, bf16[16,1536]{1,0:T(8,128)(2,1)S(1)}, u32[]{:S(2)}, u32[]{:S(2)}) collective-permute-start(bf16[16,1536]{1,0:T(8,128)(2,1)S(1)} %reshape.22), channel_id=1, source_target_pairs={{0,2},{2,0},{1,3},{3,1},{4,6},{6,4},{5,7},{7,5},{8,10},{10,8},{9,1... | collective-permute-start | bytes 147464 | tf_op jit(solution)/shard_map/ppermute | solution.py:636
  11.1 5.5 %collective-permute-start.13 = (bf16[24,96,128]{2,1,0:T(8,128)(2,1)S(1)}, bf16[24,96,128]{2,1,0:T(8,128)(2,1)S(1)}, u32[]{:S(2)}, u32[]{:S(2)}) collective-permute-start(bf16[24,96,128]{2,1,0:T(8,128)(2,1)S(1)} %copy-done.4), channel_id=1, source_target_pairs={{0,12},{12,0},{1,13},{13,1},{2,14},{14,2},{3,15},{15,3},{16,28},{2... | collective-permute-start | bytes 1769480 | tf_op jit(solution)/shard_map/ppermute | solution.py:690
  16.7 0.7 copy-done.3
  18.5 0.6 collective-permute-start.4
  19.2 4.6 %collective-permute-done.4 = bf16[3,16,1536]{2,1,0:T(8,128)(2,1)S(1)} collective-permute-done((bf16[3,16,1536]{2,1,0:T(8,128)(2,1)S(1)}, bf16[3,16,1536]{2,1,0:T(8,128)(2,1)S(1)}, u32[]{:S(2)}, u32[]{:S(2)}) %collective-permute-start.4) | collective-permute-done | bytes 147488 | tf_op jit(solution)/shard_map/ppermute | solution.py:636
  24.6 0.7 collective-permute-done.6.recv_ref
  25.3 1.2 %shard_map.73.refs_2_ = bf16[32,96,64]{2,1,0:T(8,128)(2,1)S(1)} custom-call(bf16[2,2,16,1536]{3,2,1,0:T(8,128)(2,1)S(1)} %pad_maximum_fusion.1.own_ref, bf16[2,2,16,1536]{3,2,1,0:T(8,128)(2,1)S(1)} %collective-permute-done.6.recv_ref), custom_call_target="tpu_custom_call" | custom-call | tf_op jit(solution)/shard_map/pallas_call | solution.py:101
  26.5 6.4 %shard_map.75 = (bf16[24,128,96]{2,1,0:T(8,128)(2,1)S(1)}, bf16[24,128,96]{2,1,0:T(8,128)(2,1)S(1)}, bf16[64,24,128]{2,1,0:T(8,128)(2,1)S(1)}, bf16[64,24,128]{2...) custom-call(s32[3]{0:T(128)S(1)} %pad_add_fusion.pos_ref, ...), custom_call_target="tpu_custom_call" | custom-call | flops 1283457024 | bytes 7077888 | tf_op jit(solution)/shard_map/pallas_call | solution.py:229
  33.5 0.7 collective-permute-start.11
  34.2 13.6 %collective-permute-start.9 = (bf16[48,24,128]{2,1,0:T(8,128)(2,1)S(1)}, bf16[48,24,128]{2,1,0:T(8,128)(2,1)S(1)}, u32[]{:S(2)}, u32[]{:S(2)}) collective-permute-start(bf16[48,24,128]{2,1,0:T(8,128)(2,1)S(1)} %get-tuple-element.37.rest_0_), channel_id=1, source_target_pairs={{0,4},{4,0},{8,12},{12,8},{1,5},{5,1},{9,13},{13,9},{2,6},{6,2},{1... | collective-permute-start | bytes 884744 | tf_op jit(solution)/shard_map/ppermute | solution.py:701
  47.8 0.7 collective-permute-start.12
  48.5 4.9 %shard_map.76 = (bf16[48,24,128]{2,1,0:T(8,128)(2,1)S(1)}, bf16[48,24,128]{2,1,0:T(8,128)(2,1)S(1)}) custom-call(s32[3]{0:T(128)S(1)} %pad_add_fusion.pos_ref, bf16[2,32,768]{2,1,0:T(8,128)(2,1)S(1)} %get-tuple-element.66.refs_0_, bf16[2,32,768]{2,1,0:T(8,128)(2,1)S(1)} %collective-permute-done.5.refs_1_, bf16[32,96,64]{2,1,0:T(8,128)(2,1)S(1)} %shard_map.73.refs_2_, ...), custom_call_target="tpu_custom_call" | custom-call | flops 1283457024 | bytes 7077888 | tf_op jit(solution)/shard_map/pallas_call | solution.py:229
  53.6 2.1 %collective-permute-done.9.rest_2_ = bf16[48,24,128]{2,1,0:T(8,128)(2,1)S(1)} collective-permute-done((bf16[48,24,128]{2,1,0:T(8,128)(2,1)S(1)}, bf16[48,24,128]{2,1,0:T(8,128)(2,1)S(1)}, u32[]{:S(2)}, u32[]{:S(2)}) %collective-permute-start.9) | collective-permute-done | bytes 294944 | tf_op jit(solution)/shard_map/ppermute | solution.py:701
  55.6 0.7 collective-permute-start.15
  56.3 1.3 %collective-permute-start.16 = (bf16[48,24,128]{2,1,0:T(8,128)(2,1)S(1)}, bf16[48,24,128]{2,1,0:T(8,128)(2,1)S(1)}, u32[]{:S(2)}, u32[]{:S(2)}) collective-permute-start(bf16[48,24,128]{2,1,0:T(8,128)(2,1)S(1)} %collective-permute-done.11.rest_4_), channel_id=1, source_target_pairs={{4,0},{8,12},{5,1},{9,13},{6,2},{10,14},{7,3},{11,15},{20,16},{24,... | collective-permute-start | bytes 884744 | tf_op jit(solution)/shard_map/ppermute | solution.py:701
  57.6 3.8 %collective-permute-done.10.rest_3_ = bf16[48,24,128]{2,1,0:T(8,128)(2,1)S(1)} collective-permute-done((bf16[48,24,128]{2,1,0:T(8,128)(2,1)S(1)}, bf16[48,24,128]{2,1,0:T(8,128)(2,1)S(1)}, u32[]{:S(2)}, u32[]{:S(2)}) %collective-permute-start.10) | collective-permute-done | bytes 294944 | tf_op jit(solution)/shard_map/ppermute | solution.py:701
  61.4 0.7 collective-permute-start.18
  62.1 1.3 %collective-permute-start.19 = (bf16[48,24,128]{2,1,0:T(8,128)(2,1)S(1)}, bf16[48,24,128]{2,1,0:T(8,128)(2,1)S(1)}, u32[]{:S(2)}, u32[]{:S(2)}) collective-permute-start(bf16[48,24,128]{2,1,0:T(8,128)(2,1)S(1)} %collective-permute-done.12.rest_5_), channel_id=1, source_target_pairs={{4,0},{8,12},{5,1},{9,13},{6,2},{10,14},{7,3},{11,15},{20,16},{24,... | collective-permute-start | bytes 884744 | tf_op jit(solution)/shard_map/ppermute | solution.py:701
  63.4 3.5 %shard_map.77 = (bf16[24,24,128]{2,1,0:T(8,128)(2,1)S(1)}, bf16[24,24,128]{2,1,0:T(8,128)(2,1)S(1)}, bf16[24,24,128]{2,1,0:T(8,128)(2,1)S(1)}, bf16[24,24,128]{2...) custom-call(s32[3]{0:T(128)S(1)} %pad_add_fusion.pos_ref, ...), custom_call_target="tpu_custom_call" | custom-call | flops 14155776 | bytes 2359296 | tf_op jit(solution)/shard_map/pallas_call | solution.py:499
  66.9 0.6 collective-permute-start.25
  67.5 1.7 %collective-permute-done.16.outward = bf16[48,24,128]{2,1,0:T(8,128)(2,1)S(1)} collective-permute-done((bf16[48,24,128]{2,1,0:T(8,128)(2,1)S(1)}, bf16[48,24,128]{2,1,0:T(8,128)(2,1)S(1)}, u32[]{:S(2)}, u32[]{:S(2)}) %collective-permute-start.16) | collective-permute-done | bytes 294944 | tf_op jit(solution)/shard_map/ppermute | solution.py:701
  69.2 1.7 %shard_map.78 = (bf16[12,24,128]{2,1,0:T(8,128)(2,1)S(1)}, bf16[12,24,128]{2,1,0:T(8,128)(2,1)S(1)}, bf16[12,24,128]{2,1,0:T(8,128)(2,1)S(1)}, bf16[12,24,128]{2,1,0:T(8,128)(2,1)S(1)}) custom-call(s32[3]{0:T(128)S(1)} %pad_add_fusion.pos_ref, bf16[64,24,128]{2,1,0:T(8,128)(2,1)S(1)} %get-tuple-element.35.lk_ref, ...), custom_call_target="tpu_custom_call" | custom-call | flops 14155776 | bytes 2359296 | tf_op jit(solution)/shard_map/pallas_call | solution.py:499
  71.5 3.2 %collective-permute-done.19.outward = bf16[48,24,128]{2,1,0:T(8,128)(2,1)S(1)} collective-permute-done((bf16[48,24,128]{2,1,0:T(8,128)(2,1)S(1)}, bf16[48,24,128]{2,1,0:T(8,128)(2,1)S(1)}, u32[]{:S(2)}, u32[]{:S(2)}) %collective-permute-start.19) | collective-permute-done | bytes 294944 | tf_op jit(solution)/shard_map/ppermute | solution.py:701
  74.7 1.7 %shard_map.79 = (bf16[12,24,128]{2,1,0:T(8,128)(2,1)S(1)}, bf16[12,24,128]{2,1,0:T(8,128)(2,1)S(1)}, bf16[12,24,128]{2,1,0:T(8,128)(2,1)S(1)}, bf16[12,24,128]{2,1,0:T(8,128)(2,1)S(1)}) custom-call(s32[3]{0:T(128)S(1)} %pad_add_fusion.pos_ref, bf16[64,24,128]{2,1,0:T(8,128)(2,1)S(1)} %get-tuple-element.35.lk_ref, ...), custom_call_target="tpu_custom_call" | custom-call | flops 14155776 | bytes 2359296 | tf_op jit(solution)/shard_map/pallas_call | solution.py:499
  77.2 1.5 %collective-permute-start.20 = (bf16[12,24,128]{2,1,0:T(8,128)(2,1)S(1)}, bf16[12,24,128]{2,1,0:T(8,128)(2,1)S(1)}, u32[]{:S(2)}, u32[]{:S(2)}) collective-permute-start(bf16[12,24,128]{2,1,0:T(8,128)(2,1)S(1)} %get-tuple-element.46), channel_id=1, source_target_pairs={{0,2},{2,0},{1,3},{3,1},{4,6},{6,4},{5,7},{7,5},{8,10},{10,8},{9,1... | collective-permute-start | bytes 221192 | tf_op jit(solution)/shard_map/ppermute | solution.py:636
  79.3 1.7 %shard_map.80 = (bf16[24,48,128]{2,1,0:T(8,128)(2,1)S(1)}, bf16[24,48,128]{2,1,0:T(8,128)(2,1)S(1)}, bf16[24,48,128]{2,1,0:T(8,128)(2,1)S(1)}) custom-call(s32[3]{0:T(128)S(1)} %pad_add_fusion.pos_ref, bf16[24,24,128]{2,1,0:T(8,128)(2,1)S(1)} %get-tuple-element.51.a_ref, bf16[24,24,128]{2,1,0:T(8,128)(2,1)S(1)} %collective-permute-done.25.b_ref, ...), custom_call_target="tpu_custom_call" | custom-call | flops 37748736 | bytes 1474560 | tf_op jit(solution)/shard_map/pallas_call | solution.py:623
  81.4 2.0 %collective-permute-done.20.refs_3_ = bf16[12,24,128]{2,1,0:T(8,128)(2,1)S(1)} collective-permute-done((bf16[12,24,128]{2,1,0:T(8,128)(2,1)S(1)}, bf16[12,24,128]{2,1,0:T(8,128)(2,1)S(1)}, u32[]{:S(2)}, u32[]{:S(2)}) %collective-permute-start.20) | collective-permute-done | bytes 73760 | tf_op jit(solution)/shard_map/ppermute | solution.py:636
  83.4 1.2 %collective-permute-done.24.refs_7_ = bf16[12,24,128]{2,1,0:T(8,128)(2,1)S(1)} collective-permute-done((bf16[12,24,128]{2,1,0:T(8,128)(2,1)S(1)}, bf16[12,24,128]{2,1,0:T(8,128)(2,1)S(1)}, u32[]{:S(2)}, u32[]{:S(2)}) %collective-permute-start.24) | collective-permute-done | bytes 73760 | tf_op jit(solution)/shard_map/ppermute | solution.py:646
  84.5 2.2 %shard_map.81 = bf16[24,96,128]{2,1,0:T(8,128)(2,1)} custom-call(s32[3]{0:T(128)S(1)} %pad_add_fusion.pos_ref, bf16[12,24,128]{2,1,0:T(8,128)(2,1)S(1)} %get-tuple-element.43.refs_0_, bf16[12,24,128]{2,1,0:T(8,128)(2,1)S(1)} %collective-permute-done.17.refs_1_, bf16[12,24,128]{2,1,0:T(8,128)(2,1)S(1)} %get-tuple-element.45.refs_2_, ...), custom_call_target="tpu_custom_call" | custom-call | flops 37748736 | bytes 1474560 | tf_op jit(solution)/shard_map/pallas_call | solution.py:623
  (73 shorter events, 7.4 us)
Async XLA Ops:
  2.3 5.9 %copy-start.6 = (bf16[256,32]{0,1:T(8,128)(2,1)S(1)}, bf16[256,32]{0,1:T(8,128)(2,1)}, u32[]{:S(2)}) copy-start(bf16[256,32]{0,1:T(8,128)(2,1)} %param.9) | copy-start | bytes 49156
  2.5 15.9 %collective-permute-start.2 = (bf16[16,1536]{1,0:T(8,128)(2,1)S(1)}, bf16[16,1536]{1,0:T(8,128)(2,1)S(1)}, u32[]{:S(2)}, u32[]{:S(2)}) collective-permute-start(bf16[16,1536]{1,0:T(8,128)(2,1)S(1)} %reshape.23), channel_id=1, source_target_pairs={{0,4},{4,0},{8,12},{12,8},{1,5},{5,1},{9,13},{13,9},{2,6},{6,2},{1... | collective-permute-start | bytes 147464 | tf_op jit(solution)/shard_map/ppermute | solution.py:679
  5.7 12.8 %collective-permute-start.3 = (bf16[16,1536]{1,0:T(8,128)(2,1)S(1)}, bf16[16,1536]{1,0:T(8,128)(2,1)S(1)}, u32[]{:S(2)}, u32[]{:S(2)}) collective-permute-start(bf16[16,1536]{1,0:T(8,128)(2,1)S(1)} %reshape.23), channel_id=1, source_target_pairs={{0,8},{4,12},{8,0},{12,4},{1,9},{5,13},{9,1},{13,5},{2,10},{6,14},... | collective-permute-start | bytes 147464 | tf_op jit(solution)/shard_map/ppermute | solution.py:679
  8.5 2.7 %copy-start.4 = (bf16[24,96,128]{2,1,0:T(8,128)(2,1)S(1)}, bf16[24,96,128]{2,1,0:T(8,128)(2,1)}, u32[]{:S(2)}) copy-start(bf16[24,96,128]{2,1,0:T(8,128)(2,1)} %refs_4_.1) | copy-start | bytes 1769476
  8.9 9.0 %collective-permute-start = (bf16[16,1536]{1,0:T(8,128)(2,1)S(1)}, bf16[16,1536]{1,0:T(8,128)(2,1)S(1)}, u32[]{:S(2)}, u32[]{:S(2)}) collective-permute-start(bf16[16,1536]{1,0:T(8,128)(2,1)S(1)} %reshape.22), channel_id=1, source_target_pairs={{0,2},{2,0},{1,3},{3,1},{4,6},{6,4},{5,7},{7,5},{8,10},{10,8},{9,1... | collective-permute-start | bytes 147464 | tf_op jit(solution)/shard_map/ppermute | solution.py:636
  10.6 6.1 %copy-start.1 = (bf16[1024,128]{1,0:T(8,128)(2,1)S(1)}, bf16[1024,128]{1,0:T(8,128)(2,1)}, u32[]{:S(2)}) copy-start(bf16[1024,128]{1,0:T(8,128)(2,1)} %w_ref.1) | copy-start | bytes 786436
  10.8 5.9 %copy-start.2 = (bf16[128,640]{1,0:T(8,128)(2,1)S(1)}, bf16[128,640]{1,0:T(8,128)(2,1)}, u32[]{:S(2)}) copy-start(bf16[128,640]{1,0:T(8,128)(2,1)} %n_ref.1) | copy-start | bytes 491524
  10.8 7.6 %collective-permute-start.1 = (bf16[2,16,1536]{2,1,0:T(8,128)(2,1)S(1)}, bf16[2,16,1536]{2,1,0:T(8,128)(2,1)S(1)}, u32[]{:S(2)}, u32[]{:S(2)}) collective-permute-start(bf16[2,16,1536]{2,1,0:T(8,128)(2,1)S(1)} %pad_maximum_fusion.3), channel_id=1, source_target_pairs={{0,12},{4,8},{8,4},{12,0},{1,13},{5,9},{9,5},{13,1},{2,14},{6,10},... | collective-permute-start | bytes 294920 | tf_op jit(solution)/shard_map/ppermute | solution.py:679
  11.1 36.7 %collective-permute-start.13 = (bf16[24,96,128]{2,1,0:T(8,128)(2,1)S(1)}, bf16[24,96,128]{2,1,0:T(8,128)(2,1)S(1)}, u32[]{:S(2)}, u32[]{:S(2)}) collective-permute-start(bf16[24,96,128]{2,1,0:T(8,128)(2,1)S(1)} %copy-done.4), channel_id=1, source_target_pairs={{0,12},{12,0},{1,13},{13,1},{2,14},{14,2},{3,15},{15,3},{16,28},{2... | collective-permute-start | bytes 1769480 | tf_op jit(solution)/shard_map/ppermute | solution.py:690
  18.5 5.2 %collective-permute-start.4 = (bf16[3,16,1536]{2,1,0:T(8,128)(2,1)S(1)}, bf16[3,16,1536]{2,1,0:T(8,128)(2,1)S(1)}, u32[]{:S(2)}, u32[]{:S(2)}) collective-permute-start(bf16[3,16,1536]{2,1,0:T(8,128)(2,1)S(1)} %pad_maximum_fusion.2), channel_id=1, source_target_pairs={{0,2},{2,0},{1,3},{3,1},{4,6},{6,4},{5,7},{7,5},{8,10},{10,8},{9,1... | collective-permute-start | bytes 442376 | tf_op jit(solution)/shard_map/ppermute | solution.py:636
  23.8 1.5 %collective-permute-start.6 = (bf16[2,2,16,1536]{3,2,1,0:T(8,128)(2,1)S(1)}, bf16[2,2,16,1536]{3,2,1,0:T(8,128)(2,1)S(1)}, u32[]{:S(2)}, u32[]{:S(2)}) collective-permute-start(bf16[2,2,16,1536]{3,2,1,0:T(8,128)(2,1)S(1)} %pad_maximum_fusion.1.own_ref), channel_id=1, source_target_pairs={{0,1},{1,0},{2,3},{3,2},{4,5},{5,4},{6,7},{7,6},{8,9},{9,8},{10,11... | collective-permute-start | bytes 589832 | tf_op jit(solution)/shard_map/ppermute | solution.py:636
  23.9 2.6 %collective-permute-start.5 = (bf16[2,32,768]{2,1,0:T(8,128)(2,1)S(1)}, bf16[2,32,768]{2,1,0:T(8,128)(2,1)S(1)}, u32[]{:S(2)}, u32[]{:S(2)}) collective-permute-start(bf16[2,32,768]{2,1,0:T(8,128)(2,1)S(1)} %get-tuple-element.65), channel_id=1, source_target_pairs={{0,1},{1,0},{2,3},{3,2},{4,5},{5,4},{6,7},{7,6},{8,9},{9,8},{10,11... | collective-permute-start | bytes 294920 | tf_op jit(solution)/shard_map/ppermute | solution.py:636
  32.9 14.8 %collective-permute-start.8 = (bf16[48,24,128]{2,1,0:T(8,128)(2,1)S(1)}, bf16[48,24,128]{2,1,0:T(8,128)(2,1)S(1)}, u32[]{:S(2)}, u32[]{:S(2)}) collective-permute-start(bf16[48,24,128]{2,1,0:T(8,128)(2,1)S(1)} %get-tuple-element.38), channel_id=1, source_target_pairs={{0,1},{1,0},{2,3},{3,2},{4,5},{5,4},{6,7},{7,6},{8,9},{9,8},{10,11... | collective-permute-start | bytes 884744 | tf_op jit(solution)/shard_map/ppermute | solution.py:636
  33.1 23.2 %collective-permute-start.7 = (bf16[64,24,128]{2,1,0:T(8,128)(2,1)S(1)}, bf16[64,24,128]{2,1,0:T(8,128)(2,1)S(1)}, u32[]{:S(2)}, u32[]{:S(2)}) collective-permute-start(bf16[64,24,128]{2,1,0:T(8,128)(2,1)S(1)} %get-tuple-element.36), channel_id=1, source_target_pairs={{0,1},{1,0},{2,3},{3,2},{4,5},{5,4},{6,7},{7,6},{8,9},{9,8},{10,11... | collective-permute-start | bytes 1179656 | tf_op jit(solution)/shard_map/ppermute | solution.py:636
  33.5 20.0 %collective-permute-start.11 = (bf16[48,24,128]{2,1,0:T(8,128)(2,1)S(1)}, bf16[48,24,128]{2,1,0:T(8,128)(2,1)S(1)}, u32[]{:S(2)}, u32[]{:S(2)}) collective-permute-start(bf16[48,24,128]{2,1,0:T(8,128)(2,1)S(1)} %get-tuple-element.37.rest_0_), channel_id=1, source_target_pairs={{4,8},{8,4},{5,9},{9,5},{6,10},{10,6},{7,11},{11,7},{20,24},{24,20... | collective-permute-start | bytes 884744 | tf_op jit(solution)/shard_map/ppermute | solution.py:701
  34.2 21.4 %collective-permute-start.9 = (bf16[48,24,128]{2,1,0:T(8,128)(2,1)S(1)}, bf16[48,24,128]{2,1,0:T(8,128)(2,1)S(1)}, u32[]{:S(2)}, u32[]{:S(2)}) collective-permute-start(bf16[48,24,128]{2,1,0:T(8,128)(2,1)S(1)} %get-tuple-element.37.rest_0_), channel_id=1, source_target_pairs={{0,4},{4,0},{8,12},{12,8},{1,5},{5,1},{9,13},{13,9},{2,6},{6,2},{1... | collective-permute-start | bytes 884744 | tf_op jit(solution)/shard_map/ppermute | solution.py:701
  47.7 13.6 %collective-permute-start.10 = (bf16[48,24,128]{2,1,0:T(8,128)(2,1)S(1)}, bf16[48,24,128]{2,1,0:T(8,128)(2,1)S(1)}, u32[]{:S(2)}, u32[]{:S(2)}) collective-permute-start(bf16[48,24,128]{2,1,0:T(8,128)(2,1)S(1)} %collective-permute-done.8.rest_1_), channel_id=1, source_target_pairs={{0,4},{4,0},{8,12},{12,8},{1,5},{5,1},{9,13},{13,9},{2,6},{6,2},{1... | collective-permute-start | bytes 884744 | tf_op jit(solution)/shard_map/ppermute | solution.py:701
  47.8 14.2 %collective-permute-start.12 = (bf16[48,24,128]{2,1,0:T(8,128)(2,1)S(1)}, bf16[48,24,128]{2,1,0:T(8,128)(2,1)S(1)}, u32[]{:S(2)}, u32[]{:S(2)}) collective-permute-start(bf16[48,24,128]{2,1,0:T(8,128)(2,1)S(1)} %collective-permute-done.8.rest_1_), channel_id=1, source_target_pairs={{4,8},{8,4},{5,9},{9,5},{6,10},{10,6},{7,11},{11,7},{20,24},{24,20... | collective-permute-start | bytes 884744 | tf_op jit(solution)/shard_map/ppermute | solution.py:701
  53.5 9.9 %collective-permute-start.14 = (bf16[48,24,128]{2,1,0:T(8,128)(2,1)S(1)}, bf16[48,24,128]{2,1,0:T(8,128)(2,1)S(1)}, u32[]{:S(2)}, u32[]{:S(2)}) collective-permute-start(bf16[48,24,128]{2,1,0:T(8,128)(2,1)S(1)} %get-tuple-element.40), channel_id=1, source_target_pairs={{0,1},{1,0},{2,3},{3,2},{4,5},{5,4},{6,7},{7,6},{8,9},{9,8},{10,11... | collective-permute-start | bytes 884744 | tf_op jit(solution)/shard_map/ppermute | solution.py:636
  55.6 11.9 %collective-permute-start.15 = (bf16[48,24,128]{2,1,0:T(8,128)(2,1)S(1)}, bf16[48,24,128]{2,1,0:T(8,128)(2,1)S(1)}, u32[]{:S(2)}, u32[]{:S(2)}) collective-permute-start(bf16[48,24,128]{2,1,0:T(8,128)(2,1)S(1)} %collective-permute-done.9.rest_2_), channel_id=1, source_target_pairs={{4,8},{8,4},{5,9},{9,5},{6,10},{10,6},{7,11},{11,7},{20,24},{24,20... | collective-permute-start | bytes 884744 | tf_op jit(solution)/shard_map/ppermute | solution.py:701
  56.3 12.9 %collective-permute-start.16 = (bf16[48,24,128]{2,1,0:T(8,128)(2,1)S(1)}, bf16[48,24,128]{2,1,0:T(8,128)(2,1)S(1)}, u32[]{:S(2)}, u32[]{:S(2)}) collective-permute-start(bf16[48,24,128]{2,1,0:T(8,128)(2,1)S(1)} %collective-permute-done.11.rest_4_), channel_id=1, source_target_pairs={{4,0},{8,12},{5,1},{9,13},{6,2},{10,14},{7,3},{11,15},{20,16},{24,... | collective-permute-start | bytes 884744 | tf_op jit(solution)/shard_map/ppermute | solution.py:701
  61.4 9.6 %collective-permute-start.18 = (bf16[48,24,128]{2,1,0:T(8,128)(2,1)S(1)}, bf16[48,24,128]{2,1,0:T(8,128)(2,1)S(1)}, u32[]{:S(2)}, u32[]{:S(2)}) collective-permute-start(bf16[48,24,128]{2,1,0:T(8,128)(2,1)S(1)} %collective-permute-done.10.rest_3_), channel_id=1, source_target_pairs={{4,8},{8,4},{5,9},{9,5},{6,10},{10,6},{7,11},{11,7},{20,24},{24,20... | collective-permute-start | bytes 884744 | tf_op jit(solution)/shard_map/ppermute | solution.py:701
  62.1 12.7 %collective-permute-start.19 = (bf16[48,24,128]{2,1,0:T(8,128)(2,1)S(1)}, bf16[48,24,128]{2,1,0:T(8,128)(2,1)S(1)}, u32[]{:S(2)}, u32[]{:S(2)}) collective-permute-start(bf16[48,24,128]{2,1,0:T(8,128)(2,1)S(1)} %collective-permute-done.12.rest_5_), channel_id=1, source_target_pairs={{4,0},{8,12},{5,1},{9,13},{6,2},{10,14},{7,3},{11,15},{20,16},{24,... | collective-permute-start | bytes 884744 | tf_op jit(solution)/shard_map/ppermute | solution.py:701
  66.9 10.3 %collective-permute-start.25 = (bf16[24,24,128]{2,1,0:T(8,128)(2,1)S(1)}, bf16[24,24,128]{2,1,0:T(8,128)(2,1)S(1)}, u32[]{:S(2)}, u32[]{:S(2)}) collective-permute-start(bf16[24,24,128]{2,1,0:T(8,128)(2,1)S(1)} %get-tuple-element.52), channel_id=1, source_target_pairs={{0,2},{2,0},{1,3},{3,1},{4,6},{6,4},{5,7},{7,5},{8,10},{10,8},{9,1... | collective-permute-start | bytes 442376 | tf_op jit(solution)/shard_map/ppermute | solution.py:636
  67.5 11.2 %collective-permute-start.26 = (bf16[24,24,128]{2,1,0:T(8,128)(2,1)S(1)}, bf16[24,24,128]{2,1,0:T(8,128)(2,1)S(1)}, u32[]{:S(2)}, u32[]{:S(2)}) collective-permute-start(bf16[24,24,128]{2,1,0:T(8,128)(2,1)S(1)} %get-tuple-element.53), channel_id=1, source_target_pairs={{0,1},{1,0},{2,3},{3,2},{4,5},{5,4},{6,7},{7,6},{8,9},{9,8},{10,11... | collective-permute-start | bytes 442376 | tf_op jit(solution)/shard_map/ppermute | solution.py:636
  69.2 9.7 %collective-permute-start.27 = (bf16[24,24,128]{2,1,0:T(8,128)(2,1)S(1)}, bf16[24,24,128]{2,1,0:T(8,128)(2,1)S(1)}, u32[]{:S(2)}, u32[]{:S(2)}) collective-permute-start(bf16[24,24,128]{2,1,0:T(8,128)(2,1)S(1)} %get-tuple-element.54), channel_id=1, source_target_pairs={{0,3},{1,2},{2,1},{3,0},{4,7},{5,6},{6,5},{7,4},{8,11},{9,10},{10,... | collective-permute-start | bytes 442376 | tf_op jit(solution)/shard_map/ppermute | solution.py:646
  71.0 6.1 %collective-permute-start.17 = (bf16[12,24,128]{2,1,0:T(8,128)(2,1)S(1)}, bf16[12,24,128]{2,1,0:T(8,128)(2,1)S(1)}, u32[]{:S(2)}, u32[]{:S(2)}) collective-permute-start(bf16[12,24,128]{2,1,0:T(8,128)(2,1)S(1)} %get-tuple-element.44), channel_id=1, source_target_pairs={{0,2},{2,0},{1,3},{3,1},{4,6},{6,4},{5,7},{7,5},{8,10},{10,8},{9,1... | collective-permute-start | bytes 221192 | tf_op jit(solution)/shard_map/ppermute | solution.py:636
  74.7 6.4 %collective-permute-start.21 = (bf16[12,24,128]{2,1,0:T(8,128)(2,1)S(1)}, bf16[12,24,128]{2,1,0:T(8,128)(2,1)S(1)}, u32[]{:S(2)}, u32[]{:S(2)}) collective-permute-start(bf16[12,24,128]{2,1,0:T(8,128)(2,1)S(1)} %get-tuple-element.47), channel_id=1, source_target_pairs={{0,1},{1,0},{2,3},{3,2},{4,5},{5,4},{6,7},{7,6},{8,9},{9,8},{10,11... | collective-permute-start | bytes 221192 | tf_op jit(solution)/shard_map/ppermute | solution.py:636
  77.0 4.4 %collective-permute-start.22 = (bf16[12,24,128]{2,1,0:T(8,128)(2,1)S(1)}, bf16[12,24,128]{2,1,0:T(8,128)(2,1)S(1)}, u32[]{:S(2)}, u32[]{:S(2)}) collective-permute-start(bf16[12,24,128]{2,1,0:T(8,128)(2,1)S(1)} %get-tuple-element.48), channel_id=1, source_target_pairs={{0,3},{1,2},{2,1},{3,0},{4,7},{5,6},{6,5},{7,4},{8,11},{9,10},{10,... | collective-permute-start | bytes 221192 | tf_op jit(solution)/shard_map/ppermute | solution.py:646
  77.2 6.2 %collective-permute-start.20 = (bf16[12,24,128]{2,1,0:T(8,128)(2,1)S(1)}, bf16[12,24,128]{2,1,0:T(8,128)(2,1)S(1)}, u32[]{:S(2)}, u32[]{:S(2)}) collective-permute-start(bf16[12,24,128]{2,1,0:T(8,128)(2,1)S(1)} %get-tuple-element.46), channel_id=1, source_target_pairs={{0,2},{2,0},{1,3},{3,1},{4,6},{6,4},{5,7},{7,5},{8,10},{10,8},{9,1... | collective-permute-start | bytes 221192 | tf_op jit(solution)/shard_map/ppermute | solution.py:636
  78.7 4.7 %collective-permute-start.23 = (bf16[12,24,128]{2,1,0:T(8,128)(2,1)S(1)}, bf16[12,24,128]{2,1,0:T(8,128)(2,1)S(1)}, u32[]{:S(2)}, u32[]{:S(2)}) collective-permute-start(bf16[12,24,128]{2,1,0:T(8,128)(2,1)S(1)} %get-tuple-element.49), channel_id=1, source_target_pairs={{0,1},{1,0},{2,3},{3,2},{4,5},{5,4},{6,7},{7,6},{8,9},{9,8},{10,11... | collective-permute-start | bytes 221192 | tf_op jit(solution)/shard_map/ppermute | solution.py:636
  78.9 5.6 %collective-permute-start.24 = (bf16[12,24,128]{2,1,0:T(8,128)(2,1)S(1)}, bf16[12,24,128]{2,1,0:T(8,128)(2,1)S(1)}, u32[]{:S(2)}, u32[]{:S(2)}) collective-permute-start(bf16[12,24,128]{2,1,0:T(8,128)(2,1)S(1)} %get-tuple-element.50), channel_id=1, source_target_pairs={{0,3},{1,2},{2,1},{3,0},{4,7},{5,6},{6,5},{7,4},{8,11},{9,10},{10,... | collective-permute-start | bytes 221192 | tf_op jit(solution)/shard_map/ppermute | solution.py:646
  (3 other events, 3.9 us)

commit v4 on v3

--- a/solution.py
+++ b/solution.py
@@ -48,6 +48,27 @@
 
 def lane_index(shape):
     return lax.broadcasted_iota(jnp.int32, shape, len(shape) - 1)
+
+
+def factors_kernel(x_ref, first_ref, second_ref, left_ref, right_ref):
+    rows = x_ref.shape[0]
+    step = rows // 8 if rows % 128 == 0 else rows
+    for t in range(rows // step):
+        part = slice(t * step, (t + 1) * step)
+        normed = standardize_features(x_ref[part, :].astype(jnp.float32)).astype(jnp.bfloat16)
+        right_ref[part, :] = jnp.dot(normed, second_ref[...], preferred_element_type=jnp.float32).astype(jnp.bfloat16)
+        left_ref[part, :] = jnp.dot(normed, first_ref[...], preferred_element_type=jnp.float32).astype(jnp.bfloat16)
+
+
+def factors(x, first, second):
+    shape = jax.ShapeDtypeStruct((x.shape[0], first.shape[1]), jnp.bfloat16)
+    return pl.pallas_call(
+        factors_kernel,
+        out_shape=[shape, shape],
+        in_specs=[vmem()] * 3,
+        out_specs=[vmem()] * 2,
+        compiler_params=grant(6),
+    )(x, first, second)
 
 
 def weights_kernel(fw, w_ref, n_ref, x_ref, wt_ref, nt_ref, xt_ref, sc, st):
@@ -665,18 +686,16 @@
     sub_id = pos[2:]
     m = tile_cols // residues
 
-    normed = standardize_features(homolog_activations.astype(jnp.float32)).astype(jnp.bfloat16).reshape(seqs * residues, features)
-
-    def project(matrix):
-        return jnp.dot(normed, matrix, preferred_element_type=jnp.float32).astype(jnp.bfloat16).reshape(seqs, residues * fw)
-
-    right = project(second_projection_matrix)
-    left = project(first_projection_matrix)
-
+    left, right = (
+        x.reshape(seqs, residues * fw)
+        for x in factors(homolog_activations.reshape(seqs * residues, features), first_projection_matrix, second_projection_matrix)
+    )
     span = tile_rows * fw
     fast = nr == 4 and nc == 2
     if fast:
-        hops = [lax.ppermute(x, "row", [(i, i ^ d) for i in range(nr)]) for d, x in ((3, jnp.stack([right, left])), (2, right), (1, right))]
+        hops = []
+        for d, x in ((3, jnp.stack([right, left])), (2, right), (1, right)):
+            hops.append(lax.ppermute(x, "row", [(i, i ^ d) for i in range(nr)]))
         left_x = shift(left, "col", 1)
         outer_weight, entry, exit_matrix = weights(tensor_product_matrix, multiplicative_entry_matrix, multiplicative_exit_matrix, fw)
         rows = jnp.stack([right, hops[2], hops[1], hops[0][0]])

time: 88.2 us -> 88.2 us (level)
  other arithmetic: 2.06 us -> 0.21 us
  local copies, waits for them, and re-layouts: 1.92 us -> 3.49 us
    unnamed x14, local copies, waits for them, and re-layouts: 0.73 us -> 2.68 us
    reduce_sum x2 -> x0, other arithmetic: 1.57 us -> none  [the longest x1 1.24 us: standardize_features(): centred = values - jnp.mean(values, axis=-1, keepdims=True)]
where the time goes in v4:
time: 88.2 us; the launch traced here: 86.7 us
  starting transfers between devices  37.2 us (42%)
  Pallas kernels  24.6 us (28%)
  waiting for transfers between devices  20.7 us (23%)
  local copies, waits for them, and re-layouts  3.49 us (4%)
    ppermute x8, starting transfers between devices, along(): return lax.ppermute(x, 'row', pairs)  18.8 us
    pallas_call x2, Pallas kernels, pair(): return f(pos, l, lr, rt, wt, e, went)  11.3 us
    ppermute x8, waiting for transfers between devices, along(): return lax.ppermute(x, 'row', pairs)  10.8 us
    ppermute x13, waiting for transfers between devices, shift(): return lax.ppermute(x, axis, [(i, (i + d) % n) for i in range(n)])  7.92 us
    pallas_call x3, Pallas kernels, products(): pl.pallas_call(functools.partial(kernel, J, n), out_shape=[jax.ShapeDtype...  6.94 us
    ppermute x13, starting transfers between devices, shift(): return lax.ppermute(x, axis, [(i, (i + d) % n) for i in range(n)])  6.31 us
    ppermute x3, starting transfers between devices, per_device(): hops.append(lax.ppermute(x, 'row', [(i, i ^ d) for i in range(nr)]))  5.99 us
    ppermute x1, starting transfers between devices, per_device(): lax.ppermute(edge_activations, 'row', [(0, nr - 1), (nr - 1, 0)])  5.5 us
  transfers between devices with their start and end apart: 28, of which 11 were waited for; matrix products, arithmetic and copies ran while one was open for 1% of the time, Pallas kernels for 25%

profile of v4, /device:TPU:0, one launch (start us, length us, event | category | flops | bytes accessed | tf_op | source)
XLA Modules:
  0.0 86.7 jit_solution(17044696022504952407)
XLA Ops:
  0.0 0.8 copy.10.first_ref
  1.0 1.0 %copy-done = bf16[16,48,256]{2,1,0:T(8,128)(2,1)S(1)} copy-done((bf16[16,48,256]{2,1,0:T(8,128)(2,1)S(1)}, bf16[16,48,256]{2,1,0:T(8,128)(2,1)}, u32[]{:S(2)}) %copy-start) | copy-done | bytes 393240
  2.0 0.7 shard_map.73
  2.9 3.1 %collective-permute-start.2 = (bf16[16,1536]{1,0:T(8,128)(2,1)S(1)}, bf16[16,1536]{1,0:T(8,128)(2,1)S(1)}, u32[]{:S(2)}, u32[]{:S(2)}) collective-permute-start(bf16[16,1536]{1,0:T(8,128)(2,1)S(1)} %reshape.11), channel_id=1, source_target_pairs={{0,4},{4,0},{8,12},{12,8},{1,5},{5,1},{9,13},{13,9},{2,6},{6,2},{1... | collective-permute-start | bytes 147464 | tf_op jit(solution)/shard_map/ppermute | solution.py:698
  6.0 2.6 %collective-permute-start.3 = (bf16[16,1536]{1,0:T(8,128)(2,1)S(1)}, bf16[16,1536]{1,0:T(8,128)(2,1)S(1)}, u32[]{:S(2)}, u32[]{:S(2)}) collective-permute-start(bf16[16,1536]{1,0:T(8,128)(2,1)S(1)} %reshape.11), channel_id=1, source_target_pairs={{0,8},{4,12},{8,0},{12,4},{1,9},{5,13},{9,1},{13,5},{2,10},{6,14},... | collective-permute-start | bytes 147464 | tf_op jit(solution)/shard_map/ppermute | solution.py:698
  8.8 1.5 %collective-permute-start = (bf16[16,1536]{1,0:T(8,128)(2,1)S(1)}, bf16[16,1536]{1,0:T(8,128)(2,1)S(1)}, u32[]{:S(2)}, u32[]{:S(2)}) collective-permute-start(bf16[16,1536]{1,0:T(8,128)(2,1)S(1)} %reshape.10), channel_id=1, source_target_pairs={{0,2},{2,0},{1,3},{3,1},{4,6},{6,4},{5,7},{7,5},{8,10},{10,8},{9,1... | collective-permute-start | bytes 147464 | tf_op jit(solution)/shard_map/ppermute | solution.py:657
  11.1 5.5 %collective-permute-start.13 = (bf16[24,96,128]{2,1,0:T(8,128)(2,1)S(1)}, bf16[24,96,128]{2,1,0:T(8,128)(2,1)S(1)}, u32[]{:S(2)}, u32[]{:S(2)}) collective-permute-start(bf16[24,96,128]{2,1,0:T(8,128)(2,1)S(1)} %copy-done.4), channel_id=1, source_target_pairs={{0,12},{12,0},{1,13},{13,1},{2,14},{14,2},{3,15},{15,3},{16,28},{2... | collective-permute-start | bytes 1769480 | tf_op jit(solution)/shard_map/ppermute | solution.py:709
  16.6 0.7 copy-done.3
  19.2 4.6 %collective-permute-done.4 = bf16[3,16,1536]{2,1,0:T(8,128)(2,1)S(1)} collective-permute-done((bf16[3,16,1536]{2,1,0:T(8,128)(2,1)S(1)}, bf16[3,16,1536]{2,1,0:T(8,128)(2,1)S(1)}, u32[]{:S(2)}, u32[]{:S(2)}) %collective-permute-start.4) | collective-permute-done | bytes 147488 | tf_op jit(solution)/shard_map/ppermute | solution.py:657
  24.5 0.7 collective-permute-done.6.recv_ref
  25.3 1.2 %shard_map.74.refs_2_ = bf16[32,96,64]{2,1,0:T(8,128)(2,1)S(1)} custom-call(bf16[2,2,16,1536]{3,2,1,0:T(8,128)(2,1)S(1)} %pad_maximum_fusion.1.own_ref, bf16[2,2,16,1536]{3,2,1,0:T(8,128)(2,1)S(1)} %collective-permute-done.6.recv_ref), custom_call_target="tpu_custom_call" | custom-call | tf_op jit(solution)/shard_map/pallas_call | solution.py:122
  26.5 6.4 %shard_map.76 = (bf16[24,128,96]{2,1,0:T(8,128)(2,1)S(1)}, bf16[24,128,96]{2,1,0:T(8,128)(2,1)S(1)}, bf16[64,24,128]{2,1,0:T(8,128)(2,1)S(1)}, bf16[64,24,128]{2...) custom-call(s32[3]{0:T(128)S(1)} %pad_add_fusion.pos_ref, ...), custom_call_target="tpu_custom_call" | custom-call | flops 1283457024 | bytes 7077888 | tf_op jit(solution)/shard_map/pallas_call | solution.py:250
  33.5 0.7 collective-permute-start.11
  34.2 13.5 %collective-permute-start.9 = (bf16[48,24,128]{2,1,0:T(8,128)(2,1)S(1)}, bf16[48,24,128]{2,1,0:T(8,128)(2,1)S(1)}, u32[]{:S(2)}, u32[]{:S(2)}) collective-permute-start(bf16[48,24,128]{2,1,0:T(8,128)(2,1)S(1)} %get-tuple-element.41.rest_0_), channel_id=1, source_target_pairs={{0,4},{4,0},{8,12},{12,8},{1,5},{5,1},{9,13},{13,9},{2,6},{6,2},{1... | collective-permute-start | bytes 884744 | tf_op jit(solution)/shard_map/ppermute | solution.py:720
  47.8 0.7 collective-permute-start.12
  48.4 4.9 %shard_map.77 = (bf16[48,24,128]{2,1,0:T(8,128)(2,1)S(1)}, bf16[48,24,128]{2,1,0:T(8,128)(2,1)S(1)}) custom-call(s32[3]{0:T(128)S(1)} %pad_add_fusion.pos_ref, bf16[2,32,768]{2,1,0:T(8,128)(2,1)S(1)} %get-tuple-element.70.refs_0_, bf16[2,32,768]{2,1,0:T(8,128)(2,1)S(1)} %collective-permute-done.5.refs_1_, bf16[32,96,64]{2,1,0:T(8,128)(2,1)S(1)} %shard_map.74.refs_2_, ...), custom_call_target="tpu_custom_call" | custom-call | flops 1283457024 | bytes 7077888 | tf_op jit(solution)/shard_map/pallas_call | solution.py:250
  53.5 2.1 %collective-permute-done.9.rest_2_ = bf16[48,24,128]{2,1,0:T(8,128)(2,1)S(1)} collective-permute-done((bf16[48,24,128]{2,1,0:T(8,128)(2,1)S(1)}, bf16[48,24,128]{2,1,0:T(8,128)(2,1)S(1)}, u32[]{:S(2)}, u32[]{:S(2)}) %collective-permute-start.9) | collective-permute-done | bytes 294944 | tf_op jit(solution)/shard_map/ppermute | solution.py:720
  55.5 0.7 collective-permute-start.15
  56.2 1.3 %collective-permute-start.16 = (bf16[48,24,128]{2,1,0:T(8,128)(2,1)S(1)}, bf16[48,24,128]{2,1,0:T(8,128)(2,1)S(1)}, u32[]{:S(2)}, u32[]{:S(2)}) collective-permute-start(bf16[48,24,128]{2,1,0:T(8,128)(2,1)S(1)} %collective-permute-done.11.rest_4_), channel_id=1, source_target_pairs={{4,0},{8,12},{5,1},{9,13},{6,2},{10,14},{7,3},{11,15},{20,16},{24,... | collective-permute-start | bytes 884744 | tf_op jit(solution)/shard_map/ppermute | solution.py:720
  57.5 3.8 %collective-permute-done.10.rest_3_ = bf16[48,24,128]{2,1,0:T(8,128)(2,1)S(1)} collective-permute-done((bf16[48,24,128]{2,1,0:T(8,128)(2,1)S(1)}, bf16[48,24,128]{2,1,0:T(8,128)(2,1)S(1)}, u32[]{:S(2)}, u32[]{:S(2)}) %collective-permute-start.10) | collective-permute-done | bytes 294944 | tf_op jit(solution)/shard_map/ppermute | solution.py:720
  61.3 0.7 collective-permute-start.18
  62.0 1.3 %collective-permute-start.19 = (bf16[48,24,128]{2,1,0:T(8,128)(2,1)S(1)}, bf16[48,24,128]{2,1,0:T(8,128)(2,1)S(1)}, u32[]{:S(2)}, u32[]{:S(2)}) collective-permute-start(bf16[48,24,128]{2,1,0:T(8,128)(2,1)S(1)} %collective-permute-done.12.rest_5_), channel_id=1, source_target_pairs={{4,0},{8,12},{5,1},{9,13},{6,2},{10,14},{7,3},{11,15},{20,16},{24,... | collective-permute-start | bytes 884744 | tf_op jit(solution)/shard_map/ppermute | solution.py:720
  63.3 3.5 %shard_map.78 = (bf16[24,24,128]{2,1,0:T(8,128)(2,1)S(1)}, bf16[24,24,128]{2,1,0:T(8,128)(2,1)S(1)}, bf16[24,24,128]{2,1,0:T(8,128)(2,1)S(1)}, bf16[24,24,128]{2...) custom-call(s32[3]{0:T(128)S(1)} %pad_add_fusion.pos_ref, ...), custom_call_target="tpu_custom_call" | custom-call | flops 14155776 | bytes 2359296 | tf_op jit(solution)/shard_map/pallas_call | solution.py:520
  67.4 1.7 %collective-permute-done.16.outward = bf16[48,24,128]{2,1,0:T(8,128)(2,1)S(1)} collective-permute-done((bf16[48,24,128]{2,1,0:T(8,128)(2,1)S(1)}, bf16[48,24,128]{2,1,0:T(8,128)(2,1)S(1)}, u32[]{:S(2)}, u32[]{:S(2)}) %collective-permute-start.16) | collective-permute-done | bytes 294944 | tf_op jit(solution)/shard_map/ppermute | solution.py:720
  69.1 1.7 %shard_map.79 = (bf16[12,24,128]{2,1,0:T(8,128)(2,1)S(1)}, bf16[12,24,128]{2,1,0:T(8,128)(2,1)S(1)}, bf16[12,24,128]{2,1,0:T(8,128)(2,1)S(1)}, bf16[12,24,128]{2,1,0:T(8,128)(2,1)S(1)}) custom-call(s32[3]{0:T(128)S(1)} %pad_add_fusion.pos_ref, bf16[64,24,128]{2,1,0:T(8,128)(2,1)S(1)} %get-tuple-element.39.lk_ref, ...), custom_call_target="tpu_custom_call" | custom-call | flops 14155776 | bytes 2359296 | tf_op jit(solution)/shard_map/pallas_call | solution.py:520
  71.5 3.2 %collective-permute-done.19.outward = bf16[48,24,128]{2,1,0:T(8,128)(2,1)S(1)} collective-permute-done((bf16[48,24,128]{2,1,0:T(8,128)(2,1)S(1)}, bf16[48,24,128]{2,1,0:T(8,128)(2,1)S(1)}, u32[]{:S(2)}, u32[]{:S(2)}) %collective-permute-start.19) | collective-permute-done | bytes 294944 | tf_op jit(solution)/shard_map/ppermute | solution.py:720
  74.7 1.7 %shard_map.80 = (bf16[12,24,128]{2,1,0:T(8,128)(2,1)S(1)}, bf16[12,24,128]{2,1,0:T(8,128)(2,1)S(1)}, bf16[12,24,128]{2,1,0:T(8,128)(2,1)S(1)}, bf16[12,24,128]{2,1,0:T(8,128)(2,1)S(1)}) custom-call(s32[3]{0:T(128)S(1)} %pad_add_fusion.pos_ref, bf16[64,24,128]{2,1,0:T(8,128)(2,1)S(1)} %get-tuple-element.39.lk_ref, ...), custom_call_target="tpu_custom_call" | custom-call | flops 14155776 | bytes 2359296 | tf_op jit(solution)/shard_map/pallas_call | solution.py:520
  77.1 1.5 %collective-permute-start.20 = (bf16[12,24,128]{2,1,0:T(8,128)(2,1)S(1)}, bf16[12,24,128]{2,1,0:T(8,128)(2,1)S(1)}, u32[]{:S(2)}, u32[]{:S(2)}) collective-permute-start(bf16[12,24,128]{2,1,0:T(8,128)(2,1)S(1)} %get-tuple-element.50), channel_id=1, source_target_pairs={{0,2},{2,0},{1,3},{3,1},{4,6},{6,4},{5,7},{7,5},{8,10},{10,8},{9,1... | collective-permute-start | bytes 221192 | tf_op jit(solution)/shard_map/ppermute | solution.py:657
  79.3 1.7 %shard_map.81 = (bf16[24,48,128]{2,1,0:T(8,128)(2,1)S(1)}, bf16[24,48,128]{2,1,0:T(8,128)(2,1)S(1)}, bf16[24,48,128]{2,1,0:T(8,128)(2,1)S(1)}) custom-call(s32[3]{0:T(128)S(1)} %pad_add_fusion.pos_ref, bf16[24,24,128]{2,1,0:T(8,128)(2,1)S(1)} %get-tuple-element.55.a_ref, bf16[24,24,128]{2,1,0:T(8,128)(2,1)S(1)} %collective-permute-done.25.b_ref, ...), custom_call_target="tpu_custom_call" | custom-call | flops 37748736 | bytes 1474560 | tf_op jit(solution)/shard_map/pallas_call | solution.py:644
  81.3 2.0 %collective-permute-done.20.refs_3_ = bf16[12,24,128]{2,1,0:T(8,128)(2,1)S(1)} collective-permute-done((bf16[12,24,128]{2,1,0:T(8,128)(2,1)S(1)}, bf16[12,24,128]{2,1,0:T(8,128)(2,1)S(1)}, u32[]{:S(2)}, u32[]{:S(2)}) %collective-permute-start.20) | collective-permute-done | bytes 73760 | tf_op jit(solution)/shard_map/ppermute | solution.py:657
  83.3 1.2 %collective-permute-done.24.refs_7_ = bf16[12,24,128]{2,1,0:T(8,128)(2,1)S(1)} collective-permute-done((bf16[12,24,128]{2,1,0:T(8,128)(2,1)S(1)}, bf16[12,24,128]{2,1,0:T(8,128)(2,1)S(1)}, u32[]{:S(2)}, u32[]{:S(2)}) %collective-permute-start.24) | collective-permute-done | bytes 73760 | tf_op jit(solution)/shard_map/ppermute | solution.py:667
  84.5 2.2 %shard_map.82 = bf16[24,96,128]{2,1,0:T(8,128)(2,1)} custom-call(s32[3]{0:T(128)S(1)} %pad_add_fusion.pos_ref, bf16[12,24,128]{2,1,0:T(8,128)(2,1)S(1)} %get-tuple-element.47.refs_0_, bf16[12,24,128]{2,1,0:T(8,128)(2,1)S(1)} %collective-permute-done.17.refs_1_, bf16[12,24,128]{2,1,0:T(8,128)(2,1)S(1)} %get-tuple-element.49.refs_2_, ...), custom_call_target="tpu_custom_call" | custom-call | flops 37748736 | bytes 1474560 | tf_op jit(solution)/shard_map/pallas_call | solution.py:644
  (65 shorter events, 7.3 us)
Async XLA Ops:
  1.0 1.0 %copy-start = (bf16[16,48,256]{2,1,0:T(8,128)(2,1)S(1)}, bf16[16,48,256]{2,1,0:T(8,128)(2,1)}, u32[]{:S(2)}) copy-start(bf16[16,48,256]{2,1,0:T(8,128)(2,1)} %param.7) | copy-start | bytes 1179652
  2.7 8.4 %copy-start.4 = (bf16[24,96,128]{2,1,0:T(8,128)(2,1)S(1)}, bf16[24,96,128]{2,1,0:T(8,128)(2,1)}, u32[]{:S(2)}) copy-start(bf16[24,96,128]{2,1,0:T(8,128)(2,1)} %refs_4_.1) | copy-start | bytes 1769476
  2.9 15.5 %collective-permute-start.2 = (bf16[16,1536]{1,0:T(8,128)(2,1)S(1)}, bf16[16,1536]{1,0:T(8,128)(2,1)S(1)}, u32[]{:S(2)}, u32[]{:S(2)}) collective-permute-start(bf16[16,1536]{1,0:T(8,128)(2,1)S(1)} %reshape.11), channel_id=1, source_target_pairs={{0,4},{4,0},{8,12},{12,8},{1,5},{5,1},{9,13},{13,9},{2,6},{6,2},{1... | collective-permute-start | bytes 147464 | tf_op jit(solution)/shard_map/ppermute | solution.py:698
  6.0 12.4 %collective-permute-start.3 = (bf16[16,1536]{1,0:T(8,128)(2,1)S(1)}, bf16[16,1536]{1,0:T(8,128)(2,1)S(1)}, u32[]{:S(2)}, u32[]{:S(2)}) collective-permute-start(bf16[16,1536]{1,0:T(8,128)(2,1)S(1)} %reshape.11), channel_id=1, source_target_pairs={{0,8},{4,12},{8,0},{12,4},{1,9},{5,13},{9,1},{13,5},{2,10},{6,14},... | collective-permute-start | bytes 147464 | tf_op jit(solution)/shard_map/ppermute | solution.py:698
  8.8 9.0 %collective-permute-start = (bf16[16,1536]{1,0:T(8,128)(2,1)S(1)}, bf16[16,1536]{1,0:T(8,128)(2,1)S(1)}, u32[]{:S(2)}, u32[]{:S(2)}) collective-permute-start(bf16[16,1536]{1,0:T(8,128)(2,1)S(1)} %reshape.10), channel_id=1, source_target_pairs={{0,2},{2,0},{1,3},{3,1},{4,6},{6,4},{5,7},{7,5},{8,10},{10,8},{9,1... | collective-permute-start | bytes 147464 | tf_op jit(solution)/shard_map/ppermute | solution.py:657
  10.5 6.1 %copy-start.1 = (bf16[1024,128]{1,0:T(8,128)(2,1)S(1)}, bf16[1024,128]{1,0:T(8,128)(2,1)}, u32[]{:S(2)}) copy-start(bf16[1024,128]{1,0:T(8,128)(2,1)} %w_ref.1) | copy-start | bytes 786436
  10.7 5.9 %copy-start.2 = (bf16[128,640]{1,0:T(8,128)(2,1)S(1)}, bf16[128,640]{1,0:T(8,128)(2,1)}, u32[]{:S(2)}) copy-start(bf16[128,640]{1,0:T(8,128)(2,1)} %n_ref.1) | copy-start | bytes 491524
  10.8 7.6 %collective-permute-start.1 = (bf16[2,16,1536]{2,1,0:T(8,128)(2,1)S(1)}, bf16[2,16,1536]{2,1,0:T(8,128)(2,1)S(1)}, u32[]{:S(2)}, u32[]{:S(2)}) collective-permute-start(bf16[2,16,1536]{2,1,0:T(8,128)(2,1)S(1)} %pad_maximum_fusion.3), channel_id=1, source_target_pairs={{0,12},{4,8},{8,4},{12,0},{1,13},{5,9},{9,5},{13,1},{2,14},{6,10},... | collective-permute-start | bytes 294920 | tf_op jit(solution)/shard_map/ppermute | solution.py:698
  11.1 36.7 %collective-permute-start.13 = (bf16[24,96,128]{2,1,0:T(8,128)(2,1)S(1)}, bf16[24,96,128]{2,1,0:T(8,128)(2,1)S(1)}, u32[]{:S(2)}, u32[]{:S(2)}) collective-permute-start(bf16[24,96,128]{2,1,0:T(8,128)(2,1)S(1)} %copy-done.4), channel_id=1, source_target_pairs={{0,12},{12,0},{1,13},{13,1},{2,14},{14,2},{3,15},{15,3},{16,28},{2... | collective-permute-start | bytes 1769480 | tf_op jit(solution)/shard_map/ppermute | solution.py:709
  18.5 5.2 %collective-permute-start.4 = (bf16[3,16,1536]{2,1,0:T(8,128)(2,1)S(1)}, bf16[3,16,1536]{2,1,0:T(8,128)(2,1)S(1)}, u32[]{:S(2)}, u32[]{:S(2)}) collective-permute-start(bf16[3,16,1536]{2,1,0:T(8,128)(2,1)S(1)} %pad_maximum_fusion.2), channel_id=1, source_target_pairs={{0,2},{2,0},{1,3},{3,1},{4,6},{6,4},{5,7},{7,5},{8,10},{10,8},{9,1... | collective-permute-start | bytes 442376 | tf_op jit(solution)/shard_map/ppermute | solution.py:657
  23.8 1.5 %collective-permute-start.6 = (bf16[2,2,16,1536]{3,2,1,0:T(8,128)(2,1)S(1)}, bf16[2,2,16,1536]{3,2,1,0:T(8,128)(2,1)S(1)}, u32[]{:S(2)}, u32[]{:S(2)}) collective-permute-start(bf16[2,2,16,1536]{3,2,1,0:T(8,128)(2,1)S(1)} %pad_maximum_fusion.1.own_ref), channel_id=1, source_target_pairs={{0,1},{1,0},{2,3},{3,2},{4,5},{5,4},{6,7},{7,6},{8,9},{9,8},{10,11... | collective-permute-start | bytes 589832 | tf_op jit(solution)/shard_map/ppermute | solution.py:657
  23.9 2.6 %collective-permute-start.5 = (bf16[2,32,768]{2,1,0:T(8,128)(2,1)S(1)}, bf16[2,32,768]{2,1,0:T(8,128)(2,1)S(1)}, u32[]{:S(2)}, u32[]{:S(2)}) collective-permute-start(bf16[2,32,768]{2,1,0:T(8,128)(2,1)S(1)} %get-tuple-element.69), channel_id=1, source_target_pairs={{0,1},{1,0},{2,3},{3,2},{4,5},{5,4},{6,7},{7,6},{8,9},{9,8},{10,11... | collective-permute-start | bytes 294920 | tf_op jit(solution)/shard_map/ppermute | solution.py:657
  32.9 14.7 %collective-permute-start.8 = (bf16[48,24,128]{2,1,0:T(8,128)(2,1)S(1)}, bf16[48,24,128]{2,1,0:T(8,128)(2,1)S(1)}, u32[]{:S(2)}, u32[]{:S(2)}) collective-permute-start(bf16[48,24,128]{2,1,0:T(8,128)(2,1)S(1)} %get-tuple-element.42), channel_id=1, source_target_pairs={{0,1},{1,0},{2,3},{3,2},{4,5},{5,4},{6,7},{7,6},{8,9},{9,8},{10,11... | collective-permute-start | bytes 884744 | tf_op jit(solution)/shard_map/ppermute | solution.py:657
  33.1 23.1 %collective-permute-start.7 = (bf16[64,24,128]{2,1,0:T(8,128)(2,1)S(1)}, bf16[64,24,128]{2,1,0:T(8,128)(2,1)S(1)}, u32[]{:S(2)}, u32[]{:S(2)}) collective-permute-start(bf16[64,24,128]{2,1,0:T(8,128)(2,1)S(1)} %get-tuple-element.40), channel_id=1, source_target_pairs={{0,1},{1,0},{2,3},{3,2},{4,5},{5,4},{6,7},{7,6},{8,9},{9,8},{10,11... | collective-permute-start | bytes 1179656 | tf_op jit(solution)/shard_map/ppermute | solution.py:657
  33.5 19.9 %collective-permute-start.11 = (bf16[48,24,128]{2,1,0:T(8,128)(2,1)S(1)}, bf16[48,24,128]{2,1,0:T(8,128)(2,1)S(1)}, u32[]{:S(2)}, u32[]{:S(2)}) collective-permute-start(bf16[48,24,128]{2,1,0:T(8,128)(2,1)S(1)} %get-tuple-element.41.rest_0_), channel_id=1, source_target_pairs={{4,8},{8,4},{5,9},{9,5},{6,10},{10,6},{7,11},{11,7},{20,24},{24,20... | collective-permute-start | bytes 884744 | tf_op jit(solution)/shard_map/ppermute | solution.py:720
  34.2 21.4 %collective-permute-start.9 = (bf16[48,24,128]{2,1,0:T(8,128)(2,1)S(1)}, bf16[48,24,128]{2,1,0:T(8,128)(2,1)S(1)}, u32[]{:S(2)}, u32[]{:S(2)}) collective-permute-start(bf16[48,24,128]{2,1,0:T(8,128)(2,1)S(1)} %get-tuple-element.41.rest_0_), channel_id=1, source_target_pairs={{0,4},{4,0},{8,12},{12,8},{1,5},{5,1},{9,13},{13,9},{2,6},{6,2},{1... | collective-permute-start | bytes 884744 | tf_op jit(solution)/shard_map/ppermute | solution.py:720
  47.7 13.6 %collective-permute-start.10 = (bf16[48,24,128]{2,1,0:T(8,128)(2,1)S(1)}, bf16[48,24,128]{2,1,0:T(8,128)(2,1)S(1)}, u32[]{:S(2)}, u32[]{:S(2)}) collective-permute-start(bf16[48,24,128]{2,1,0:T(8,128)(2,1)S(1)} %collective-permute-done.8.rest_1_), channel_id=1, source_target_pairs={{0,4},{4,0},{8,12},{12,8},{1,5},{5,1},{9,13},{13,9},{2,6},{6,2},{1... | collective-permute-start | bytes 884744 | tf_op jit(solution)/shard_map/ppermute | solution.py:720
  47.8 14.2 %collective-permute-start.12 = (bf16[48,24,128]{2,1,0:T(8,128)(2,1)S(1)}, bf16[48,24,128]{2,1,0:T(8,128)(2,1)S(1)}, u32[]{:S(2)}, u32[]{:S(2)}) collective-permute-start(bf16[48,24,128]{2,1,0:T(8,128)(2,1)S(1)} %collective-permute-done.8.rest_1_), channel_id=1, source_target_pairs={{4,8},{8,4},{5,9},{9,5},{6,10},{10,6},{7,11},{11,7},{20,24},{24,20... | collective-permute-start | bytes 884744 | tf_op jit(solution)/shard_map/ppermute | solution.py:720
  53.4 9.9 %collective-permute-start.14 = (bf16[48,24,128]{2,1,0:T(8,128)(2,1)S(1)}, bf16[48,24,128]{2,1,0:T(8,128)(2,1)S(1)}, u32[]{:S(2)}, u32[]{:S(2)}) collective-permute-start(bf16[48,24,128]{2,1,0:T(8,128)(2,1)S(1)} %get-tuple-element.44), channel_id=1, source_target_pairs={{0,1},{1,0},{2,3},{3,2},{4,5},{5,4},{6,7},{7,6},{8,9},{9,8},{10,11... | collective-permute-start | bytes 884744 | tf_op jit(solution)/shard_map/ppermute | solution.py:657
  55.5 11.9 %collective-permute-start.15 = (bf16[48,24,128]{2,1,0:T(8,128)(2,1)S(1)}, bf16[48,24,128]{2,1,0:T(8,128)(2,1)S(1)}, u32[]{:S(2)}, u32[]{:S(2)}) collective-permute-start(bf16[48,24,128]{2,1,0:T(8,128)(2,1)S(1)} %collective-permute-done.9.rest_2_), channel_id=1, source_target_pairs={{4,8},{8,4},{5,9},{9,5},{6,10},{10,6},{7,11},{11,7},{20,24},{24,20... | collective-permute-start | bytes 884744 | tf_op jit(solution)/shard_map/ppermute | solution.py:720
  56.2 12.9 %collective-permute-start.16 = (bf16[48,24,128]{2,1,0:T(8,128)(2,1)S(1)}, bf16[48,24,128]{2,1,0:T(8,128)(2,1)S(1)}, u32[]{:S(2)}, u32[]{:S(2)}) collective-permute-start(bf16[48,24,128]{2,1,0:T(8,128)(2,1)S(1)} %collective-permute-done.11.rest_4_), channel_id=1, source_target_pairs={{4,0},{8,12},{5,1},{9,13},{6,2},{10,14},{7,3},{11,15},{20,16},{24,... | collective-permute-start | bytes 884744 | tf_op jit(solution)/shard_map/ppermute | solution.py:720
  61.3 9.6 %collective-permute-start.18 = (bf16[48,24,128]{2,1,0:T(8,128)(2,1)S(1)}, bf16[48,24,128]{2,1,0:T(8,128)(2,1)S(1)}, u32[]{:S(2)}, u32[]{:S(2)}) collective-permute-start(bf16[48,24,128]{2,1,0:T(8,128)(2,1)S(1)} %collective-permute-done.10.rest_3_), channel_id=1, source_target_pairs={{4,8},{8,4},{5,9},{9,5},{6,10},{10,6},{7,11},{11,7},{20,24},{24,20... | collective-permute-start | bytes 884744 | tf_op jit(solution)/shard_map/ppermute | solution.py:720
  62.0 12.7 %collective-permute-start.19 = (bf16[48,24,128]{2,1,0:T(8,128)(2,1)S(1)}, bf16[48,24,128]{2,1,0:T(8,128)(2,1)S(1)}, u32[]{:S(2)}, u32[]{:S(2)}) collective-permute-start(bf16[48,24,128]{2,1,0:T(8,128)(2,1)S(1)} %collective-permute-done.12.rest_5_), channel_id=1, source_target_pairs={{4,0},{8,12},{5,1},{9,13},{6,2},{10,14},{7,3},{11,15},{20,16},{24,... | collective-permute-start | bytes 884744 | tf_op jit(solution)/shard_map/ppermute | solution.py:720
  66.8 10.3 %collective-permute-start.25 = (bf16[24,24,128]{2,1,0:T(8,128)(2,1)S(1)}, bf16[24,24,128]{2,1,0:T(8,128)(2,1)S(1)}, u32[]{:S(2)}, u32[]{:S(2)}) collective-permute-start(bf16[24,24,128]{2,1,0:T(8,128)(2,1)S(1)} %get-tuple-element.56), channel_id=1, source_target_pairs={{0,2},{2,0},{1,3},{3,1},{4,6},{6,4},{5,7},{7,5},{8,10},{10,8},{9,1... | collective-permute-start | bytes 442376 | tf_op jit(solution)/shard_map/ppermute | solution.py:657
  67.4 11.2 %collective-permute-start.26 = (bf16[24,24,128]{2,1,0:T(8,128)(2,1)S(1)}, bf16[24,24,128]{2,1,0:T(8,128)(2,1)S(1)}, u32[]{:S(2)}, u32[]{:S(2)}) collective-permute-start(bf16[24,24,128]{2,1,0:T(8,128)(2,1)S(1)} %get-tuple-element.57), channel_id=1, source_target_pairs={{0,1},{1,0},{2,3},{3,2},{4,5},{5,4},{6,7},{7,6},{8,9},{9,8},{10,11... | collective-permute-start | bytes 442376 | tf_op jit(solution)/shard_map/ppermute | solution.py:657
  69.1 9.7 %collective-permute-start.27 = (bf16[24,24,128]{2,1,0:T(8,128)(2,1)S(1)}, bf16[24,24,128]{2,1,0:T(8,128)(2,1)S(1)}, u32[]{:S(2)}, u32[]{:S(2)}) collective-permute-start(bf16[24,24,128]{2,1,0:T(8,128)(2,1)S(1)} %get-tuple-element.58), channel_id=1, source_target_pairs={{0,3},{1,2},{2,1},{3,0},{4,7},{5,6},{6,5},{7,4},{8,11},{9,10},{10,... | collective-permute-start | bytes 442376 | tf_op jit(solution)/shard_map/ppermute | solution.py:667
  70.9 6.1 %collective-permute-start.17 = (bf16[12,24,128]{2,1,0:T(8,128)(2,1)S(1)}, bf16[12,24,128]{2,1,0:T(8,128)(2,1)S(1)}, u32[]{:S(2)}, u32[]{:S(2)}) collective-permute-start(bf16[12,24,128]{2,1,0:T(8,128)(2,1)S(1)} %get-tuple-element.48), channel_id=1, source_target_pairs={{0,2},{2,0},{1,3},{3,1},{4,6},{6,4},{5,7},{7,5},{8,10},{10,8},{9,1... | collective-permute-start | bytes 221192 | tf_op jit(solution)/shard_map/ppermute | solution.py:657
  74.7 6.4 %collective-permute-start.21 = (bf16[12,24,128]{2,1,0:T(8,128)(2,1)S(1)}, bf16[12,24,128]{2,1,0:T(8,128)(2,1)S(1)}, u32[]{:S(2)}, u32[]{:S(2)}) collective-permute-start(bf16[12,24,128]{2,1,0:T(8,128)(2,1)S(1)} %get-tuple-element.51), channel_id=1, source_target_pairs={{0,1},{1,0},{2,3},{3,2},{4,5},{5,4},{6,7},{7,6},{8,9},{9,8},{10,11... | collective-permute-start | bytes 221192 | tf_op jit(solution)/shard_map/ppermute | solution.py:657
  76.9 4.4 %collective-permute-start.22 = (bf16[12,24,128]{2,1,0:T(8,128)(2,1)S(1)}, bf16[12,24,128]{2,1,0:T(8,128)(2,1)S(1)}, u32[]{:S(2)}, u32[]{:S(2)}) collective-permute-start(bf16[12,24,128]{2,1,0:T(8,128)(2,1)S(1)} %get-tuple-element.52), channel_id=1, source_target_pairs={{0,3},{1,2},{2,1},{3,0},{4,7},{5,6},{6,5},{7,4},{8,11},{9,10},{10,... | collective-permute-start | bytes 221192 | tf_op jit(solution)/shard_map/ppermute | solution.py:667
  77.1 6.2 %collective-permute-start.20 = (bf16[12,24,128]{2,1,0:T(8,128)(2,1)S(1)}, bf16[12,24,128]{2,1,0:T(8,128)(2,1)S(1)}, u32[]{:S(2)}, u32[]{:S(2)}) collective-permute-start(bf16[12,24,128]{2,1,0:T(8,128)(2,1)S(1)} %get-tuple-element.50), channel_id=1, source_target_pairs={{0,2},{2,0},{1,3},{3,1},{4,6},{6,4},{5,7},{7,5},{8,10},{10,8},{9,1... | collective-permute-start | bytes 221192 | tf_op jit(solution)/shard_map/ppermute | solution.py:657
  78.6 4.7 %collective-permute-start.23 = (bf16[12,24,128]{2,1,0:T(8,128)(2,1)S(1)}, bf16[12,24,128]{2,1,0:T(8,128)(2,1)S(1)}, u32[]{:S(2)}, u32[]{:S(2)}) collective-permute-start(bf16[12,24,128]{2,1,0:T(8,128)(2,1)S(1)} %get-tuple-element.53), channel_id=1, source_target_pairs={{0,1},{1,0},{2,3},{3,2},{4,5},{5,4},{6,7},{7,6},{8,9},{9,8},{10,11... | collective-permute-start | bytes 221192 | tf_op jit(solution)/shard_map/ppermute | solution.py:657
  78.8 5.6 %collective-permute-start.24 = (bf16[12,24,128]{2,1,0:T(8,128)(2,1)S(1)}, bf16[12,24,128]{2,1,0:T(8,128)(2,1)S(1)}, u32[]{:S(2)}, u32[]{:S(2)}) collective-permute-start(bf16[12,24,128]{2,1,0:T(8,128)(2,1)S(1)} %get-tuple-element.54), channel_id=1, source_target_pairs={{0,3},{1,2},{2,1},{3,0},{4,7},{5,6},{6,5},{7,4},{8,11},{9,10},{10,... | collective-permute-start | bytes 221192 | tf_op jit(solution)/shard_map/ppermute | solution.py:667
  (2 other events, 1.6 us)

commit v5 on v4

--- a/solution.py
+++ b/solution.py
@@ -50,14 +50,17 @@
     return lax.broadcasted_iota(jnp.int32, shape, len(shape) - 1)
 
 
-def factors_kernel(x_ref, first_ref, second_ref, left_ref, right_ref):
+def factors_kernel(x_ref, both_ref, left_ref, right_ref):
     rows = x_ref.shape[0]
+    fw = left_ref.shape[1]
     step = rows // 8 if rows % 128 == 0 else rows
     for t in range(rows // step):
         part = slice(t * step, (t + 1) * step)
         normed = standardize_features(x_ref[part, :].astype(jnp.float32)).astype(jnp.bfloat16)
-        right_ref[part, :] = jnp.dot(normed, second_ref[...], preferred_element_type=jnp.float32).astype(jnp.bfloat16)
-        left_ref[part, :] = jnp.dot(normed, first_ref[...], preferred_element_type=jnp.float32).astype(jnp.bfloat16)
+        for k, out_ref in enumerate((right_ref, left_ref)):
+            matrix = both_ref[k * fw : (k + 1) * fw, :]
+            out = lax.dot_general(normed, matrix, (((1,), (1,)), ((), ())), preferred_element_type=jnp.float32)
+            out_ref[part, :] = out.astype(jnp.bfloat16)
 
 
 def factors(x, first, second):
@@ -65,10 +68,10 @@
     return pl.pallas_call(
         factors_kernel,
         out_shape=[shape, shape],
-        in_specs=[vmem()] * 3,
+        in_specs=[vmem()] * 2,
         out_specs=[vmem()] * 2,
         compiler_params=grant(6),
-    )(x, first, second)
+    )(x, jnp.concatenate([second.T, first.T], axis=0))
 
 
 def weights_kernel(fw, w_ref, n_ref, x_ref, wt_ref, nt_ref, xt_ref, sc, st):
@@ -740,7 +743,8 @@
             kernel = functools.partial(late_kernel, u)
             send, sendo, keep, keepo = products(kernel, rk.shape, acc, (1,), 4, pos, lk, lr, [rest, resto], [last_in[u], last_out[u]], tile_cols, nr)
             own += [keep, shift(send, "col", 1)]
-            other += [shift(keepo, "sub", 1), across(sendo, 1)]
+            diagonal = across(sendo, 1)
+            other += [shift(keepo, "sub", 1), diagonal]
         return finish_group(finish_late_kernel, [edge_activations.shape], width, tile_rows, pos, *own, *other, done1, mid2, gate2, exit_matrix)[0]
 
     outer_weight, entry, exit_matrix = weights(tensor_product_matrix, multiplicative_entry_matrix, multiplicative_exit_matrix, fw)

time: 88.2 us -> 87.9 us (level)
  local copies, waits for them, and re-layouts: 3.49 us -> 2.52 us
    unnamed x14 -> x10, local copies, waits for them, and re-layouts: 2.68 us -> 1.71 us
where the time goes in v5:
time: 87.9 us; the launch traced here: 86.4 us
  starting transfers between devices  37.3 us (42%)
  Pallas kernels  24.6 us (28%)
  waiting for transfers between devices  20.7 us (24%)
  local copies, waits for them, and re-layouts  2.52 us (3%)
  other arithmetic  0.95 us (1%)
    ppermute x8, starting transfers between devices, along(): return lax.ppermute(x, 'row', pairs)  18.8 us
    pallas_call x2, Pallas kernels, pair(): return f(pos, l, lr, rt, wt, e, went)  11.3 us
    ppermute x8, waiting for transfers between devices, along(): return lax.ppermute(x, 'row', pairs)  10.7 us
    ppermute x13, waiting for transfers between devices, shift(): return lax.ppermute(x, axis, [(i, (i + d) % n) for i in range(n)])  7.91 us
    pallas_call x3, Pallas kernels, products(): pl.pallas_call(functools.partial(kernel, J, n), out_shape=[jax.ShapeDtype...  6.94 us
    ppermute x13, starting transfers between devices, shift(): return lax.ppermute(x, axis, [(i, (i + d) % n) for i in range(n)])  6.31 us
    ppermute x3, starting transfers between devices, per_device(): hops.append(lax.ppermute(x, 'row', [(i, i ^ d) for i in range(nr)]))  6 us
    ppermute x1, starting transfers between devices, per_device(): lax.ppermute(edge_activations, 'row', [(0, nr - 1), (nr - 1, 0)])  5.5 us
  transfers between devices with their start and end apart: 28, of which 11 were waited for; matrix products, arithmetic and copies ran while one was open for 1% of the time, Pallas kernels for 25%

profile of v5, /device:TPU:0, one launch (start us, length us, event | category | flops | bytes accessed | tf_op | source)
XLA Modules:
  0.0 86.4 jit_solution(7833948984644864603)
XLA Ops:
  0.0 0.7 pad_maximum_fusion.4.both_ref
  0.7 1.0 %copy-done = bf16[16,48,256]{2,1,0:T(8,128)(2,1)S(1)} copy-done((bf16[16,48,256]{2,1,0:T(8,128)(2,1)S(1)}, bf16[16,48,256]{2,1,0:T(8,128)(2,1)}, u32[]{:S(2)}) %copy-start) | copy-done | bytes 393240
  1.7 0.7 shard_map.73
  2.6 3.1 %collective-permute-start.2 = (bf16[16,1536]{1,0:T(8,128)(2,1)S(1)}, bf16[16,1536]{1,0:T(8,128)(2,1)S(1)}, u32[]{:S(2)}, u32[]{:S(2)}) collective-permute-start(bf16[16,1536]{1,0:T(8,128)(2,1)S(1)} %reshape.11), channel_id=1, source_target_pairs={{0,4},{4,0},{8,12},{12,8},{1,5},{5,1},{9,13},{13,9},{2,6},{6,2},{1... | collective-permute-start | bytes 147464 | tf_op jit(solution)/shard_map/ppermute | solution.py:701
  5.7 2.6 %collective-permute-start.3 = (bf16[16,1536]{1,0:T(8,128)(2,1)S(1)}, bf16[16,1536]{1,0:T(8,128)(2,1)S(1)}, u32[]{:S(2)}, u32[]{:S(2)}) collective-permute-start(bf16[16,1536]{1,0:T(8,128)(2,1)S(1)} %reshape.11), channel_id=1, source_target_pairs={{0,8},{4,12},{8,0},{12,4},{1,9},{5,13},{9,1},{13,5},{2,10},{6,14},... | collective-permute-start | bytes 147464 | tf_op jit(solution)/shard_map/ppermute | solution.py:701
  8.5 1.6 %collective-permute-start = (bf16[16,1536]{1,0:T(8,128)(2,1)S(1)}, bf16[16,1536]{1,0:T(8,128)(2,1)S(1)}, u32[]{:S(2)}, u32[]{:S(2)}) collective-permute-start(bf16[16,1536]{1,0:T(8,128)(2,1)S(1)} %reshape.10), channel_id=1, source_target_pairs={{0,2},{2,0},{1,3},{3,1},{4,6},{6,4},{5,7},{7,5},{8,10},{10,8},{9,1... | collective-permute-start | bytes 147464 | tf_op jit(solution)/shard_map/ppermute | solution.py:660
  10.8 5.5 %collective-permute-start.13 = (bf16[24,96,128]{2,1,0:T(8,128)(2,1)S(1)}, bf16[24,96,128]{2,1,0:T(8,128)(2,1)S(1)}, u32[]{:S(2)}, u32[]{:S(2)}) collective-permute-start(bf16[24,96,128]{2,1,0:T(8,128)(2,1)S(1)} %copy-done.4), channel_id=1, source_target_pairs={{0,12},{12,0},{1,13},{13,1},{2,14},{14,2},{3,15},{15,3},{16,28},{2... | collective-permute-start | bytes 1769480 | tf_op jit(solution)/shard_map/ppermute | solution.py:712
  16.4 0.7 copy-done.3
  18.9 4.6 %collective-permute-done.4 = bf16[3,16,1536]{2,1,0:T(8,128)(2,1)S(1)} collective-permute-done((bf16[3,16,1536]{2,1,0:T(8,128)(2,1)S(1)}, bf16[3,16,1536]{2,1,0:T(8,128)(2,1)S(1)}, u32[]{:S(2)}, u32[]{:S(2)}) %collective-permute-start.4) | collective-permute-done | bytes 147488 | tf_op jit(solution)/shard_map/ppermute | solution.py:660
  24.3 0.7 collective-permute-done.6.recv_ref
  25.0 1.2 %shard_map.74.refs_2_ = bf16[32,96,64]{2,1,0:T(8,128)(2,1)S(1)} custom-call(bf16[2,2,16,1536]{3,2,1,0:T(8,128)(2,1)S(1)} %pad_maximum_fusion.1.own_ref, bf16[2,2,16,1536]{3,2,1,0:T(8,128)(2,1)S(1)} %collective-permute-done.6.recv_ref), custom_call_target="tpu_custom_call" | custom-call | tf_op jit(solution)/shard_map/pallas_call | solution.py:125
  26.3 6.4 %shard_map.76 = (bf16[24,128,96]{2,1,0:T(8,128)(2,1)S(1)}, bf16[24,128,96]{2,1,0:T(8,128)(2,1)S(1)}, bf16[64,24,128]{2,1,0:T(8,128)(2,1)S(1)}, bf16[64,24,128]{2...) custom-call(s32[3]{0:T(128)S(1)} %pad_add_fusion.pos_ref, ...), custom_call_target="tpu_custom_call" | custom-call | flops 1283457024 | bytes 7077888 | tf_op jit(solution)/shard_map/pallas_call | solution.py:253
  33.2 0.7 collective-permute-start.11
  33.9 13.5 %collective-permute-start.9 = (bf16[48,24,128]{2,1,0:T(8,128)(2,1)S(1)}, bf16[48,24,128]{2,1,0:T(8,128)(2,1)S(1)}, u32[]{:S(2)}, u32[]{:S(2)}) collective-permute-start(bf16[48,24,128]{2,1,0:T(8,128)(2,1)S(1)} %get-tuple-element.41.rest_0_), channel_id=1, source_target_pairs={{0,4},{4,0},{8,12},{12,8},{1,5},{5,1},{9,13},{13,9},{2,6},{6,2},{1... | collective-permute-start | bytes 884744 | tf_op jit(solution)/shard_map/ppermute | solution.py:723
  47.5 0.7 collective-permute-start.12
  48.2 4.9 %shard_map.77 = (bf16[48,24,128]{2,1,0:T(8,128)(2,1)S(1)}, bf16[48,24,128]{2,1,0:T(8,128)(2,1)S(1)}) custom-call(s32[3]{0:T(128)S(1)} %pad_add_fusion.pos_ref, bf16[2,32,768]{2,1,0:T(8,128)(2,1)S(1)} %get-tuple-element.70.refs_0_, bf16[2,32,768]{2,1,0:T(8,128)(2,1)S(1)} %collective-permute-done.5.refs_1_, bf16[32,96,64]{2,1,0:T(8,128)(2,1)S(1)} %shard_map.74.refs_2_, ...), custom_call_target="tpu_custom_call" | custom-call | flops 1283457024 | bytes 7077888 | tf_op jit(solution)/shard_map/pallas_call | solution.py:253
  53.2 2.1 %collective-permute-done.9.rest_2_ = bf16[48,24,128]{2,1,0:T(8,128)(2,1)S(1)} collective-permute-done((bf16[48,24,128]{2,1,0:T(8,128)(2,1)S(1)}, bf16[48,24,128]{2,1,0:T(8,128)(2,1)S(1)}, u32[]{:S(2)}, u32[]{:S(2)}) %collective-permute-start.9) | collective-permute-done | bytes 294944 | tf_op jit(solution)/shard_map/ppermute | solution.py:723
  55.3 0.7 collective-permute-start.15
  55.9 1.3 %collective-permute-start.16 = (bf16[48,24,128]{2,1,0:T(8,128)(2,1)S(1)}, bf16[48,24,128]{2,1,0:T(8,128)(2,1)S(1)}, u32[]{:S(2)}, u32[]{:S(2)}) collective-permute-start(bf16[48,24,128]{2,1,0:T(8,128)(2,1)S(1)} %collective-permute-done.11.rest_4_), channel_id=1, source_target_pairs={{4,0},{8,12},{5,1},{9,13},{6,2},{10,14},{7,3},{11,15},{20,16},{24,... | collective-permute-start | bytes 884744 | tf_op jit(solution)/shard_map/ppermute | solution.py:723
  57.2 3.8 %collective-permute-done.10.rest_3_ = bf16[48,24,128]{2,1,0:T(8,128)(2,1)S(1)} collective-permute-done((bf16[48,24,128]{2,1,0:T(8,128)(2,1)S(1)}, bf16[48,24,128]{2,1,0:T(8,128)(2,1)S(1)}, u32[]{:S(2)}, u32[]{:S(2)}) %collective-permute-start.10) | collective-permute-done | bytes 294944 | tf_op jit(solution)/shard_map/ppermute | solution.py:723
  61.0 0.7 collective-permute-start.18
  61.7 1.3 %collective-permute-start.19 = (bf16[48,24,128]{2,1,0:T(8,128)(2,1)S(1)}, bf16[48,24,128]{2,1,0:T(8,128)(2,1)S(1)}, u32[]{:S(2)}, u32[]{:S(2)}) collective-permute-start(bf16[48,24,128]{2,1,0:T(8,128)(2,1)S(1)} %collective-permute-done.12.rest_5_), channel_id=1, source_target_pairs={{4,0},{8,12},{5,1},{9,13},{6,2},{10,14},{7,3},{11,15},{20,16},{24,... | collective-permute-start | bytes 884744 | tf_op jit(solution)/shard_map/ppermute | solution.py:723
  63.0 3.5 %shard_map.78 = (bf16[24,24,128]{2,1,0:T(8,128)(2,1)S(1)}, bf16[24,24,128]{2,1,0:T(8,128)(2,1)S(1)}, bf16[24,24,128]{2,1,0:T(8,128)(2,1)S(1)}, bf16[24,24,128]{2...) custom-call(s32[3]{0:T(128)S(1)} %pad_add_fusion.pos_ref, ...), custom_call_target="tpu_custom_call" | custom-call | flops 14155776 | bytes 2359296 | tf_op jit(solution)/shard_map/pallas_call | solution.py:523
  67.2 1.7 %collective-permute-done.16.outward = bf16[48,24,128]{2,1,0:T(8,128)(2,1)S(1)} collective-permute-done((bf16[48,24,128]{2,1,0:T(8,128)(2,1)S(1)}, bf16[48,24,128]{2,1,0:T(8,128)(2,1)S(1)}, u32[]{:S(2)}, u32[]{:S(2)}) %collective-permute-start.16) | collective-permute-done | bytes 294944 | tf_op jit(solution)/shard_map/ppermute | solution.py:723
  68.9 1.7 %shard_map.79 = (bf16[12,24,128]{2,1,0:T(8,128)(2,1)S(1)}, bf16[12,24,128]{2,1,0:T(8,128)(2,1)S(1)}, bf16[12,24,128]{2,1,0:T(8,128)(2,1)S(1)}, bf16[12,24,128]{2,1,0:T(8,128)(2,1)S(1)}) custom-call(s32[3]{0:T(128)S(1)} %pad_add_fusion.pos_ref, bf16[64,24,128]{2,1,0:T(8,128)(2,1)S(1)} %get-tuple-element.39.lk_ref, ...), custom_call_target="tpu_custom_call" | custom-call | flops 14155776 | bytes 2359296 | tf_op jit(solution)/shard_map/pallas_call | solution.py:523
  71.2 3.2 %collective-permute-done.19.outward = bf16[48,24,128]{2,1,0:T(8,128)(2,1)S(1)} collective-permute-done((bf16[48,24,128]{2,1,0:T(8,128)(2,1)S(1)}, bf16[48,24,128]{2,1,0:T(8,128)(2,1)S(1)}, u32[]{:S(2)}, u32[]{:S(2)}) %collective-permute-start.19) | collective-permute-done | bytes 294944 | tf_op jit(solution)/shard_map/ppermute | solution.py:723
  74.4 1.7 %shard_map.80 = (bf16[12,24,128]{2,1,0:T(8,128)(2,1)S(1)}, bf16[12,24,128]{2,1,0:T(8,128)(2,1)S(1)}, bf16[12,24,128]{2,1,0:T(8,128)(2,1)S(1)}, bf16[12,24,128]{2,1,0:T(8,128)(2,1)S(1)}) custom-call(s32[3]{0:T(128)S(1)} %pad_add_fusion.pos_ref, bf16[64,24,128]{2,1,0:T(8,128)(2,1)S(1)} %get-tuple-element.39.lk_ref, ...), custom_call_target="tpu_custom_call" | custom-call | flops 14155776 | bytes 2359296 | tf_op jit(solution)/shard_map/pallas_call | solution.py:523
  76.9 1.5 %collective-permute-start.20 = (bf16[12,24,128]{2,1,0:T(8,128)(2,1)S(1)}, bf16[12,24,128]{2,1,0:T(8,128)(2,1)S(1)}, u32[]{:S(2)}, u32[]{:S(2)}) collective-permute-start(bf16[12,24,128]{2,1,0:T(8,128)(2,1)S(1)} %get-tuple-element.50), channel_id=1, source_target_pairs={{0,2},{2,0},{1,3},{3,1},{4,6},{6,4},{5,7},{7,5},{8,10},{10,8},{9,1... | collective-permute-start | bytes 221192 | tf_op jit(solution)/shard_map/ppermute | solution.py:660
  79.0 1.7 %shard_map.81 = (bf16[24,48,128]{2,1,0:T(8,128)(2,1)S(1)}, bf16[24,48,128]{2,1,0:T(8,128)(2,1)S(1)}, bf16[24,48,128]{2,1,0:T(8,128)(2,1)S(1)}) custom-call(s32[3]{0:T(128)S(1)} %pad_add_fusion.pos_ref, bf16[24,24,128]{2,1,0:T(8,128)(2,1)S(1)} %get-tuple-element.55.a_ref, bf16[24,24,128]{2,1,0:T(8,128)(2,1)S(1)} %collective-permute-done.25.b_ref, ...), custom_call_target="tpu_custom_call" | custom-call | flops 37748736 | bytes 1474560 | tf_op jit(solution)/shard_map/pallas_call | solution.py:647
  81.0 2.0 %collective-permute-done.20.refs_3_ = bf16[12,24,128]{2,1,0:T(8,128)(2,1)S(1)} collective-permute-done((bf16[12,24,128]{2,1,0:T(8,128)(2,1)S(1)}, bf16[12,24,128]{2,1,0:T(8,128)(2,1)S(1)}, u32[]{:S(2)}, u32[]{:S(2)}) %collective-permute-start.20) | collective-permute-done | bytes 73760 | tf_op jit(solution)/shard_map/ppermute | solution.py:660
  83.0 1.2 %collective-permute-done.24.refs_7_ = bf16[12,24,128]{2,1,0:T(8,128)(2,1)S(1)} collective-permute-done((bf16[12,24,128]{2,1,0:T(8,128)(2,1)S(1)}, bf16[12,24,128]{2,1,0:T(8,128)(2,1)S(1)}, u32[]{:S(2)}, u32[]{:S(2)}) %collective-permute-start.24) | collective-permute-done | bytes 73760 | tf_op jit(solution)/shard_map/ppermute | solution.py:670
  84.2 2.2 %shard_map.82 = bf16[24,96,128]{2,1,0:T(8,128)(2,1)} custom-call(s32[3]{0:T(128)S(1)} %pad_add_fusion.pos_ref, bf16[12,24,128]{2,1,0:T(8,128)(2,1)S(1)} %get-tuple-element.47.refs_0_, bf16[12,24,128]{2,1,0:T(8,128)(2,1)S(1)} %collective-permute-done.17.refs_1_, bf16[12,24,128]{2,1,0:T(8,128)(2,1)S(1)} %get-tuple-element.49.refs_2_, ...), custom_call_target="tpu_custom_call" | custom-call | flops 37748736 | bytes 1474560 | tf_op jit(solution)/shard_map/pallas_call | solution.py:647
  (62 shorter events, 7.2 us)
Async XLA Ops:
  0.7 1.0 %copy-start = (bf16[16,48,256]{2,1,0:T(8,128)(2,1)S(1)}, bf16[16,48,256]{2,1,0:T(8,128)(2,1)}, u32[]{:S(2)}) copy-start(bf16[16,48,256]{2,1,0:T(8,128)(2,1)} %param.7) | copy-start | bytes 1179652
  2.4 8.4 %copy-start.4 = (bf16[24,96,128]{2,1,0:T(8,128)(2,1)S(1)}, bf16[24,96,128]{2,1,0:T(8,128)(2,1)}, u32[]{:S(2)}) copy-start(bf16[24,96,128]{2,1,0:T(8,128)(2,1)} %refs_4_.1) | copy-start | bytes 1769476
  2.6 15.5 %collective-permute-start.2 = (bf16[16,1536]{1,0:T(8,128)(2,1)S(1)}, bf16[16,1536]{1,0:T(8,128)(2,1)S(1)}, u32[]{:S(2)}, u32[]{:S(2)}) collective-permute-start(bf16[16,1536]{1,0:T(8,128)(2,1)S(1)} %reshape.11), channel_id=1, source_target_pairs={{0,4},{4,0},{8,12},{12,8},{1,5},{5,1},{9,13},{13,9},{2,6},{6,2},{1... | collective-permute-start | bytes 147464 | tf_op jit(solution)/shard_map/ppermute | solution.py:701
  5.7 12.4 %collective-permute-start.3 = (bf16[16,1536]{1,0:T(8,128)(2,1)S(1)}, bf16[16,1536]{1,0:T(8,128)(2,1)S(1)}, u32[]{:S(2)}, u32[]{:S(2)}) collective-permute-start(bf16[16,1536]{1,0:T(8,128)(2,1)S(1)} %reshape.11), channel_id=1, source_target_pairs={{0,8},{4,12},{8,0},{12,4},{1,9},{5,13},{9,1},{13,5},{2,10},{6,14},... | collective-permute-start | bytes 147464 | tf_op jit(solution)/shard_map/ppermute | solution.py:701
  8.5 9.0 %collective-permute-start = (bf16[16,1536]{1,0:T(8,128)(2,1)S(1)}, bf16[16,1536]{1,0:T(8,128)(2,1)S(1)}, u32[]{:S(2)}, u32[]{:S(2)}) collective-permute-start(bf16[16,1536]{1,0:T(8,128)(2,1)S(1)} %reshape.10), channel_id=1, source_target_pairs={{0,2},{2,0},{1,3},{3,1},{4,6},{6,4},{5,7},{7,5},{8,10},{10,8},{9,1... | collective-permute-start | bytes 147464 | tf_op jit(solution)/shard_map/ppermute | solution.py:660
  10.3 6.1 %copy-start.1 = (bf16[1024,128]{1,0:T(8,128)(2,1)S(1)}, bf16[1024,128]{1,0:T(8,128)(2,1)}, u32[]{:S(2)}) copy-start(bf16[1024,128]{1,0:T(8,128)(2,1)} %w_ref.1) | copy-start | bytes 786436
  10.5 5.9 %copy-start.2 = (bf16[128,640]{1,0:T(8,128)(2,1)S(1)}, bf16[128,640]{1,0:T(8,128)(2,1)}, u32[]{:S(2)}) copy-start(bf16[128,640]{1,0:T(8,128)(2,1)} %n_ref.1) | copy-start | bytes 491524
  10.5 7.6 %collective-permute-start.1 = (bf16[2,16,1536]{2,1,0:T(8,128)(2,1)S(1)}, bf16[2,16,1536]{2,1,0:T(8,128)(2,1)S(1)}, u32[]{:S(2)}, u32[]{:S(2)}) collective-permute-start(bf16[2,16,1536]{2,1,0:T(8,128)(2,1)S(1)} %pad_maximum_fusion.3), channel_id=1, source_target_pairs={{0,12},{4,8},{8,4},{12,0},{1,13},{5,9},{9,5},{13,1},{2,14},{6,10},... | collective-permute-start | bytes 294920 | tf_op jit(solution)/shard_map/ppermute | solution.py:701
  10.8 36.7 %collective-permute-start.13 = (bf16[24,96,128]{2,1,0:T(8,128)(2,1)S(1)}, bf16[24,96,128]{2,1,0:T(8,128)(2,1)S(1)}, u32[]{:S(2)}, u32[]{:S(2)}) collective-permute-start(bf16[24,96,128]{2,1,0:T(8,128)(2,1)S(1)} %copy-done.4), channel_id=1, source_target_pairs={{0,12},{12,0},{1,13},{13,1},{2,14},{14,2},{3,15},{15,3},{16,28},{2... | collective-permute-start | bytes 1769480 | tf_op jit(solution)/shard_map/ppermute | solution.py:712
  18.3 5.2 %collective-permute-start.4 = (bf16[3,16,1536]{2,1,0:T(8,128)(2,1)S(1)}, bf16[3,16,1536]{2,1,0:T(8,128)(2,1)S(1)}, u32[]{:S(2)}, u32[]{:S(2)}) collective-permute-start(bf16[3,16,1536]{2,1,0:T(8,128)(2,1)S(1)} %pad_maximum_fusion.2), channel_id=1, source_target_pairs={{0,2},{2,0},{1,3},{3,1},{4,6},{6,4},{5,7},{7,5},{8,10},{10,8},{9,1... | collective-permute-start | bytes 442376 | tf_op jit(solution)/shard_map/ppermute | solution.py:660
  23.5 1.5 %collective-permute-start.6 = (bf16[2,2,16,1536]{3,2,1,0:T(8,128)(2,1)S(1)}, bf16[2,2,16,1536]{3,2,1,0:T(8,128)(2,1)S(1)}, u32[]{:S(2)}, u32[]{:S(2)}) collective-permute-start(bf16[2,2,16,1536]{3,2,1,0:T(8,128)(2,1)S(1)} %pad_maximum_fusion.1.own_ref), channel_id=1, source_target_pairs={{0,1},{1,0},{2,3},{3,2},{4,5},{5,4},{6,7},{7,6},{8,9},{9,8},{10,11... | collective-permute-start | bytes 589832 | tf_op jit(solution)/shard_map/ppermute | solution.py:660
  23.7 2.6 %collective-permute-start.5 = (bf16[2,32,768]{2,1,0:T(8,128)(2,1)S(1)}, bf16[2,32,768]{2,1,0:T(8,128)(2,1)S(1)}, u32[]{:S(2)}, u32[]{:S(2)}) collective-permute-start(bf16[2,32,768]{2,1,0:T(8,128)(2,1)S(1)} %get-tuple-element.69), channel_id=1, source_target_pairs={{0,1},{1,0},{2,3},{3,2},{4,5},{5,4},{6,7},{7,6},{8,9},{9,8},{10,11... | collective-permute-start | bytes 294920 | tf_op jit(solution)/shard_map/ppermute | solution.py:660
  32.7 14.7 %collective-permute-start.8 = (bf16[48,24,128]{2,1,0:T(8,128)(2,1)S(1)}, bf16[48,24,128]{2,1,0:T(8,128)(2,1)S(1)}, u32[]{:S(2)}, u32[]{:S(2)}) collective-permute-start(bf16[48,24,128]{2,1,0:T(8,128)(2,1)S(1)} %get-tuple-element.42), channel_id=1, source_target_pairs={{0,1},{1,0},{2,3},{3,2},{4,5},{5,4},{6,7},{7,6},{8,9},{9,8},{10,11... | collective-permute-start | bytes 884744 | tf_op jit(solution)/shard_map/ppermute | solution.py:660
  32.9 23.1 %collective-permute-start.7 = (bf16[64,24,128]{2,1,0:T(8,128)(2,1)S(1)}, bf16[64,24,128]{2,1,0:T(8,128)(2,1)S(1)}, u32[]{:S(2)}, u32[]{:S(2)}) collective-permute-start(bf16[64,24,128]{2,1,0:T(8,128)(2,1)S(1)} %get-tuple-element.40), channel_id=1, source_target_pairs={{0,1},{1,0},{2,3},{3,2},{4,5},{5,4},{6,7},{7,6},{8,9},{9,8},{10,11... | collective-permute-start | bytes 1179656 | tf_op jit(solution)/shard_map/ppermute | solution.py:660
  33.2 19.9 %collective-permute-start.11 = (bf16[48,24,128]{2,1,0:T(8,128)(2,1)S(1)}, bf16[48,24,128]{2,1,0:T(8,128)(2,1)S(1)}, u32[]{:S(2)}, u32[]{:S(2)}) collective-permute-start(bf16[48,24,128]{2,1,0:T(8,128)(2,1)S(1)} %get-tuple-element.41.rest_0_), channel_id=1, source_target_pairs={{4,8},{8,4},{5,9},{9,5},{6,10},{10,6},{7,11},{11,7},{20,24},{24,20... | collective-permute-start | bytes 884744 | tf_op jit(solution)/shard_map/ppermute | solution.py:723
  33.9 21.3 %collective-permute-start.9 = (bf16[48,24,128]{2,1,0:T(8,128)(2,1)S(1)}, bf16[48,24,128]{2,1,0:T(8,128)(2,1)S(1)}, u32[]{:S(2)}, u32[]{:S(2)}) collective-permute-start(bf16[48,24,128]{2,1,0:T(8,128)(2,1)S(1)} %get-tuple-element.41.rest_0_), channel_id=1, source_target_pairs={{0,4},{4,0},{8,12},{12,8},{1,5},{5,1},{9,13},{13,9},{2,6},{6,2},{1... | collective-permute-start | bytes 884744 | tf_op jit(solution)/shard_map/ppermute | solution.py:723
  47.4 13.6 %collective-permute-start.10 = (bf16[48,24,128]{2,1,0:T(8,128)(2,1)S(1)}, bf16[48,24,128]{2,1,0:T(8,128)(2,1)S(1)}, u32[]{:S(2)}, u32[]{:S(2)}) collective-permute-start(bf16[48,24,128]{2,1,0:T(8,128)(2,1)S(1)} %collective-permute-done.8.rest_1_), channel_id=1, source_target_pairs={{0,4},{4,0},{8,12},{12,8},{1,5},{5,1},{9,13},{13,9},{2,6},{6,2},{1... | collective-permute-start | bytes 884744 | tf_op jit(solution)/shard_map/ppermute | solution.py:723
  47.5 14.2 %collective-permute-start.12 = (bf16[48,24,128]{2,1,0:T(8,128)(2,1)S(1)}, bf16[48,24,128]{2,1,0:T(8,128)(2,1)S(1)}, u32[]{:S(2)}, u32[]{:S(2)}) collective-permute-start(bf16[48,24,128]{2,1,0:T(8,128)(2,1)S(1)} %collective-permute-done.8.rest_1_), channel_id=1, source_target_pairs={{4,8},{8,4},{5,9},{9,5},{6,10},{10,6},{7,11},{11,7},{20,24},{24,20... | collective-permute-start | bytes 884744 | tf_op jit(solution)/shard_map/ppermute | solution.py:723
  53.1 9.9 %collective-permute-start.14 = (bf16[48,24,128]{2,1,0:T(8,128)(2,1)S(1)}, bf16[48,24,128]{2,1,0:T(8,128)(2,1)S(1)}, u32[]{:S(2)}, u32[]{:S(2)}) collective-permute-start(bf16[48,24,128]{2,1,0:T(8,128)(2,1)S(1)} %get-tuple-element.44), channel_id=1, source_target_pairs={{0,1},{1,0},{2,3},{3,2},{4,5},{5,4},{6,7},{7,6},{8,9},{9,8},{10,11... | collective-permute-start | bytes 884744 | tf_op jit(solution)/shard_map/ppermute | solution.py:660
  55.3 11.9 %collective-permute-start.15 = (bf16[48,24,128]{2,1,0:T(8,128)(2,1)S(1)}, bf16[48,24,128]{2,1,0:T(8,128)(2,1)S(1)}, u32[]{:S(2)}, u32[]{:S(2)}) collective-permute-start(bf16[48,24,128]{2,1,0:T(8,128)(2,1)S(1)} %collective-permute-done.9.rest_2_), channel_id=1, source_target_pairs={{4,8},{8,4},{5,9},{9,5},{6,10},{10,6},{7,11},{11,7},{20,24},{24,20... | collective-permute-start | bytes 884744 | tf_op jit(solution)/shard_map/ppermute | solution.py:723
  55.9 12.9 %collective-permute-start.16 = (bf16[48,24,128]{2,1,0:T(8,128)(2,1)S(1)}, bf16[48,24,128]{2,1,0:T(8,128)(2,1)S(1)}, u32[]{:S(2)}, u32[]{:S(2)}) collective-permute-start(bf16[48,24,128]{2,1,0:T(8,128)(2,1)S(1)} %collective-permute-done.11.rest_4_), channel_id=1, source_target_pairs={{4,0},{8,12},{5,1},{9,13},{6,2},{10,14},{7,3},{11,15},{20,16},{24,... | collective-permute-start | bytes 884744 | tf_op jit(solution)/shard_map/ppermute | solution.py:723
  61.0 9.6 %collective-permute-start.18 = (bf16[48,24,128]{2,1,0:T(8,128)(2,1)S(1)}, bf16[48,24,128]{2,1,0:T(8,128)(2,1)S(1)}, u32[]{:S(2)}, u32[]{:S(2)}) collective-permute-start(bf16[48,24,128]{2,1,0:T(8,128)(2,1)S(1)} %collective-permute-done.10.rest_3_), channel_id=1, source_target_pairs={{4,8},{8,4},{5,9},{9,5},{6,10},{10,6},{7,11},{11,7},{20,24},{24,20... | collective-permute-start | bytes 884744 | tf_op jit(solution)/shard_map/ppermute | solution.py:723
  61.7 12.7 %collective-permute-start.19 = (bf16[48,24,128]{2,1,0:T(8,128)(2,1)S(1)}, bf16[48,24,128]{2,1,0:T(8,128)(2,1)S(1)}, u32[]{:S(2)}, u32[]{:S(2)}) collective-permute-start(bf16[48,24,128]{2,1,0:T(8,128)(2,1)S(1)} %collective-permute-done.12.rest_5_), channel_id=1, source_target_pairs={{4,0},{8,12},{5,1},{9,13},{6,2},{10,14},{7,3},{11,15},{20,16},{24,... | collective-permute-start | bytes 884744 | tf_op jit(solution)/shard_map/ppermute | solution.py:723
  66.5 10.3 %collective-permute-start.25 = (bf16[24,24,128]{2,1,0:T(8,128)(2,1)S(1)}, bf16[24,24,128]{2,1,0:T(8,128)(2,1)S(1)}, u32[]{:S(2)}, u32[]{:S(2)}) collective-permute-start(bf16[24,24,128]{2,1,0:T(8,128)(2,1)S(1)} %get-tuple-element.56), channel_id=1, source_target_pairs={{0,2},{2,0},{1,3},{3,1},{4,6},{6,4},{5,7},{7,5},{8,10},{10,8},{9,1... | collective-permute-start | bytes 442376 | tf_op jit(solution)/shard_map/ppermute | solution.py:660
  67.2 11.2 %collective-permute-start.26 = (bf16[24,24,128]{2,1,0:T(8,128)(2,1)S(1)}, bf16[24,24,128]{2,1,0:T(8,128)(2,1)S(1)}, u32[]{:S(2)}, u32[]{:S(2)}) collective-permute-start(bf16[24,24,128]{2,1,0:T(8,128)(2,1)S(1)} %get-tuple-element.57), channel_id=1, source_target_pairs={{0,1},{1,0},{2,3},{3,2},{4,5},{5,4},{6,7},{7,6},{8,9},{9,8},{10,11... | collective-permute-start | bytes 442376 | tf_op jit(solution)/shard_map/ppermute | solution.py:660
  68.9 9.7 %collective-permute-start.27 = (bf16[24,24,128]{2,1,0:T(8,128)(2,1)S(1)}, bf16[24,24,128]{2,1,0:T(8,128)(2,1)S(1)}, u32[]{:S(2)}, u32[]{:S(2)}) collective-permute-start(bf16[24,24,128]{2,1,0:T(8,128)(2,1)S(1)} %get-tuple-element.58), channel_id=1, source_target_pairs={{0,3},{1,2},{2,1},{3,0},{4,7},{5,6},{6,5},{7,4},{8,11},{9,10},{10,... | collective-permute-start | bytes 442376 | tf_op jit(solution)/shard_map/ppermute | solution.py:670
  70.6 6.1 %collective-permute-start.17 = (bf16[12,24,128]{2,1,0:T(8,128)(2,1)S(1)}, bf16[12,24,128]{2,1,0:T(8,128)(2,1)S(1)}, u32[]{:S(2)}, u32[]{:S(2)}) collective-permute-start(bf16[12,24,128]{2,1,0:T(8,128)(2,1)S(1)} %get-tuple-element.48), channel_id=1, source_target_pairs={{0,2},{2,0},{1,3},{3,1},{4,6},{6,4},{5,7},{7,5},{8,10},{10,8},{9,1... | collective-permute-start | bytes 221192 | tf_op jit(solution)/shard_map/ppermute | solution.py:660
  74.4 6.4 %collective-permute-start.21 = (bf16[12,24,128]{2,1,0:T(8,128)(2,1)S(1)}, bf16[12,24,128]{2,1,0:T(8,128)(2,1)S(1)}, u32[]{:S(2)}, u32[]{:S(2)}) collective-permute-start(bf16[12,24,128]{2,1,0:T(8,128)(2,1)S(1)} %get-tuple-element.51), channel_id=1, source_target_pairs={{0,1},{1,0},{2,3},{3,2},{4,5},{5,4},{6,7},{7,6},{8,9},{9,8},{10,11... | collective-permute-start | bytes 221192 | tf_op jit(solution)/shard_map/ppermute | solution.py:660
  76.7 4.4 %collective-permute-start.22 = (bf16[12,24,128]{2,1,0:T(8,128)(2,1)S(1)}, bf16[12,24,128]{2,1,0:T(8,128)(2,1)S(1)}, u32[]{:S(2)}, u32[]{:S(2)}) collective-permute-start(bf16[12,24,128]{2,1,0:T(8,128)(2,1)S(1)} %get-tuple-element.52), channel_id=1, source_target_pairs={{0,3},{1,2},{2,1},{3,0},{4,7},{5,6},{6,5},{7,4},{8,11},{9,10},{10,... | collective-permute-start | bytes 221192 | tf_op jit(solution)/shard_map/ppermute | solution.py:670
  76.9 6.2 %collective-permute-start.20 = (bf16[12,24,128]{2,1,0:T(8,128)(2,1)S(1)}, bf16[12,24,128]{2,1,0:T(8,128)(2,1)S(1)}, u32[]{:S(2)}, u32[]{:S(2)}) collective-permute-start(bf16[12,24,128]{2,1,0:T(8,128)(2,1)S(1)} %get-tuple-element.50), channel_id=1, source_target_pairs={{0,2},{2,0},{1,3},{3,1},{4,6},{6,4},{5,7},{7,5},{8,10},{10,8},{9,1... | collective-permute-start | bytes 221192 | tf_op jit(solution)/shard_map/ppermute | solution.py:660
  78.3 4.7 %collective-permute-start.23 = (bf16[12,24,128]{2,1,0:T(8,128)(2,1)S(1)}, bf16[12,24,128]{2,1,0:T(8,128)(2,1)S(1)}, u32[]{:S(2)}, u32[]{:S(2)}) collective-permute-start(bf16[12,24,128]{2,1,0:T(8,128)(2,1)S(1)} %get-tuple-element.53), channel_id=1, source_target_pairs={{0,1},{1,0},{2,3},{3,2},{4,5},{5,4},{6,7},{7,6},{8,9},{9,8},{10,11... | collective-permute-start | bytes 221192 | tf_op jit(solution)/shard_map/ppermute | solution.py:660
  78.5 5.6 %collective-permute-start.24 = (bf16[12,24,128]{2,1,0:T(8,128)(2,1)S(1)}, bf16[12,24,128]{2,1,0:T(8,128)(2,1)S(1)}, u32[]{:S(2)}, u32[]{:S(2)}) collective-permute-start(bf16[12,24,128]{2,1,0:T(8,128)(2,1)S(1)} %get-tuple-element.54), channel_id=1, source_target_pairs={{0,3},{1,2},{2,1},{3,0},{4,7},{5,6},{6,5},{7,4},{8,11},{9,10},{10,... | collective-permute-start | bytes 221192 | tf_op jit(solution)/shard_map/ppermute | solution.py:670
  (1 other events, 0.8 us)
